TPU v7x, 32 devices: a whole 2x2x4 slice. The times are simulated.
32 devices in a mesh: dp: 8 (over z, x), tensor: 4 (over y, core).
Axes of the slice: x: 2, y: 2, z: 4, core: 2. Of those that a mesh axis runs over, the one named last changes fastest.
Arguments:
- tokens: bfloat16 [48, 260, 768], P('dp'), may hold values from -6 to 6
- cotangent: bfloat16 [48, 260, 768], P('dp'), may hold values from -6 to 6
- split_point: int32 [48], P('dp'), may hold values from 0 to 32
- w_qkv: bfloat16 [3, 768, 768], P(None, None, 'tensor'), may hold values from -0.21875 to 0.21875
- w_out: bfloat16 [768, 768], P('tensor'), may hold values from -0.75 to 0.75
- w_up: bfloat16 [768, 3072], P(None, 'tensor'), may hold values from -0.21875 to 0.21875
- w_down: bfloat16 [3072, 768], P('tensor'), may hold values from -0.109375 to 0.109375
- gain_one: float32 [768], replicated, may hold values from 0.1 to 1.9
- shift_one: float32 [768], replicated, may hold values from -3 to 3
- gain_two: float32 [768], replicated, may hold values from 0.1 to 1.9
- shift_two: float32 [768], replicated, may hold values from -3 to 3
Outputs:
- output: bfloat16 [48, 260, 768], P('dp')
- grad_tokens: bfloat16 [48, 260, 768], P('dp')
- grad_qkv: float32 [3, 768, 768], P(None, 'dp', 'tensor')
- grad_out: float32 [768, 768], P('tensor', 'dp')
- grad_up: float32 [768, 3072], P('dp', 'tensor')
- grad_down: float32 [3072, 768], P('tensor', 'dp')
- grad_gain_one: float32 [768], P('dp')
- grad_shift_one: float32 [768], P('dp')
- grad_gain_two: float32 [768], P('dp')
- grad_shift_two: float32 [768], P('dp')
All inputs are finite; a program needn't handle non-finite values.
Results may differ from a plain program's by a relative error of at most 0.013.
Values sent between devices are 32-bit elements; how exact they have to be, the bound alone decides.
A program may use at most 128 MiB of HBM per device.

v0:
```python
from functools import partial

import jax
import jax.numpy as jnp
from jax import lax
from jax.sharding import PartitionSpec as P

HD = 64
PATCHES = 196


EPSILON = 1e-05


def layer_norm(values, gain_vec, shift_vec):
    row_mean = jnp.mean(values, axis=-1, keepdims=True)
    centered = values - row_mean
    variance = jnp.mean(centered * centered, axis=-1, keepdims=True)
    return centered * lax.rsqrt(variance + EPSILON) * gain_vec + shift_vec


def attention_forward(inputs, allowed, w_qkv, w_out, gain_one, shift_one):
    batch, length, width = inputs.shape
    local = w_qkv.shape[2]
    head_count = local // HD
    normed = layer_norm(inputs, gain_one, shift_one).astype(jnp.bfloat16)
    packed = jnp.einsum("btd,cde->cbte", normed, w_qkv, preferred_element_type=jnp.float32).astype(
        jnp.bfloat16
    )
    queries = packed[0].reshape(batch, length, head_count, HD)
    keys = packed[1].reshape(batch, length, head_count, HD)
    values = packed[2].reshape(batch, length, head_count, HD)
    scores = jnp.einsum(
        "bqhe,bkhe->bhqk", queries, keys, preferred_element_type=jnp.float32
    ) * HD ** (-0.5)
    scores = jnp.where(allowed[:, None], scores, -1e30)
    log_total = jax.nn.logsumexp(scores, axis=-1, keepdims=True)
    attn_probs = jnp.exp(scores - log_total)
    probs_low = attn_probs.astype(jnp.bfloat16)
    mixed = jnp.einsum("bhqk,bkhe->bqhe", probs_low, values, preferred_element_type=jnp.float32)
    mixed = mixed.reshape(batch, length, local).astype(jnp.bfloat16)
    partial_out = jnp.einsum("btk,kd->btd", mixed, w_out, preferred_element_type=jnp.float32)
    return (normed, queries, keys, values, attn_probs, probs_low, mixed, partial_out)


def mlp_forward(middle, w_up, gain_two, shift_two):
    normed_two = layer_norm(middle, gain_two, shift_two).astype(jnp.bfloat16)
    pre_act = jnp.einsum("btd,df->btf", normed_two, w_up, preferred_element_type=jnp.float32)
    activated = jax.nn.gelu(pre_act, approximate=False).astype(jnp.bfloat16)
    return (normed_two, pre_act, activated)


def per_device(
    tokens,
    cotangent,
    split_point,
    w_qkv,
    w_out,
    w_up,
    w_down,
    gain_one,
    shift_one,
    gain_two,
    shift_two,
):
    inputs = tokens.astype(jnp.float32)
    batch, length, width = tokens.shape
    local = w_qkv.shape[2]
    head_count = local // HD
    score_scale = HD ** (-0.5)
    places = jnp.arange(length, dtype=jnp.int32)
    limit = jnp.maximum(places[None, :, None], PATCHES + split_point[:, None, None] - 1)
    allowed = places[None, None, :] <= limit
    normed, queries, keys, values, attn_probs, probs_low, mixed, partial_out = attention_forward(
        inputs, allowed, w_qkv, w_out, gain_one, shift_one
    )
    middle = inputs + lax.psum(partial_out, "tensor")
    normed_two, pre_act, activated = mlp_forward(middle, w_up, gain_two, shift_two)
    branch = jnp.einsum("btf,fd->btd", activated, w_down, preferred_element_type=jnp.float32)
    output = (middle + lax.psum(branch, "tensor")).astype(jnp.bfloat16)
    normed, queries, keys, values, attn_probs, probs_low, mixed, partial_out = attention_forward(
        inputs, allowed, w_qkv, w_out, gain_one, shift_one
    )
    middle = inputs + lax.psum(partial_out, "tensor")
    normed_two, pre_act, activated = mlp_forward(middle, w_up, gain_two, shift_two)
    grad_output = cotangent.astype(jnp.float32)
    grad_act = jnp.einsum("btd,fd->btf", cotangent, w_down, preferred_element_type=jnp.float32)
    gelu_pull = jax.vjp(partial(jax.nn.gelu, approximate=False), pre_act)[1]
    grad_pre = gelu_pull(grad_act)[0].astype(jnp.bfloat16)
    grad_down_local = jnp.einsum(
        "btf,btd->fd", activated, cotangent, preferred_element_type=jnp.float32
    )
    grad_up_local = jnp.einsum(
        "btd,btf->df", normed_two, grad_pre, preferred_element_type=jnp.float32
    )
    grad_normed_two = lax.psum(
        jnp.einsum("btf,df->btd", grad_pre, w_up, preferred_element_type=jnp.float32), "tensor"
    )
    norm_two_pull = jax.vjp(layer_norm, middle, gain_two, shift_two)[1]
    grad_mid_norm, grad_gain_two, grad_shift_two = norm_two_pull(grad_normed_two)
    grad_middle = grad_output + grad_mid_norm
    grad_mid_low = grad_middle.astype(jnp.bfloat16)
    grad_out_local = jnp.einsum(
        "btk,btd->kd", mixed, grad_mid_low, preferred_element_type=jnp.float32
    )
    grad_mix = jnp.einsum("btd,kd->btk", grad_mid_low, w_out, preferred_element_type=jnp.float32)
    grad_mix = grad_mix.astype(jnp.bfloat16).reshape(batch, length, head_count, HD)
    grad_probs = jnp.einsum("bqhe,bkhe->bhqk", grad_mix, values, preferred_element_type=jnp.float32)
    row_terms = jnp.sum(attn_probs * grad_probs, axis=-1, keepdims=True)
    grad_scores = (attn_probs * (grad_probs - row_terms)).astype(jnp.bfloat16)
    grad_query = (
        jnp.einsum("bhqk,bkhe->bqhe", grad_scores, keys, preferred_element_type=jnp.float32)
        * score_scale
    )
    grad_key = (
        jnp.einsum("bhqk,bqhe->bkhe", grad_scores, queries, preferred_element_type=jnp.float32)
        * score_scale
    )
    grad_value = jnp.einsum(
        "bhqk,bqhe->bkhe", probs_low, grad_mix, preferred_element_type=jnp.float32
    )
    grad_packed = (
        jnp.stack([grad_query, grad_key, grad_value])
        .reshape(3, batch, length, local)
        .astype(jnp.bfloat16)
    )
    grad_qkv_local = jnp.einsum(
        "btd,cbte->cde", normed, grad_packed, preferred_element_type=jnp.float32
    )
    grad_normed = lax.psum(
        jnp.einsum("cbte,cde->btd", grad_packed, w_qkv, preferred_element_type=jnp.float32),
        "tensor",
    )
    norm_one_pull = jax.vjp(layer_norm, inputs, gain_one, shift_one)[1]
    grad_in_norm, grad_gain_one, grad_shift_one = norm_one_pull(grad_normed)
    grad_tokens = (grad_middle + grad_in_norm).astype(jnp.bfloat16)
    (
        qkv_part,
        out_part,
        up_part,
        down_part,
        gain_one_part,
        shift_one_part,
        gain_two_part,
        shift_two_part,
    ) = (
        lax.psum_scatter(grad_qkv_local, "dp", scatter_dimension=1, tiled=True),
        lax.psum_scatter(grad_out_local, "dp", scatter_dimension=1, tiled=True),
        lax.psum_scatter(grad_up_local, "dp", scatter_dimension=0, tiled=True),
        lax.psum_scatter(grad_down_local, "dp", scatter_dimension=1, tiled=True),
        lax.psum_scatter(grad_gain_one, "dp", scatter_dimension=0, tiled=True),
        lax.psum_scatter(grad_shift_one, "dp", scatter_dimension=0, tiled=True),
        lax.psum_scatter(grad_gain_two, "dp", scatter_dimension=0, tiled=True),
        lax.psum_scatter(grad_shift_two, "dp", scatter_dimension=0, tiled=True),
    )
    return (
        output,
        grad_tokens,
        qkv_part,
        out_part,
        up_part,
        down_part,
        gain_one_part,
        shift_one_part,
        gain_two_part,
        shift_two_part,
    )


def solution(mesh):
    in_specs = (
        P("dp", None, None),
        P("dp", None, None),
        P("dp"),
        P(None, None, "tensor"),
        P("tensor", None),
        P(None, "tensor"),
        P("tensor", None),
        P(),
        P(),
        P(),
        P(),
    )
    out_specs = (
        P("dp", None, None),
        P("dp", None, None),
        P(None, "dp", "tensor"),
        P("tensor", "dp"),
        P("dp", "tensor"),
        P("tensor", "dp"),
        P("dp"),
        P("dp"),
        P("dp"),
        P("dp"),
    )
    return jax.shard_map(
        per_device, mesh=mesh, in_specs=in_specs, out_specs=out_specs, check_vma=False
    )
```

profile of v0, /device:TPU:0, one launch (start us, length us, event | category | flops | bytes accessed | tf_op | source)
XLA Modules:
  0.0 753.7 jit_solution(12247592497835204554)
XLA Ops:
  34.3 98.9 %all-reduce.10.cloned.1.call-done = f32[6,260,768]{2,1,0:T(8,128)} async-done(((f32[6,260,768]{2,1,0:T(8,128)}), f32[6,260,768]{2,1,0:T(8,128)}) %all-reduce.10.cloned.1.call-update) | async-done | bytes 4792336 | tf_op jit(solution)/shard_map/psum | solution.py:77
  141.5 11.6 %multiply_convert_fusion.1 = (bf16[6,260,768]{2,1,0:T(8,128)(2,1)}, f32[6,260,768]{2,1,0:T(8,128)S(1)}) fusion(f32[6,260,768]{2,1,0:T(8,128)S(1)} %get-tuple-element.66, u8[260,768]{1,0:T(8,128)(4,1)S(1)} %get-tuple-element.48, u8[260,768]{1,0:T(8,128)(4,1)S(1)} %get-tuple-element.47), kind=kLoop, calls=%fused_computation.35 | loop fusion | flops 83865600 | bytes 12380160 | tf_op jit(solution)/shard_map/convert_element_type | solution.py:49
  158.0 4.3 fusion.27
  162.6 96.6 %all-reduce.12.cloned.1.call-done = f32[6,260,768]{2,1,0:T(8,128)} async-done(((f32[6,260,768]{2,1,0:T(8,128)}), f32[6,260,768]{2,1,0:T(8,128)}) %all-reduce.12.cloned.1.call-update) | async-done | bytes 4792336 | tf_op jit(solution)/shard_map/psum | solution.py:96
  259.1 4.9 multiply_reduce_fusion.1
  277.8 6.5 convolution_convert_fusion
  284.3 6.8 multiply_reduce_fusion
  291.3 6.3 multiply_convert_fusion
  309.9 5.0 convolution_bitcast_fusion.3
  317.7 4.7 reshape.158
  322.6 6.1 fusion.25
  328.7 4.5 convolution_bitcast_fusion
  333.5 7.4 convolution_bitcast_fusion.2
  341.0 6.2 convolution_bitcast_fusion.1
  348.5 5.2 reduce-scatter.15.cloned.1.call-done
  355.4 68.4 %reduce-scatter.13.cloned.1.call-done = f32[96,576]{1,0:T(8,128)} async-done(((f32[768,576]{1,0:T(8,128)}), f32[96,576]{1,0:T(8,128)}) %reduce-scatter.13.cloned.1.call-update) | async-done | bytes 221200
  425.8 174.9 %all-reduce.14.cloned.1.call-done = (f32[6,260,768]{2,1,0:T(8,128)}, f32[6,260,768]{2,1,0:T(8,128)}) async-done(((f32[6,260,768]{2,1,0:T(8,128)}, f32[6,260,768]{2,1,0:T(8,128)}), (f32[6,260,768]{2,1,0:T(8,128)}, f32[6,260,768]{2,1,0:T(8,128)})) %all-reduce.14.cloned.1.call-update) | async-done | bytes 9584656 | tf_op jit(solution)/shard_map/psum | solution.py:80
  600.6 4.6 fusion.44
  605.2 3.9 fusion.9
  609.1 37.2 %all-reduce.4 = (f32[768]{0:T(1024)S(1)}, f32[768]{0:T(1024)S(1)}, f32[768]{0:T(1024)S(1)}, f32[768]{0:T(1024)S(1)}) all-reduce(f32[768]{0:T(1024)S(1)} %get-tuple-element.42, f32[768]{0:T(1024)S(1)} %get-tuple-element.45, f32[768]{0:T(1024)S(1)} %get-tuple-element.40, ...), channel_id=6, replica_groups=mesh['dp'=8,'tensor'=4] {'dp'}, use_global_device_ids=true, to_apply=%region_20.21.clone | all-reduce | flops 3072 | bytes 24576
  648.7 6.0 add_convert_fusion.2
  656.7 5.0 add_convert_fusion
  661.7 12.3 %reduce-scatter.9.cloned.1.call-done = f32[96,768]{1,0:T(8,128)} async-done(((f32[768,768]{1,0:T(8,128)}), f32[96,768]{1,0:T(8,128)}) %reduce-scatter.9.cloned.1.call-update) | async-done | bytes 294928 | tf_op jit(solution)/shard_map/reduce_scatter | solution.py:149
  674.0 72.4 %reduce-scatter.11.cloned.1.call-done = f32[768,96]{0,1:T(8,128)} async-done(((f32[768,768]{0,1:T(8,128)}), f32[768,96]{0,1:T(8,128)}) %reduce-scatter.11.cloned.1.call-update) | async-done | bytes 294928 | tf_op jit(solution)/shard_map/reduce_scatter | solution.py:150
  (136 shorter events, 78.2 us)
Async XLA Ops:
  7.2 130.5 %copy-start = (bf16[768,768]{1,0:T(8,128)(2,1)S(1)}, bf16[768,768]{1,0:T(8,128)(2,1)}, u32[]{:S(2)}) copy-start(bf16[768,768]{1,0:T(8,128)(2,1)} %param.16) | copy-start | bytes 3538948
  7.2 6.2 copy-start.25
  7.2 6.2 copy-start.31
  7.2 6.2 copy-start.29
  7.2 126.0 %all-reduce.10.cloned.1.call-start = ((), (), s32[]{:S(2)}) async-start(), calls=%async_computation.4 | async-start | bytes 9732096 | tf_op jit(solution)/shard_map/psum | solution.py:77
  7.3 6.1 copy-start.4
  33.8 225.3 %all-reduce.12.cloned.1.call-start = ((), (), s32[]{:S(2)}) async-start(), calls=%async_computation.5 | async-start | bytes 9732096 | tf_op jit(solution)/shard_map/psum | solution.py:96
  141.5 11.7 %copy-start.11 = (bf16[6,260,768]{2,1,0:T(8,128)(2,1)S(1)}, bf16[6,260,768]{2,1,0:T(8,128)(2,1)}, u32[]{:S(2)}) copy-start(bf16[6,260,768]{2,1,0:T(8,128)(2,1)} %param.12) | copy-start | bytes 7188484
  141.5 11.6 %copy-start.27 = (bf16[768,768]{1,0:T(8,128)(2,1)S(1)}, bf16[768,768]{1,0:T(8,128)(2,1)}, u32[]{:S(2)}) copy-start(bf16[768,768]{1,0:T(8,128)(2,1)} %param.17) | copy-start | bytes 3538948
  162.3 191.5 %reduce-scatter.15.cloned.1.call-start = ((), (), s32[]{:S(2)}) async-start(), calls=%async_computation.9 | async-start | bytes 884736
  277.8 6.5 copy-start.15
  277.8 6.5 copy-start.16
  291.1 132.8 %reduce-scatter.13.cloned.1.call-start = ((), (), s32[]{:S(2)}) async-start(), calls=%async_computation.8 | async-start | bytes 2211840
  299.4 6.4 copy-start.13
  322.5 278.2 %all-reduce.14.cloned.1.call-start = ((), (), s32[]{:S(2)}) async-start(), calls=%async_computation.10 | async-start | bytes 19464192 | tf_op jit(solution)/shard_map/psum | solution.py:80
  322.5 6.1 copy-start.20
  322.5 6.1 copy-start.21
  333.2 340.8 %reduce-scatter.9.cloned.1.call-start = ((), (), s32[]{:S(2)}) async-start(), calls=%async_computation.6 | async-start | bytes 2654208 | tf_op jit(solution)/shard_map/reduce_scatter | solution.py:149
  341.0 6.3 copy-start.33
  341.0 405.4 %reduce-scatter.11.cloned.1.call-start = ((), (), s32[]{:S(2)}) async-start(), calls=%async_computation.7 | async-start | bytes 2654208 | tf_op jit(solution)/shard_map/reduce_scatter | solution.py:150
  605.2 49.4 %slice-start = ((s8[4866048]{0:T(1024)(128)(4,1)}), s8[671744]{0:T(1024)(128)(4,1)S(1)}, s32[]{:S(2)}) async-start(s8[4866048]{0:T(1024)(128)(4,1)} %bitcast.87), calls=%async_computation.11 | async-start | bytes 1343488
  648.6 6.5 slice-start.1
  648.6 8.1 %copy-start.9 = (f32[6,260,768]{2,1,0:T(8,128)S(1)}, f32[6,260,768]{2,1,0:T(8,128)}, u32[]{:S(2)}) copy-start(f32[6,260,768]{2,1,0:T(8,128)} %get-tuple-element.54) | copy-start | bytes 14376964
  648.6 97.8 %copy-start.1 = (bf16[768,768]{1,0:T(8,128)(2,1)S(1)}, bf16[768,768]{1,0:T(8,128)(2,1)}, u32[]{:S(2)}) copy-start(bf16[768,768]{1,0:T(8,128)(2,1)} %param.16) | copy-start | bytes 3538948
  (20 other events, 68.2 us)
Sparse Core Ops, SparseCore 0:
  33.9 99.2 all-reduce.9
  162.5 96.6 all-reduce.11
  291.2 62.5 reduce-scatter.14
  358.1 65.7 reduce-scatter.12
  426.4 174.2 all-reduce.13
  604.9 69.0 reduce-scatter.8
  678.5 67.8 reduce-scatter.10
where the time goes:
time: 762 us; the launch traced here: 754 us
  waiting for transfers between devices  529 us (69%)
  matrix products  75.3 us (10%)
  other arithmetic  58.8 us (8%)
  blocking collectives  37.2 us (5%)
  local copies, waits for them, and re-layouts  36.4 us (5%)
  between operations  15.8 us (2%)
    psum x1, waiting for transfers between devices, per_device(): output = (middle + lax.psum(branch, 'tensor')).astype(jnp.bfloat16)  175 us
    psum x1, waiting for transfers between devices, per_device(): middle = inputs + lax.psum(partial_out, 'tensor')  98.9 us
    psum x1, waiting for transfers between devices, per_device(): lax.psum(jnp.einsum('btf,df->btd', grad_pre, w_up, preferred_element_type...  96.6 us
    unnamed x9, waiting for transfers between devices  73.8 us
    reduce_scatter x1, waiting for transfers between devices, per_device(): lax.psum_scatter(grad_down_local, 'dp', scatter_dimension=1, tiled=True)  72.4 us
    unnamed x1, blocking collectives  37.2 us
    unnamed x84, local copies, waits for them, and re-layouts  23.5 us
  transfers between devices with their start and end apart: 7, of which 7 were waited for; matrix products, arithmetic and copies ran while one was open for 11% of the time, Pallas kernels for 0%

commit v1 on v0

--- a/solution.py
+++ b/solution.py
@@ -3,13 +3,553 @@
 import jax
 import jax.numpy as jnp
 from jax import lax
+from jax.experimental import pallas as pl
+from jax.experimental.pallas import tpu as pltpu
 from jax.sharding import PartitionSpec as P
 
 HD = 64
 PATCHES = 196
-
-
 EPSILON = 1e-05
+MESH = pl.DeviceIdType.MESH
+F32 = jnp.float32
+BF16 = jnp.bfloat16
+ANY = pl.BlockSpec(memory_space=pl.ANY)
+VM = pl.BlockSpec(memory_space=pltpu.VMEM)
+SM = pl.BlockSpec(memory_space=pltpu.SMEM)
+VLIM = 60 * 1024 * 1024
+NT = (((1,), (1,)), ((), ()))
+
+
+def mm(a, b):
+    return jnp.dot(a, b, preferred_element_type=F32)
+
+
+def mm_nt(a, b):
+    return lax.dot_general(a, b, NT, preferred_element_type=F32)
+
+
+def mm_tn(a, b):
+    return lax.dot_general(a, b, (((0,), (0,)), ((), ())), preferred_element_type=F32)
+
+
+class Place:
+    def __init__(self):
+        d, t = lax.axis_index("dp"), lax.axis_index("tensor")
+        self.d, self.t = d, t
+        self.z, self.x = d // 2, lax.rem(d, 2)
+        self.y, self.c = t // 2, lax.rem(t, 2)
+        self.sib = (d, self.y * 2 + 1 - self.c)
+        self.ynb = (d, (1 - self.y) * 2 + self.c)
+        self.xnb = (self.z * 2 + 1 - self.x, t)
+
+    def zof(self, k):
+        return lax.rem(self.z + k, 4)
+
+    def znb(self, k):
+        return (self.zof(k) * 2 + self.x, self.t)
+
+
+def greet(place, with_y, with_dp):
+    peers = [place.sib, place.xnb] + [place.znb(k) for k in (1, 2, 3)]
+    if with_y:
+        peers.append(place.ynb)
+    if with_dp:
+        peers += [(place.zof(k) * 2 + 1 - place.x, place.t) for k in (1, 2, 3)]
+    barrier = pltpu.get_barrier_semaphore()
+    for p in peers:
+        pl.semaphore_signal(barrier, 1, device_id=p, device_id_type=MESH)
+    pl.semaphore_wait(barrier, len(peers))
+
+
+def rcopy(src, dst, ssem, rsem, dev):
+    return pltpu.make_async_remote_copy(
+        src_ref=src, dst_ref=dst, send_sem=ssem, recv_sem=rsem, device_id=dev, device_id_type=MESH
+    )
+
+
+def gather_kernel(own, wf, lsem, csend, crecv, ysend, yrecv, zsend, xsend, brecv):
+    me = Place()
+    greet(me, True, False)
+    local = pltpu.make_async_copy(own, wf.at[0], lsem)
+    local.start()
+    sends = []
+
+    def go(cp):
+        cp.start()
+        sends.append(cp)
+        return cp
+
+    d = me.d
+    ysl = [go(rcopy(own.at[p, d], wf.at[2, p, d], ysend.at[p], yrecv.at[p], me.ynb)) for p in (0, 1)]
+    c1 = [go(rcopy(own.at[p], wf.at[1, p], csend.at[p], crecv.at[p], me.sib)) for p in (0, 1, 2)]
+    yd = go(rcopy(own.at[2], wf.at[2, 2], ysend.at[2], yrecv.at[2], me.ynb))
+    c3 = []
+    for p in (0, 1):
+        ysl[p].wait_recv()
+        src = wf.at[2, p, d]
+        for k in (1, 2, 3):
+            go(rcopy(src, src, zsend.at[p, k - 1], brecv.at[p, 3 - k], me.znb(k)))
+        go(rcopy(src, src, xsend.at[p, 0], brecv.at[p, 3], me.xnb))
+    for p in (0, 1):
+        for k in (1, 2, 3):
+            s = me.zof(k) * 2 + me.x
+            blk = wf.at[2, p, s]
+            rcopy(blk, blk, zsend.at[p, k - 1], brecv.at[p, k - 1], me.znb(k)).wait_recv()
+            go(rcopy(blk, blk, xsend.at[p, k], brecv.at[p, 3 + k], me.xnb))
+        for k in (0, 1, 2, 3):
+            s = me.zof(k) * 2 + 1 - me.x
+            blk = wf.at[2, p, s]
+            rcopy(blk, blk, xsend.at[p, k], brecv.at[p, 3 + k], me.xnb).wait_recv()
+        c3.append(go(rcopy(wf.at[2, p], wf.at[3, p], csend.at[3 + p], crecv.at[3 + p], me.sib)))
+    yd.wait_recv()
+    c3.append(go(rcopy(wf.at[2, 2], wf.at[3, 2], csend.at[5], crecv.at[5], me.sib)))
+    for cp in c1 + c3:
+        cp.wait_recv()
+    for cp in sends:
+        cp.wait_send()
+    local.wait()
+
+
+def gather(own):
+    n = own.shape
+    dma = pltpu.SemaphoreType.DMA
+    return pl.pallas_call(
+        gather_kernel,
+        out_shape=jax.ShapeDtypeStruct((4,) + n, F32),
+        in_specs=[ANY],
+        out_specs=ANY,
+        scratch_shapes=[
+            dma, dma((6,)), dma((6,)), dma((3,)), dma((3,)), dma((2, 3)), dma((2, 4)), dma((2, 7)),
+        ],
+        compiler_params=pltpu.CompilerParams(collective_id=0, has_side_effects=True),
+        name="gather",
+    )(own)
+
+
+def ln_stats(v):
+    mean = jnp.mean(v, axis=-1, keepdims=True)
+    cen = v - mean
+    var = jnp.mean(cen * cen, axis=-1, keepdims=True)
+    rstd = lax.rsqrt(var + EPSILON)
+    return cen * rstd, rstd
+
+
+def lanes(shape):
+    return lax.broadcasted_iota(jnp.int32, shape, len(shape) - 1)
+
+
+HEADS = ((0, 1, 2, False), (0, 1, 2, True), (3, 4, 3, False))
+
+
+def attn_fwd_kernel(split, tok, g1, s1, g2, s2, wf, n1, qkv, prob, mx, mid, n2, wst, wbf, s_a, s_b, sem):
+    ex, rows, rpad = tok.shape[0], tok.shape[1], n1.shape[1]
+
+    def fetch(j):
+        return pltpu.make_async_copy(wf.at[j, 0], wst.at[j % 2], sem.at[j % 2])
+
+    fetch(0).start()
+    n1[...] = jnp.zeros_like(n1)
+
+    @pl.loop(0, ex)
+    def _(e):
+        xhat, _ = ln_stats(tok[e].astype(F32))
+        n1[e, :rows, :] = (xhat * g1[...] + s1[...]).astype(BF16)
+
+    low_half = lanes((rpad, 128)) < HD
+    qi = lax.broadcasted_iota(jnp.int32, (rpad, rpad), 0)
+    kj = lax.broadcasted_iota(jnp.int32, (rpad, rpad), 1)
+    for j in range(4):
+        if j < 3:
+            fetch(j + 1).start()
+        fetch(j).wait()
+        wbf[...] = wst[j % 2].astype(BF16)
+        n1f = n1[...].reshape(ex * rpad, -1)
+        qkv[j] = mm(n1f, wbf[:, :640]).astype(BF16).reshape(ex, rpad, 640)
+
+        @pl.loop(0, ex)
+        def _(e):
+            allowed = kj <= jnp.maximum(qi, PATCHES - 1 + split[e])
+            outs = []
+            for h, (gq, gk, gv, high) in enumerate(HEADS):
+                q = qkv[j, e, :, gq * 128 : gq * 128 + 128]
+                q = jnp.where(low_half != high, q, jnp.zeros_like(q))
+                k = qkv[j, e, :, gk * 128 : gk * 128 + 128]
+                s = mm_nt(q, k) * (HD ** -0.5)
+                s = jnp.where(allowed, s, -1e30)
+                top = jnp.max(s, axis=-1, keepdims=True)
+                p = jnp.exp(s - top)
+                p = (p * (1.0 / jnp.sum(p, axis=-1, keepdims=True))).astype(BF16)
+                prob[j, e, h] = p
+                outs.append(mm(p, qkv[j, e, :, gv * 128 : gv * 128 + 128]))
+            zero = jnp.zeros((rpad, 128), F32)
+            mx[j, e, :, :128] = jnp.where(low_half, zero, outs[2]).astype(BF16)
+            mx[j, e, :, 128:] = jnp.where(low_half, outs[0], outs[1]).astype(BF16)
+
+        s = mm_nt(mx[j].reshape(ex * rpad, 256), wbf[:, 512:]).reshape(ex, rpad, -1)
+        acc = s_a if j < 2 else s_b
+        if j % 2 == 0:
+            acc[...] = s
+        else:
+            acc[...] += s
+    mid[...] = jnp.zeros_like(mid)
+
+    @pl.loop(0, ex)
+    def _(e):
+        mid[e, :rows, :] = tok[e].astype(F32) + (s_a[e, :rows, :] + s_b[e, :rows, :])
+        xhat, _ = ln_stats(mid[e])
+        n2[e] = (xhat * g2[...] + s2[...]).astype(BF16)
+
+
+def attn_fwd(split, tok, g1, s1, g2, s2, wf):
+    ex, rows, width = tok.shape
+    rpad = -(-rows // 16) * 16
+    sds = jax.ShapeDtypeStruct
+    return pl.pallas_call(
+        attn_fwd_kernel,
+        out_shape=(
+            sds((ex, rpad, width), BF16), sds((4, ex, rpad, 640), BF16), sds((4, ex, 3, rpad, rpad), BF16),
+            sds((4, ex, rpad, 256), BF16), sds((ex, rpad, width), F32), sds((ex, rpad, width), BF16),
+        ),
+        in_specs=[SM, VM, VM, VM, VM, VM, ANY],
+        out_specs=(VM,) * 6,
+        scratch_shapes=[
+            pltpu.VMEM((2, width, 768), F32), pltpu.VMEM((width, 768), BF16),
+            pltpu.VMEM((ex, rpad, width), F32), pltpu.VMEM((ex, rpad, width), F32),
+            pltpu.SemaphoreType.DMA((2,)),
+        ],
+        compiler_params=pltpu.CompilerParams(vmem_limit_bytes=VLIM),
+        name="attn_fwd",
+    )(split, tok, g1, s1, g2, s2, wf)
+
+
+CH = 256
+
+
+def mlp_kernel(cot, mid, n2, wf, out, gn2, gup, gdn, cotp, cot_t, n2_t, ust, dst, br_a, br_b, gn_b, gst_u, gst_d, sem, gsem):
+    ex, rows, rpad = cot.shape[0], cot.shape[1], n2.shape[1]
+    t = ex * rpad
+    nch = wf.shape[3] // CH
+    order = [(j, i) for j in (1, 0, 3, 2) for i in range(nch)]
+
+    def fetch(n):
+        j, i = order[n]
+        b = n % 2
+        return (
+            pltpu.make_async_copy(wf.at[j, 1, :, pl.ds(i * CH, CH)], ust.at[b], sem.at[0, b]),
+            pltpu.make_async_copy(wf.at[j, 2, pl.ds(i * CH, CH), :], dst.at[b], sem.at[1, b]),
+        )
+
+    for cp in fetch(0):
+        cp.start()
+    cotp[...] = jnp.zeros_like(cotp)
+
+    @pl.loop(0, ex)
+    def _(e):
+        cotp[e, :rows, :] = cot[e]
+
+    cot_t[...] = cotp[...].reshape(t, -1).T
+    n2_t[...] = n2[...].reshape(t, -1).T
+
+    def store(n):
+        j, i = order[n]
+        b = n % 2
+        return (
+            pltpu.make_async_copy(gst_u.at[b], gup.at[j, :, pl.ds(i * CH, CH)], gsem.at[0, b]),
+            pltpu.make_async_copy(gst_d.at[b], gdn.at[j, :, pl.ds(i * CH, CH)], gsem.at[1, b]),
+        )
+
+    for n, (j, i) in enumerate(order):
+        if n + 1 < len(order):
+            for cp in fetch(n + 1):
+                cp.start()
+        for cp in fetch(n):
+            cp.wait()
+        u = ust[n % 2].astype(BF16)
+        dn = dst[n % 2].astype(BF16)
+        pre = mm(n2[...].reshape(t, -1), u)
+        ga = mm_nt(cotp[...].reshape(t, -1), dn)
+        phi = 0.5 * (1.0 + lax.erf(pre * (0.5 ** 0.5)))
+        act = (pre * phi).astype(BF16)
+        gpre = (ga * (phi + pre * jnp.exp(-0.5 * pre * pre) * 0.3989422804014327)).astype(BF16)
+        br = br_a if j < 2 else br_b
+        gn = gn2 if j < 2 else gn_b
+        b2 = mm(act, dn).reshape(ex, rpad, -1)
+        g2 = mm_nt(gpre, u).reshape(ex, rpad, -1)
+        if n % (2 * nch) == 0:
+            br[...] = b2
+            gn[...] = g2
+        else:
+            br[...] += b2
+            gn[...] += g2
+        if j < 2:
+            if n >= 2:
+                for cp in store(n - 2):
+                    cp.wait()
+            gst_d[n % 2] = mm(cot_t[...], act)
+            gst_u[n % 2] = mm(n2_t[...], gpre)
+            for cp in store(n):
+                cp.start()
+    out[...] = mid[...] + (br_a[...] + br_b[...])
+    gn2[...] += gn_b[...]
+    for n in (2 * nch - 2, 2 * nch - 1):
+        for cp in store(n):
+            cp.wait()
+
+
+def mlp(cot, mid, n2, wf):
+    ex, rows, width = cot.shape
+    rpad = n2.shape[1]
+    t = ex * rpad
+    sds = jax.ShapeDtypeStruct
+    act = (ex, rpad, width)
+    return pl.pallas_call(
+        mlp_kernel,
+        out_shape=(sds(act, F32), sds(act, F32), sds((2, width, 768), F32), sds((2, width, 768), F32)),
+        in_specs=[VM, VM, VM, ANY],
+        out_specs=(VM, VM, ANY, ANY),
+        scratch_shapes=[
+            pltpu.VMEM(act, BF16), pltpu.VMEM((width, t), BF16), pltpu.VMEM((width, t), BF16),
+            pltpu.VMEM((2, width, CH), F32), pltpu.VMEM((2, CH, width), F32),
+            pltpu.VMEM(act, F32), pltpu.VMEM(act, F32), pltpu.VMEM(act, F32),
+            pltpu.VMEM((2, width, CH), F32), pltpu.VMEM((2, width, CH), F32),
+            pltpu.SemaphoreType.DMA((2, 2)), pltpu.SemaphoreType.DMA((2, 2)),
+        ],
+        compiler_params=pltpu.CompilerParams(vmem_limit_bytes=VLIM),
+        name="mlp",
+    )(cot, mid, n2, wf)
+
+
+def ln_back(v, gy, gain):
+    xhat, rstd = ln_stats(v)
+    gx = gy * gain
+    m1 = jnp.mean(gx, axis=-1, keepdims=True)
+    m2 = jnp.mean(gx * xhat, axis=-1, keepdims=True)
+    return rstd * (gx - m1 - xhat * m2), jnp.sum(gy * xhat, axis=0, keepdims=True), jnp.sum(gy, axis=0, keepdims=True)
+
+
+def attn_bwd_kernel(tok, cot, mid, gn2, n1, qkv, prob, mx, g1, g2, wf, gtok, ga, gv, wst, wbf, gm, gml, gml_t, n1_t, gp, gmix, gn_a, gn_b, sem):
+    ex, rows, rpad = tok.shape[0], tok.shape[1], n1.shape[1]
+    t = ex * rpad
+
+    def fetch(n):
+        return pltpu.make_async_copy(wf.at[(1, 0, 3, 2)[n], 0], wst.at[n % 2], sem.at[n % 2])
+
+    fetch(0).start()
+    gv[...] = jnp.zeros_like(gv)
+    gm[...] = jnp.zeros_like(gm)
+
+    @pl.loop(0, ex)
+    def _(e):
+        back, dg, ds = ln_back(mid[e], gn2[e], g2[...])
+        gv[2:3, :] += dg
+        gv[3:4, :] += ds
+        gm[e, :rows, :] = cot[e].astype(F32) + back[:rows]
+        gml[e] = gm[e].astype(BF16)
+
+    gml_t[...] = gml[...].reshape(t, -1).T
+    n1_t[...] = n1[...].reshape(t, -1).T
+    low_half = lanes((rpad, 128)) < HD
+    scale = HD ** -0.5
+    for n, j in enumerate((1, 0, 3, 2)):
+        if n < 3:
+            fetch(n + 1).start()
+        fetch(n).wait()
+        wbf[...] = wst[n % 2].astype(BF16)
+        gmix[...] = mm(gml[...].reshape(t, -1), wbf[:, 512:]).astype(BF16).reshape(ex, rpad, 256)
+
+        @pl.loop(0, ex)
+        def _(e):
+            dq, dk, dv = [], [], []
+            for h, (gq, gk, gv_, high) in enumerate(HEADS):
+                gx = gmix[e, :, :128] if h == 2 else gmix[e, :, 128:]
+                gx = jnp.where(low_half != (high or h == 2), gx, jnp.zeros_like(gx))
+                p = prob[j, e, h]
+                dp = mm_nt(gx, qkv[j, e, :, gv_ * 128 : gv_ * 128 + 128])
+                pf = p.astype(F32)
+                pd = pf * dp
+                ds = (pd - pf * jnp.sum(pd, axis=-1, keepdims=True)).astype(BF16)
+                dq.append(mm(ds, qkv[j, e, :, gk * 128 : gk * 128 + 128]) * scale)
+                dk.append(mm_tn(ds, qkv[j, e, :, gq * 128 : gq * 128 + 128]) * scale)
+                dv.append(mm_tn(p, gx))
+            zero = jnp.zeros((rpad, 128), F32)
+            gp[e, :, 0:128] = jnp.where(low_half, dq[0], dq[1]).astype(BF16)
+            gp[e, :, 128:256] = jnp.where(low_half, dk[0], dk[1]).astype(BF16)
+            gp[e, :, 256:384] = jnp.where(low_half, dv[0], dv[1]).astype(BF16)
+            gp[e, :, 384:512] = jnp.where(low_half, dq[2], dv[2]).astype(BF16)
+            gp[e, :, 512:640] = jnp.where(low_half, dk[2], zero).astype(BF16)
+
+        gpf = gp[...].reshape(t, 640)
+        gn = gn_a if j < 2 else gn_b
+        g = mm_nt(gpf, wbf[:, :640]).reshape(ex, rpad, -1)
+        if n % 2 == 0:
+            gn[...] = g
+        else:
+            gn[...] += g
+        if j < 2:
+            ga[j, :, :512] = mm(n1_t[...], gpf[:, :512])
+            og = mm(gml_t[...], mx[j].reshape(t, 256))
+            ga[j, :, 512:640] = og[:, :128] + mm(n1_t[...], gpf[:, 512:640])
+            ga[j, :, 640:] = og[:, 128:]
+
+    @pl.loop(0, ex)
+    def _(e):
+        gy = gn_a[e, :rows, :] + gn_b[e, :rows, :]
+        back, dg, ds = ln_back(tok[e].astype(F32), gy, g1[...])
+        gv[0:1, :] += dg
+        gv[1:2, :] += ds
+        gtok[e] = gm[e, :rows, :] + back
+
+
+def attn_bwd(tok, cot, mid, gn2, n1, qkv, prob, mx, g1, g2, wf):
+    ex, rows, width = tok.shape
+    rpad = n1.shape[1]
+    t = ex * rpad
+    act = (ex, rpad, width)
+    sds = jax.ShapeDtypeStruct
+    return pl.pallas_call(
+        attn_bwd_kernel,
+        out_shape=(sds((ex, rows, width), F32), sds((2, width, 768), F32), sds((8, width), F32)),
+        in_specs=[VM] * 10 + [ANY],
+        out_specs=(VM, VM, VM),
+        scratch_shapes=[
+            pltpu.VMEM((2, width, 768), F32), pltpu.VMEM((width, 768), BF16),
+            pltpu.VMEM(act, F32), pltpu.VMEM(act, BF16), pltpu.VMEM((width, t), BF16), pltpu.VMEM((width, t), BF16),
+            pltpu.VMEM((ex, rpad, 640), BF16), pltpu.VMEM((ex, rpad, 256), BF16),
+            pltpu.VMEM(act, F32), pltpu.VMEM(act, F32),
+            pltpu.SemaphoreType.DMA((2,)),
+        ],
+        compiler_params=pltpu.CompilerParams(vmem_limit_bytes=VLIM),
+        name="attn_bwd",
+    )(tok, cot, mid, gn2, n1, qkv, prob, mx, g1, g2, wf)
+
+
+def reduce_kernel(ga, gu, gd, vec, out, gtok, res, vecs, outs, gtoks, po, cr, xr, zr, vown, vcr, vr,
+                  lsem, csend, crecv, xsend, xrecv, zsend, zrecv, vsend, vrecv):
+    me = Place()
+    greet(me, False, True)
+    sends = []
+
+    def go(cp):
+        cp.start()
+        sends.append(cp)
+        return cp
+
+    parts = (gd, gu, ga)
+    cc, ll = [], []
+    for p, g in enumerate(parts):
+        cc.append(go(rcopy(g.at[1], cr.at[p], csend.at[p], crecv.at[p], me.sib)))
+        lc = pltpu.make_async_copy(g.at[0], po.at[p], lsem.at[p])
+        lc.start()
+        ll.append(lc)
+    oc = go(rcopy(out, outs, csend.at[3], crecv.at[3], me.sib))
+    gc = go(rcopy(gtok, gtoks, csend.at[4], crecv.at[4], me.sib))
+    vc = go(rcopy(vec, vcr, csend.at[5], crecv.at[5], me.sib))
+    d = me.d
+    xs = []
+    for p in range(3):
+        cc[p].wait_recv()
+        ll[p].wait()
+        xp = []
+        for k in (0, 1, 2, 3):
+            s = me.zof(k) * 2 + 1 - me.x
+            po[p, s] += cr[p, s]
+            xp.append(go(rcopy(po.at[p, s], xr.at[p, me.zof(k)], xsend.at[p, k], xrecv.at[p, k], me.xnb)))
+        xs.append(xp)
+    for p in range(3):
+        for k in (0, 1, 2, 3):
+            s = me.zof(k) * 2 + me.x
+            po[p, s] += cr[p, s]
+    vc.wait_recv()
+    vown[...] = vec[...] + vcr[...]
+    vp = []
+    for k in range(1, 8):
+        to = lax.rem(d + k, 8)
+        vp.append(go(rcopy(vown, vr.at[7 - k], vsend.at[k - 1], vrecv.at[7 - k], (to, me.t))))
+    zs = []
+    for p in range(3):
+        for k in (1, 2, 3, 0):
+            s = me.zof(k) * 2 + me.x
+            xs[p][k].wait_recv()
+            po[p, s] += xr[p, me.zof(k)]
+            if k:
+                zs.append(go(rcopy(po.at[p, s], zr.at[p, 3 - k], zsend.at[p, k - 1], zrecv.at[p, 3 - k], me.znb(k))))
+    for p in range(3):
+        for k in (1, 2, 3):
+            rcopy(zr.at[p, k - 1], zr.at[p, k - 1], zsend.at[p, k - 1], zrecv.at[p, k - 1], me.znb(k)).wait_recv()
+        res[p] = po[p, d] + zr[p, 0] + zr[p, 1] + zr[p, 2]
+    for k in range(1, 8):
+        rcopy(vown, vr.at[k - 1], vsend.at[k - 1], vrecv.at[k - 1], me.sib).wait_recv()
+    acc = None
+    for i in range(8):
+        k = lax.rem(i - d + 8, 8)
+        slot = jnp.maximum(k - 1, 0)
+        term = jnp.where(k == 0, vown[...], vr[slot])
+        acc = term if acc is None else acc + term
+    vecs[...] = acc
+    oc.wait_recv()
+    gc.wait_recv()
+    for cp in sends:
+        cp.wait_send()
+
+
+def reduce(ga, gu, gd, vec, out, gtok):
+    sds = jax.ShapeDtypeStruct
+    dma = pltpu.SemaphoreType.DMA
+    blk = ga.shape[1:]
+    return pl.pallas_call(
+        reduce_kernel,
+        out_shape=(sds((3,) + blk[1:], F32), sds(vec.shape, F32), sds(out.shape, F32), sds(gtok.shape, F32)),
+        in_specs=[ANY] * 3 + [VM] + [ANY] * 2,
+        out_specs=(VM, VM, ANY, ANY),
+        scratch_shapes=[
+            pltpu.VMEM((3,) + blk, F32), pltpu.VMEM((3,) + blk, F32), pltpu.VMEM((3, 4) + blk[1:], F32),
+            pltpu.VMEM((3, 3) + blk[1:], F32), pltpu.VMEM(vec.shape, F32), pltpu.VMEM(vec.shape, F32),
+            pltpu.VMEM((7,) + vec.shape, F32),
+            dma((3,)), dma((6,)), dma((6,)), dma((3, 4)), dma((3, 4)), dma((3, 3)), dma((3, 3)), dma((7,)), dma((7,)),
+        ],
+        compiler_params=pltpu.CompilerParams(collective_id=1, has_side_effects=True, vmem_limit_bytes=VLIM),
+        name="reduce",
+    )(ga, gu, gd, vec, out, gtok)
+
+
+def fast_device(tokens, cotangent, split_point, w_qkv, w_out, w_up, w_down, gain_one, shift_one, gain_two, shift_two):
+    batch, length, width = tokens.shape
+    c = lax.rem(lax.axis_index("tensor"), 2)
+    d = lax.axis_index("dp")
+    ex = batch // 2
+    tok = lax.dynamic_slice_in_dim(tokens, c * ex, ex, 0)
+    cot = lax.dynamic_slice_in_dim(cotangent, c * ex, ex, 0)
+    split = lax.dynamic_slice_in_dim(split_point, c * ex, ex, 0)
+    q, k, v, o = w_qkv[0], w_qkv[1], w_qkv[2], w_out.T
+    attn = jnp.concatenate(
+        [q[:, :128], k[:, :128], v[:, :128], q[:, 128:], v[:, 128:], k[:, 128:], o[:, 128:], o[:, :128]], axis=1
+    )
+    own = jnp.stack([attn, w_up, w_down]).astype(F32).reshape(3, 8, width // 8, 768)
+    row = lambda v_: v_.reshape(1, -1)
+    g1, s1, g2, s2 = row(gain_one), row(shift_one), row(gain_two), row(shift_two)
+    wf = gather(own).reshape(4, 3, width, 768)
+    n1, qkv, prob, mx, mid, n2 = attn_fwd(split, tok, g1, s1, g2, s2, wf)
+    out, gn2, gup, gdn = mlp(cot, mid, n2, wf)
+    gtok, ga, vec = attn_bwd(tok, cot, mid, gn2, n1, qkv, prob, mx, g1, g2, wf)
+    blk = (2, 8, width // 8, 768)
+    res, vecs, outs, gtoks = reduce(ga.reshape(blk), gup.reshape(blk), gdn.reshape(blk), vec, out, gtok)
+
+    def both(mine, other):
+        first = jnp.where(c == 0, mine, other)
+        second = jnp.where(c == 0, other, mine)
+        return jnp.concatenate([first, second], axis=0).astype(BF16)
+
+    output = both(out[:, :length], outs[:, :length])
+    grad_tokens = both(gtok, gtoks)
+    rd, ru, ra = res[0], res[1], res[2]
+    gq = jnp.concatenate([ra[:, 0:128], ra[:, 384:448]], axis=1)
+    gk = jnp.concatenate([ra[:, 128:256], ra[:, 512:576]], axis=1)
+    gv = jnp.concatenate([ra[:, 256:384], ra[:, 448:512]], axis=1)
+    go = jnp.concatenate([ra[:, 640:768], ra[:, 576:640]], axis=1).T
+    mine = lax.dynamic_slice_in_dim(vecs, d * (width // 8), width // 8, 1)
+    return (
+        output, grad_tokens, jnp.stack([gq, gk, gv]), go, ru, rd.T, mine[0], mine[1], mine[2], mine[3],
+    )
 
 
 def layer_norm(values, gain_vec, shift_vec):
@@ -193,6 +733,7 @@
         P("dp"),
         P("dp"),
     )
+    fast = mesh.shape["dp"] == 8 and mesh.shape["tensor"] == 4
     return jax.shard_map(
-        per_device, mesh=mesh, in_specs=in_specs, out_specs=out_specs, check_vma=False
-    )
+        fast_device if fast else per_device, mesh=mesh, in_specs=in_specs, out_specs=out_specs, check_vma=False
+    )

time: 762 us -> 479 us (0.63)
  waiting for transfers between devices: 529 us -> 0 us
  Pallas kernels: 0 us -> 441 us
  matrix products: 75.3 us -> 0 us
  other arithmetic: 58.8 us -> 10.9 us
  blocking collectives: 37.2 us -> 0 us
  local copies, waits for them, and re-layouts: 36.4 us -> 16.6 us
  between operations: 15.8 us -> 1.29 us
    pallas_call x0 -> x5, Pallas kernels: none -> 441 us  [the longest x1 221 us: gather(): pl.pallas_call(gather_kernel, out_shape=jax.ShapeDtypeStruct((4,) + n, F3...]
    psum x3 -> x0, waiting for transfers between devices: 370 us -> none  [the longest x1 175 us: per_device(): output = (middle + lax.psum(branch, 'tensor')).astype(jnp.bfloat16)]
    reduce_scatter x2 -> x0, waiting for transfers between devices: 84.7 us -> none  [the longest x1 72.4 us: per_device(): lax.psum_scatter(grad_down_local, 'dp', scatter_dimension=1, tiled=True)]
    dot_general x18 -> x0, matrix products: 75.3 us -> none  [the longest x1 7.44 us: per_device(): jnp.einsum('btd,btf->df', normed_two, grad_pre, preferred_element_type=jn...]
    unnamed x9 -> x0, waiting for transfers between devices: 73.8 us -> none
    unnamed x1 -> x0, blocking collectives: 37.2 us -> none
    reduce_sum x9 -> x0, other arithmetic: 28 us -> none  [the longest x3 13.4 us: layer_norm(): return centered * lax.rsqrt(variance + EPSILON) * gain_vec + shift_vec]
    convert_element_type x5 -> x1, other arithmetic: 29.5 us -> 3.41 us  [fast_device(): jnp.stack([attn, w_up, w_down]).astype(F32).reshape(3, 8, width // 8, 768)]
  transfers between devices with their start and end apart: 7 -> 0, of which waited for: 7 -> 0; matrix products, arithmetic and copies ran while one was open for 11% -> 0% of each run, Pallas kernels for 0% -> 0%
where the time goes in v1:
time: 479 us; the launch traced here: 470 us
  Pallas kernels  441 us (92%)
  local copies, waits for them, and re-layouts  16.6 us (3%)
  other arithmetic  10.9 us (2%)
    pallas_call x1, Pallas kernels, gather(): pl.pallas_call(gather_kernel, out_shape=jax.ShapeDtypeStruct((4,) + n, F3...  221 us
    pallas_call x1, Pallas kernels, reduce(): pl.pallas_call(reduce_kernel, out_shape=(sds((3,) + blk[1:], F32), sds(ve...  105 us
    pallas_call x1, Pallas kernels, attn_bwd(): pl.pallas_call(attn_bwd_kernel, out_shape=(sds((ex, rows, width), F32), s...  48.4 us
    pallas_call x1, Pallas kernels, attn_fwd(): pl.pallas_call(attn_fwd_kernel, out_shape=(sds((ex, rpad, width), BF16),...  34.9 us
    pallas_call x1, Pallas kernels, mlp(): pl.pallas_call(mlp_kernel, out_shape=(sds(act, F32), sds(act, F32), sds((...  31.7 us

profile of v1, /device:TPU:0, one launch (start us, length us, event | category | flops | bytes accessed | tf_op | source)
XLA Modules:
  0.0 470.1 jit_solution(4661649914135140311)
XLA Ops:
  0.7 1.2 dynamic_slice.13.split
  1.9 1.3 reshape.51.g1
  3.2 1.3 reshape.53.g2
  4.4 1.3 reshape.52.s1
  5.7 1.3 reshape.54.s2
  7.0 1.2 slice_bitcast_fusion.3
  8.3 0.8 copy-done.5
  9.2 0.6 copy.21
  9.8 3.4 constant_dynamic-slice_fusion.1
  13.3 3.4 maximum_convert_fusion.own
  16.7 221.0 %gather.1 = f32[4,3,8,96,768]{4,3,2,1,0:T(8,128)} custom-call(f32[3,8,96,768]{3,2,1,0:T(8,128)} %maximum_convert_fusion.own), custom_call_target="tpu_custom_call" | custom-call | tf_op jit(solution)/shard_map/gather/pallas_call | solution.py:116
  237.6 34.9 %attn_fwd.1 = (bf16[3,272,768]{2,1,0:T(8,128)(2,1)}, bf16[4,3,272,640]{3,2,1,0:T(8,128)(2,1)}, bf16[4,3,3,272,272]{4,3,2,1,0:T(8,128)(2,1)}, bf16[4,3,272,256]{3...) custom-call(s32[3]{0:T(128)} %dynamic_slice.13.split, ...), custom_call_target="tpu_custom_call" | custom-call | tf_op jit(solution)/shard_map/attn_fwd/pallas_call | solution.py:207
  272.5 31.7 %mlp.1 = (f32[3,272,768]{2,1,0:T(8,128)}, f32[3,272,768]{2,1,0:T(8,128)}, f32[2,768,768]{2,1,0:T(8,128)}, f32[2,768,768]{2,1,0:T(8,128)}) custom-call(bf16[3,260,768]{2,1,0:T(8,128)(2,1)} %get-tuple-element.77.cot, f32[3,272,768]{2,1,0:T(8,128)} %get-tuple-element.27.mid, bf16[3,272,768]{2,1,0:T(8,128)(2,1)} %get-tuple-element.28.n2, f32[4,3,768,768]{3,2,1,0:T(8,128)} %bitcast.39), custom_call_target="tpu_custom_call" | custom-call | tf_op jit(solution)/shard_map/mlp/pallas_call | solution.py:305
  304.2 48.4 %attn_bwd.1 = (f32[3,260,768]{2,1,0:T(8,128)}, f32[2,768,768]{2,1,0:T(8,128)}, f32[8,768]{1,0:T(8,128)}) custom-call(bf16[3,260,768]{2,1,0:T(8,128)(2,1)} %get-tuple-element.76.tok, bf16[3,260,768]{2,1,0:T(8,128)(2,1)} %get-tuple-element.77.cot, f32[3,272,768]{2,1,0:T(8,128)} %get-tuple-element.27.mid, f32[3,272,768]{2,1,0:T(8,128)} %get-tuple-element.30.gn2, ...), custom_call_target="tpu_custom_call" | custom-call | tf_op jit(solution)/shard_map/attn_bwd/pallas_call | solution.py:409
  352.7 105.4 %reduce.1 = (f32[3,96,768]{2,1,0:T(8,128)}, f32[8,768]{1,0:T(8,128)}, f32[3,272,768]{2,1,0:T(8,128)}, f32[3,260,768]{2,1,0:T(8,128)}) custom-call(f32[2,8,96,768]{3,2,1,0:T(8,128)} %bitcast.44, f32[2,8,96,768]{3,2,1,0:T(8,128)} %bitcast.42, f32[2,8,96,768]{3,2,1,0:T(8,128)} %bitcast.43, f32[8,768]{1,0:T(8,128)} %get-tuple-element.38.vec, ...), custom_call_target="tpu_custom_call" | custom-call | tf_op jit(solution)/shard_map/reduce/pallas_call | solution.py:499
  458.1 2.8 select_convert_fusion.3
  461.2 0.7 copy-done.1
  461.9 0.6 select_convert_fusion.1
  462.5 1.6 pad_maximum_fusion.1
  464.2 1.6 pad_maximum_fusion
  465.8 0.8 constant_dynamic-slice_fusion
  467.1 0.9 slice_bitcast_fusion
  468.1 0.7 copy.22
  468.9 0.7 pad_maximum_fusion.2
  (25 shorter events, 1.1 us)
Async XLA Ops:
  8.2 1.0 copy-start.5
  9.8 3.4 copy-start.2
  9.8 3.4 copy-start.3
  458.1 3.2 copy-start
  458.1 3.9 copy-start.1
  464.2 2.9 copy-start.4

commit v2 on v0

--- a/solution.py
+++ b/solution.py
@@ -3,13 +3,594 @@
 import jax
 import jax.numpy as jnp
 from jax import lax
+from jax.experimental import pallas as pl
+from jax.experimental.pallas import tpu as pltpu
 from jax.sharding import PartitionSpec as P
 
 HD = 64
 PATCHES = 196
-
-
 EPSILON = 1e-05
+MESH = pl.DeviceIdType.MESH
+F32 = jnp.float32
+BF16 = jnp.bfloat16
+CH = 256
+
+
+def mm(a, b):
+    return jnp.dot(a, b, preferred_element_type=F32)
+
+
+def mm_nt(a, b):
+    return lax.dot_general(a, b, (((1,), (1,)), ((), ())), preferred_element_type=F32)
+
+
+def mm_tn(a, b):
+    return lax.dot_general(a, b, (((0,), (0,)), ((), ())), preferred_element_type=F32)
+
+
+def ln_stats(v):
+    mean = jnp.mean(v, axis=-1, keepdims=True)
+    cen = v - mean
+    var = jnp.mean(cen * cen, axis=-1, keepdims=True)
+    rstd = lax.rsqrt(var + EPSILON)
+    return cen * rstd, rstd
+
+
+def ln_back(v, gy, gain):
+    xhat, rstd = ln_stats(v)
+    gx = gy * gain
+    m1 = jnp.mean(gx, axis=-1, keepdims=True)
+    m2 = jnp.mean(gx * xhat, axis=-1, keepdims=True)
+    return rstd * (gx - m1 - xhat * m2), jnp.sum(gy * xhat, axis=0, keepdims=True), jnp.sum(gy, axis=0, keepdims=True)
+
+
+def rcopy(src, dst, ssem, rsem, dev):
+    return pltpu.make_async_remote_copy(
+        src_ref=src, dst_ref=dst, send_sem=ssem, recv_sem=rsem, device_id=dev, device_id_type=MESH
+    )
+
+
+HEADS = ((0, 1, 2, False), (0, 1, 2, True), (3, 4, 3, False))
+SL = 512
+
+
+def layer_kernel(
+    split, tokens, cots, g1, s1, g2, s2, own,
+    wf, res, vecs, out, outs, gtok, gtoks,
+    tok, cotr, cotp, n1, qkv, prob, mx, mid, br, gn, n2, ust, dst, wbf, ta, tb, gp, gmix,
+    po, ps, cr, xr, zr, gv, vcr, vr,
+    isem, wsem, csend, crecv, ysend, yrecv, dsend, drecv, zsend, zrecv, xsend, xrecv,
+    rcs, rcr, rxs, rxr, rzs, rzr, osend, orecv, vsend, vrecv,
+):
+    ex, rows, width = tok.shape
+    rpad = n1.shape[1]
+    t = ex * rpad
+    d, tt = lax.axis_index("dp"), lax.axis_index("tensor")
+    z, x = d // 2, lax.rem(d, 2)
+    y, c = tt // 2, lax.rem(tt, 2)
+    sib = (d, y * 2 + 1 - c)
+    ynb = (d, (1 - y) * 2 + c)
+    xnb = (z * 2 + 1 - x, tt)
+
+    def band(i):
+        return pl.ds(pl.multiple_of(i * (width // 8), width // 8), width // 8)
+
+    def zof(k):
+        return lax.rem(z + k, 4)
+
+    def znb(k):
+        return (zof(k) * 2 + x, tt)
+
+    peers = [sib, ynb] + [(lax.rem(d + k, 8), tt) for k in range(1, 8)]
+    barrier = pltpu.get_barrier_semaphore()
+    for p in peers:
+        pl.semaphore_signal(barrier, 1, device_id=p, device_id_type=MESH)
+    pl.semaphore_wait(barrier, len(peers))
+
+    def y_slice(p):
+        return rcopy(own.at[p, band(d), :SL], wf.at[1, p, band(d), :SL], ysend.at[p], yrecv.at[p], ynb)
+
+    def y_direct(p):
+        return rcopy(own.at[p, :, SL:], wf.at[1, p, :, SL:], dsend.at[p], drecv.at[p], ynb)
+
+    def c_first(p):
+        return rcopy(own.at[p], wf.at[0, p], csend.at[p], crecv.at[p], sib)
+
+    def c_second(p):
+        return rcopy(wf.at[1, p], wf.at[2, p], csend.at[3 + p], crecv.at[3 + p], sib)
+
+    def z_copy(p, k, slot, sem):
+        blk = wf.at[1, p, band(slot), :SL]
+        return rcopy(blk, blk, zsend.at[p, k - 1], zrecv.at[p, sem], znb(k))
+
+    def x_copy(p, k, slot):
+        blk = wf.at[1, p, band(slot), :SL]
+        return rcopy(blk, blk, xsend.at[p, k], xrecv.at[p, k], xnb)
+
+    def g1_step(p):
+        y_slice(p).wait_recv()
+        for k in (1, 2, 3):
+            z_copy(p, k, d, 3 - k).start()
+        x_copy(p, 0, d).start()
+
+    def g2_step(p):
+        for k in (1, 2, 3):
+            s = zof(k) * 2 + x
+            z_copy(p, k, s, k - 1).wait_recv()
+            x_copy(p, k, s).start()
+
+    def g3_step(p):
+        for k in (0, 1, 2, 3):
+            x_copy(p, k, zof(k) * 2 + 1 - x).wait_recv()
+        y_direct(p).wait_recv()
+        c_second(p).start()
+
+    def fetch(j, p, i, b):
+        def src(ref):
+            if p == 2:
+                return ref.at[pl.ds(pl.multiple_of(i * CH, CH), CH), :]
+            return ref.at[:, pl.ds(pl.multiple_of(i * CH, CH), CH)]
+
+        dstr = (dst if p == 2 else ust).at[b]
+        sem = wsem.at[1 if p == 2 else 0, b]
+
+        @pl.when(j == 0)
+        def _():
+            pltpu.make_async_copy(src(own.at[p]), dstr, sem).start()
+
+        @pl.when(j > 0)
+        def _():
+            pltpu.make_async_copy(src(wf.at[jnp.maximum(j - 1, 0), p]), dstr, sem).start()
+
+    def fetched(p, b):
+        dstr = (dst if p == 2 else ust).at[b]
+        pltpu.make_async_copy(dstr, dstr, wsem.at[1 if p == 2 else 0, b]).wait()
+
+    def load_attn(j):
+        fetch(j, 0, 0, 0)
+        for i in range(3):
+            if i < 2:
+                fetch(j, 0, i + 1, (i + 1) % 2)
+            fetched(0, i % 2)
+            wbf[:, i * CH : (i + 1) * CH] = ust[i % 2].astype(BF16)
+
+    def c_grad(u, slot):
+        return rcopy(ps.at[slot], cr.at[u], rcs.at[u], rcr.at[u], sib)
+
+    def x_grad(u, pu, side):
+        return rcopy(po.at[pu, :, side], xr.at[u], rxs.at[u], rxr.at[u], xnb)
+
+    def z_grad(u, pu, k, slot):
+        return rcopy(po.at[pu, zof(k), x], zr.at[u, slot], rzs.at[u, k - 1], rzr.at[u, slot], znb(k))
+
+    def r1_step(u, pu):
+        c_grad(u, 0).wait_recv()
+        po[pu, :, 1 - x] += cr[u, :, 1 - x]
+        x_grad(u, pu, 1 - x).start()
+        po[pu, :, x] += cr[u, :, x]
+
+    def r2_step(u, pu):
+        x_grad(u, pu, x).wait_recv()
+        po[pu, :, x] += xr[u]
+        for k in (1, 2, 3):
+            z_grad(u, pu, k, 3 - k).start()
+
+    def r3_step(u, pu):
+        for k in (1, 2, 3):
+            z_grad(u, pu, k, k - 1).wait_recv()
+        res[u] = po[pu, z, x] + zr[u, 0] + zr[u, 1] + zr[u, 2]
+
+    for p in range(3):
+        y_slice(p).start()
+    c_first(0).start()
+    y_direct(0).start()
+    tin = pltpu.make_async_copy(tokens.at[pl.ds(c * ex, ex)], tok, isem.at[0])
+    tin.start()
+    tin.wait()
+    n1[...] = jnp.zeros_like(n1)
+    mid[...] = jnp.zeros_like(mid)
+    cotp[...] = jnp.zeros_like(cotp)
+    gv[...] = jnp.zeros_like(gv)
+
+    @pl.loop(0, ex)
+    def _(e):
+        v = tok[e].astype(F32)
+        xhat, _ = ln_stats(v)
+        n1[e, :rows, :] = (xhat * g1[...][None] + s1[...][None]).astype(BF16)
+        mid[e, :rows, :] = v
+
+    c_first(1).start()
+    c_first(2).start()
+
+    low_half = lax.broadcasted_iota(jnp.int32, (rpad, 128), 1) < HD
+    qi = lax.broadcasted_iota(jnp.int32, (rpad, rpad), 0)
+    kj = lax.broadcasted_iota(jnp.int32, (rpad, rpad), 1)
+
+    @pl.loop(0, 4)
+    def _(j):
+        @pl.when(j == 1)
+        def _():
+            g1_step(0)
+            c_first(0).wait_recv()
+
+        @pl.when(j == 2)
+        def _():
+            ccopy = pltpu.make_async_copy(cots.at[pl.ds(c * ex, ex)], cotr, isem.at[1])
+            ccopy.start()
+            ccopy.wait()
+
+            @pl.loop(0, ex)
+            def _(e):
+                cotp[e, :rows, :] = cotr[e]
+
+            ta[...] = cotp[...].reshape(t, width).T
+            g2_step(0)
+            y_direct(1).start()
+            y_direct(2).start()
+            g3_step(0)
+            g1_step(1)
+
+        @pl.when(j == 3)
+        def _():
+            g1_step(2)
+            c_second(0).wait_recv()
+
+        load_attn(j)
+        qkv[j] = mm(n1[...].reshape(t, width), wbf[:, :640]).astype(BF16).reshape(ex, rpad, 640)
+
+        @pl.loop(0, ex)
+        def _(e):
+            allowed = kj <= jnp.maximum(qi, PATCHES - 1 + split[c * ex + e])
+            outs_h = []
+            for h, (gq, gk, gvv, high) in enumerate(HEADS):
+                q = qkv[j, e, :, gq * 128 : gq * 128 + 128]
+                q = jnp.where(low_half != high, q, jnp.zeros_like(q))
+                k = qkv[j, e, :, gk * 128 : gk * 128 + 128]
+                s = mm_nt(q, k) * (HD ** -0.5)
+                s = jnp.where(allowed, s, -1e30)
+                top = jnp.max(s, axis=-1, keepdims=True)
+                p = jnp.exp(s - top)
+                p = (p * (1.0 / jnp.sum(p, axis=-1, keepdims=True))).astype(BF16)
+                prob[j, e, h] = p
+                outs_h.append(mm(p, qkv[j, e, :, gvv * 128 : gvv * 128 + 128]))
+            zero = jnp.zeros((rpad, 128), F32)
+            mx[j, e, :, :128] = jnp.where(low_half, zero, outs_h[2]).astype(BF16)
+            mx[j, e, :, 128:] = jnp.where(low_half, outs_h[0], outs_h[1]).astype(BF16)
+
+        mid[...] += mm_nt(mx[j].reshape(t, 256), wbf[:, 512:]).reshape(ex, rpad, width)
+
+    g2_step(1)
+
+    @pl.loop(0, ex)
+    def _(e):
+        keep = lax.broadcasted_iota(jnp.int32, (rpad, 1), 0) < rows
+        v = jnp.where(keep, mid[e], 0.0)
+        mid[e] = v
+        xhat, _ = ln_stats(v)
+        n2[e] = (xhat * g2[...][None] + s2[...][None]).astype(BF16)
+        br[e] = v
+        gn[e] = jnp.zeros((rpad, width), F32)
+
+    tb[...] = n2[...].reshape(t, width).T
+
+    def chunk(b):
+        u = ust[b].astype(BF16)
+        dn = dst[b].astype(BF16)
+        pre = mm(n2[...].reshape(t, width), u)
+        ga = mm_nt(cotp[...].reshape(t, width), dn)
+        phi = 0.5 * (1.0 + lax.erf(pre * (0.5 ** 0.5)))
+        act = (pre * phi).astype(BF16)
+        gpre = (ga * (phi + pre * jnp.exp(-0.5 * pre * pre) * 0.3989422804014327)).astype(BF16)
+        br[...] += mm(act, dn).reshape(ex, rpad, width)
+        gn[...] += mm_nt(gpre, u).reshape(ex, rpad, width)
+        return act, gpre
+
+    def fetch2(j, i, b):
+        fetch(j, 1, i, b)
+        fetch(j, 2, i, b)
+
+    def fetched2(b):
+        fetched(1, b)
+        fetched(2, b)
+
+    c_first(1).wait_recv()
+    c_first(2).wait_recv()
+    fetch2(1, 0, 0)
+    shape5 = po.shape[1:]
+
+    @pl.loop(0, 6)
+    def _(n):
+        i, b = n // 2, lax.rem(n, 2)
+
+        @pl.when(n < 5)
+        def _():
+            fetch2(b, (n + 1) // 2, 1 - b)
+
+        fetched2(b)
+        act, gpre = chunk(b)
+        gd = mm(ta[...], act).reshape(shape5)
+        gu = mm(tb[...], gpre).reshape(shape5)
+        slot = 2 * lax.rem(i, 2)
+
+        @pl.when(b == 0)
+        def _():
+            @pl.when(i == 2)
+            def _():
+                c_grad(0, 0).wait_send()
+                c_grad(1, 1).wait_send()
+
+            ps[slot] = gd
+            ps[slot + 1] = gu
+            c_grad(2 * i, slot).start()
+            c_grad(2 * i + 1, slot + 1).start()
+
+        @pl.when(b == 1)
+        def _():
+            po[2 * i] = gd
+            po[2 * i + 1] = gu
+            r1_step(2 * i, 2 * i)
+            r1_step(2 * i + 1, 2 * i + 1)
+
+        @pl.when(n == 1)
+        def _():
+            g2_step(2)
+
+        @pl.when(n == 3)
+        def _():
+            g3_step(1)
+
+    g3_step(2)
+    fetch2(2, 0, 0)
+
+    @pl.loop(0, 6)
+    def _(n):
+        b = lax.rem(n, 2)
+
+        @pl.when(n == 2)
+        def _():
+            c_second(1).wait_recv()
+            c_second(2).wait_recv()
+
+        @pl.when(n < 5)
+        def _():
+            fetch2(2 + (n + 1) // 3, lax.rem(n + 1, 3), 1 - b)
+
+        fetched2(b)
+        chunk(b)
+
+    o_copy = rcopy(br, outs, osend.at[0], orecv.at[0], sib)
+    o_copy.start()
+    o_keep = pltpu.make_async_copy(br, out, isem.at[2])
+    o_keep.start()
+    r2_step(0, 0)
+    r2_step(1, 1)
+
+    @pl.loop(0, ex)
+    def _(e):
+        back, dg, ds = ln_back(mid[e], gn[e], g2[...][None])
+        gv[2:3, :] += dg
+        gv[3:4, :] += ds
+        gm = cotp[e].astype(F32) + back
+        mid[e] = gm
+        n2[e] = gm.astype(BF16)
+        gn[e] = jnp.zeros((rpad, width), F32)
+
+    gml = n2
+    ta[...] = gml[...].reshape(t, width).T
+    tb[...] = n1[...].reshape(t, width).T
+    scale = HD ** -0.5
+
+    @pl.loop(0, 4)
+    def _(n):
+        j = jnp.where(n < 2, 1 - n, n)
+        load_attn(j)
+        gmix[...] = mm(gml[...].reshape(t, width), wbf[:, 512:]).astype(BF16).reshape(ex, rpad, 256)
+
+        @pl.loop(0, ex)
+        def _(e):
+            dq, dk, dv = [], [], []
+            for h, (gq, gk, gvv, high) in enumerate(HEADS):
+                gx = gmix[e, :, :128] if h == 2 else gmix[e, :, 128:]
+                gx = jnp.where(low_half != (high or h == 2), gx, jnp.zeros_like(gx))
+                p = prob[j, e, h]
+                dp = mm_nt(gx, qkv[j, e, :, gvv * 128 : gvv * 128 + 128])
+                pf = p.astype(F32)
+                pd = pf * dp
+                ds = (pd - pf * jnp.sum(pd, axis=-1, keepdims=True)).astype(BF16)
+                dq.append(mm(ds, qkv[j, e, :, gk * 128 : gk * 128 + 128]) * scale)
+                dk.append(mm_tn(ds, qkv[j, e, :, gq * 128 : gq * 128 + 128]) * scale)
+                dv.append(mm_tn(p, gx))
+            zero = jnp.zeros((rpad, 128), F32)
+            gp[e, :, 0:128] = jnp.where(low_half, dq[0], dq[1]).astype(BF16)
+            gp[e, :, 128:256] = jnp.where(low_half, dk[0], dk[1]).astype(BF16)
+            gp[e, :, 256:384] = jnp.where(low_half, dv[0], dv[1]).astype(BF16)
+            gp[e, :, 384:512] = jnp.where(low_half, dq[2], dv[2]).astype(BF16)
+            gp[e, :, 512:640] = jnp.where(low_half, dk[2], zero).astype(BF16)
+
+        gpf = gp[...].reshape(t, 640)
+        gn[...] += mm_nt(gpf, wbf[:, :640]).reshape(ex, rpad, width)
+
+        def grads(write):
+            write(0, mm(tb[...], gpf[:, :256]).reshape(shape5))
+            write(1, mm(tb[...], gpf[:, 256:512]).reshape(shape5))
+            og = mm(ta[...], mx[j].reshape(t, 256))
+            k2 = mm(tb[...], gpf[:, 512:640])
+            write(2, jnp.concatenate([og[:, :128] + k2, og[:, 128:]], axis=1).reshape(shape5))
+
+        @pl.when(n == 0)
+        def _():
+            for u in range(2, 6):
+                c_grad(u, (0, 1, 2, 3, 0, 1)[u]).wait_send()
+
+            def write(i, g):
+                ps[i] = g
+                c_grad(6 + i, i).start()
+
+            grads(write)
+
+        @pl.when(n == 1)
+        def _():
+            r3_step(0, 0)
+            r3_step(1, 1)
+            r2_step(2, 2)
+            r2_step(3, 3)
+            for u in range(2):
+                x_grad(u, u, 1 - x).wait_send()
+                for k in (1, 2, 3):
+                    z_grad(u, u, k, 3 - k).wait_send()
+
+            def write(i, g):
+                pu = (0, 1, 6)[i]
+                po[pu] = g
+                r1_step(6 + i, pu)
+
+            grads(write)
+
+        @pl.when(n == 2)
+        def _():
+            r3_step(2, 2)
+            r3_step(3, 3)
+            r2_step(4, 4)
+            r2_step(5, 5)
+
+    r2_step(6, 0)
+
+    o_copy.wait_send()
+    o_keep.wait()
+
+    @pl.loop(0, ex)
+    def _(e):
+        back, dg, ds = ln_back(tok[e].astype(F32), gn[e, :rows, :], g1[...][None])
+        gv[0:1, :] += dg
+        gv[1:2, :] += ds
+        br[e, :rows, :] = mid[e, :rows, :] + back
+
+    t_copy = rcopy(br, gtoks, osend.at[1], orecv.at[1], sib)
+    t_copy.start()
+    t_keep = pltpu.make_async_copy(br, gtok, isem.at[2])
+    t_keep.start()
+    v_copy = rcopy(gv, vcr, osend.at[2], orecv.at[2], sib)
+    v_copy.start()
+    r2_step(7, 1)
+    v_copy.wait()
+    gv[...] += vcr[...]
+    v_sends = []
+    for k in range(1, 8):
+        cp = rcopy(gv, vr.at[7 - k], vsend.at[k - 1], vrecv.at[7 - k], (lax.rem(d + k, 8), tt))
+        cp.start()
+        v_sends.append(cp)
+    r2_step(8, 6)
+    for u in range(4, 9):
+        r3_step(u, (0, 1, 2, 3, 4, 5, 0, 1, 6)[u])
+    for k in range(1, 8):
+        rcopy(gv, vr.at[k - 1], vsend.at[k - 1], vrecv.at[k - 1], sib).wait_recv()
+    acc = None
+    for i in range(8):
+        k = lax.rem(i - d + 8, 8)
+        term = jnp.where(k == 0, gv[...], vr[jnp.maximum(k - 1, 0)])
+        acc = term if acc is None else acc + term
+    vecs[...] = acc
+
+    c_second(1).wait_send()
+    o_copy.wait_recv()
+    t_copy.wait()
+    t_keep.wait()
+    for cp in v_sends:
+        cp.wait_send()
+    for p in range(3):
+        y_slice(p).wait_send()
+        y_direct(p).wait_send()
+        c_first(p).wait_send()
+        for k in (1, 2, 3):
+            z_copy(p, k, d, 3 - k).wait_send()
+        for k in (0, 1, 2, 3):
+            x_copy(p, k, d).wait_send()
+    c_second(0).wait_send()
+    c_second(2).wait_send()
+    for u in range(2, 9):
+        pu = (0, 1, 2, 3, 4, 5, 0, 1, 6)[u]
+        x_grad(u, pu, 1 - x).wait_send()
+        for k in (1, 2, 3):
+            z_grad(u, pu, k, 3 - k).wait_send()
+    for u in range(6, 9):
+        c_grad(u, u - 6).wait_send()
+
+
+def layer(split, tokens, cots, g1, s1, g2, s2, own):
+    batch, rows, width = tokens.shape
+    ex = batch // 2
+    rpad = -(-rows // 16) * 16
+    t = ex * rpad
+    band = width // 8
+    sds = jax.ShapeDtypeStruct
+    dma = pltpu.SemaphoreType.DMA
+    vm = pltpu.VMEM
+    ANY = pl.BlockSpec(memory_space=pl.ANY)
+    VM = pl.BlockSpec(memory_space=pltpu.VMEM)
+    SM = pl.BlockSpec(memory_space=pltpu.SMEM)
+    act = (ex, rpad, width)
+    return pl.pallas_call(
+        layer_kernel,
+        out_shape=(
+            sds((3, 3, width, 768), F32), sds((9, band, CH), F32), sds((8, width), F32),
+            sds(act, F32), sds(act, F32), sds(act, F32), sds(act, F32),
+        ),
+        in_specs=[SM, ANY, ANY, VM, VM, VM, VM, ANY],
+        out_specs=(ANY, VM, VM, ANY, ANY, ANY, ANY),
+        scratch_shapes=[
+            vm((ex, rows, width), BF16), vm((ex, rows, width), BF16), vm(act, BF16), vm(act, BF16),
+            vm((4, ex, rpad, 640), BF16), vm((4, ex, 3, rpad, rpad), BF16), vm((4, ex, rpad, 256), BF16),
+            vm(act, F32), vm(act, F32), vm(act, F32), vm(act, BF16),
+            vm((2, width, CH), F32), vm((2, CH, width), F32), vm((width, 768), BF16),
+            vm((width, t), BF16), vm((width, t), BF16), vm((ex, rpad, 640), BF16), vm((ex, rpad, 256), BF16),
+            vm((7, 4, 2, band, CH), F32), vm((4, 4, 2, band, CH), F32), vm((9, 4, 2, band, CH), F32),
+            vm((9, 4, band, CH), F32), vm((9, 3, band, CH), F32),
+            vm((8, width), F32), vm((8, width), F32), vm((7, 8, width), F32),
+            dma((3,)), dma((2, 2)), dma((6,)), dma((6,)), dma((3,)), dma((3,)), dma((3,)), dma((3,)),
+            dma((3, 3)), dma((3, 3)), dma((3, 4)), dma((3, 4)),
+            dma((9,)), dma((9,)), dma((9,)), dma((9,)), dma((9, 3)), dma((9, 3)), dma((3,)), dma((3,)),
+            dma((7,)), dma((7,)),
+        ],
+        compiler_params=pltpu.CompilerParams(collective_id=0, has_side_effects=True, vmem_limit_bytes=VLIM),
+        name="layer",
+    )(split, tokens, cots, g1, s1, g2, s2, own)
+
+
+VLIM = 64 * 1024 * 1024 - 64 * 1024
+
+
+def fast_device(tokens, cotangent, split_point, w_qkv, w_out, w_up, w_down, gain_one, shift_one, gain_two, shift_two):
+    batch, length, width = tokens.shape
+    c = lax.rem(lax.axis_index("tensor"), 2)
+    d = lax.axis_index("dp")
+    band = width // 8
+    q, k, v, o = w_qkv[0], w_qkv[1], w_qkv[2], w_out.T
+    attn = jnp.concatenate(
+        [q[:, :128], k[:, :128], v[:, :128], q[:, 128:], v[:, 128:], k[:, 128:], o[:, 128:], o[:, :128]], axis=1
+    )
+    own = jnp.stack([attn, w_up, w_down]).astype(F32)
+    _, res, vecs, out, outs, gtok, gtoks = layer(
+        split_point, tokens, cotangent, gain_one, shift_one, gain_two, shift_two, own
+    )
+
+    def both(mine, other):
+        mine, other = mine[:, :length], other[:, :length]
+        first = jnp.where(c == 0, mine, other)
+        second = jnp.where(c == 0, other, mine)
+        return jnp.concatenate([first, second], axis=0).astype(BF16)
+
+    ra = jnp.concatenate([res[6], res[7], res[8]], axis=1)
+    gq = jnp.concatenate([ra[:, 0:128], ra[:, 384:448]], axis=1)
+    gk = jnp.concatenate([ra[:, 128:256], ra[:, 512:576]], axis=1)
+    gv = jnp.concatenate([ra[:, 256:384], ra[:, 448:512]], axis=1)
+    go = jnp.concatenate([ra[:, 640:768], ra[:, 576:640]], axis=1).T
+    ru = jnp.concatenate([res[1], res[3], res[5]], axis=1)
+    rd = jnp.concatenate([res[0], res[2], res[4]], axis=1).T
+    mine = lax.dynamic_slice_in_dim(vecs, d * band, band, 1)
+    return (
+        both(out, outs), both(gtok, gtoks), jnp.stack([gq, gk, gv]), go, ru, rd,
+        mine[0], mine[1], mine[2], mine[3],
+    )
 
 
 def layer_norm(values, gain_vec, shift_vec):
@@ -193,6 +774,7 @@
         P("dp"),
         P("dp"),
     )
+    fast = mesh.shape["dp"] == 8 and mesh.shape["tensor"] == 4
     return jax.shard_map(
-        per_device, mesh=mesh, in_specs=in_specs, out_specs=out_specs, check_vma=False
-    )
+        fast_device if fast else per_device, mesh=mesh, in_specs=in_specs, out_specs=out_specs, check_vma=False
+    )

time: 762 us -> 242 us (0.32); the launches traced: 754 us -> 241 us
  waiting for transfers between devices: 529 us -> 0 us
  Pallas kernels: 0 us -> 215 us
  matrix products: 75.3 us -> 0 us
  other arithmetic: 58.8 us -> 12.8 us
  blocking collectives: 37.2 us -> 0 us
  local copies, waits for them, and re-layouts: 36.4 us -> 13.3 us
  between operations: 15.8 us -> 0.77 us
    psum x3 -> x0, waiting for transfers between devices: 370 us -> none  [the longest x1 175 us: per_device(): output = (middle + lax.psum(branch, 'tensor')).astype(jnp.bfloat16)]
    pallas_call x0 -> x1, Pallas kernels: none -> 215 us  [layer(): pl.pallas_call(layer_kernel, out_shape=(sds((3, 3, width, 768), F32), sds...]
    reduce_scatter x2 -> x0, waiting for transfers between devices: 84.7 us -> none  [the longest x1 72.4 us: per_device(): lax.psum_scatter(grad_down_local, 'dp', scatter_dimension=1, tiled=True)]
    dot_general x18 -> x0, matrix products: 75.3 us -> none  [the longest x1 7.44 us: per_device(): jnp.einsum('btd,btf->df', normed_two, grad_pre, preferred_element_type=jn...]
    unnamed x9 -> x0, waiting for transfers between devices: 73.8 us -> none
    unnamed x1 -> x0, blocking collectives: 37.2 us -> none
    reduce_sum x9 -> x0, other arithmetic: 28 us -> none  [the longest x3 13.4 us: layer_norm(): return centered * lax.rsqrt(variance + EPSILON) * gain_vec + shift_vec]
    convert_element_type x5 -> x1, other arithmetic: 29.5 us -> 3.48 us  [fast_device(): own = jnp.stack([attn, w_up, w_down]).astype(F32)]
  transfers between devices with their start and end apart: 7 -> 0, of which waited for: 7 -> 0; matrix products, arithmetic and copies ran while one was open for 11% -> 0% of each run, Pallas kernels for 0% -> 0%
where the time goes in v2:
time: 242 us; the launch traced here: 241 us
  Pallas kernels  215 us (89%)
  local copies, waits for them, and re-layouts  13.3 us (5%)
  other arithmetic  12.8 us (5%)
    pallas_call x1, Pallas kernels, layer(): pl.pallas_call(layer_kernel, out_shape=(sds((3, 3, width, 768), F32), sds...  215 us

profile of v2, /device:TPU:0, one launch (start us, length us, event | category | flops | bytes accessed | tf_op | source)
XLA Modules:
  0.0 241.4 jit_solution(17449418972321781502)
XLA Ops:
  0.6 1.2 fusion
  1.9 0.2 copy.26
  2.0 0.7 slice.144
  2.7 0.2 copy.27
  2.9 0.7 slice.145
  3.8 0.7 slice.146
  4.5 0.7 slice.147
  5.1 0.7 slice.148
  5.8 0.7 slice.149
  6.5 0.2 copy.24
  6.7 0.7 slice.150
  7.4 0.7 slice.151
  8.1 2.4 concatenate.29
  10.5 3.5 %maximum_convert_fusion.own = f32[3,768,768]{2,1,0:T(8,128)} fusion(bf16[1,768,768]{2,1,0:T(8,128)(2,1)S(1)} %bitcast.52, bf16[1,768,768]{2,1,0:T(8,128)(2,1)S(1)} %bitcast.53, bf16[1,768,768]{2,1,0:T(8,128)(2,1)S(1)} %bitcast.43), kind=kLoop, calls=%fused_computation | loop fusion | flops 5308416 | bytes 10616832 | tf_op jit(solution)/shard_map/convert_element_type | solution.py:571
  14.0 214.6 %layer.1 = (f32[3,3,768,768]{3,2,1,0:T(8,128)}, f32[9,96,256]{2,1,0:T(8,128)}, f32[8,768]{1,0:T(8,128)}, f32[3,272,768]{2,1,0:T(8,128)}, f32[3,272,768]{2,1,0:T(...) custom-call(s32[6]{0:T(128)} %split.1, bf16[6,260,768]{2,1,0:T(8,128)(2,1)} %tokens.1, bf16[6,260,768]{2,1,0:T(8,128)(2,1)} %cots.1, ...), custom_call_target="tpu_custom_call" | custom-call | tf_op jit(solution)/shard_map/layer/pallas_call | solution.py:532
  228.5 1.3 slice_bitcast_fusion.2
  229.9 0.9 pad_maximum_fusion.3
  230.9 0.7 pad_maximum_fusion.2
  231.6 4.4 %select_convert_fusion.1 = (bf16[3,260,768]{2,1,0:T(8,128)(2,1)S(1)}, bf16[3,260,768]{2,1,0:T(8,128)(2,1)S(1)}, bf16[3,260,768]{2,1,0:T(8,128)(2,1)S(1)}, bf16[3,260,768]{2,1,0:T(8,128)(2,1)S(1)}) fusion(f32[3,272,768]{2,1,0:T(8,128)} %get-tuple-element.19, f32[3,272,768]{2,1,0:T(8,128)} %get-tuple-element.18, pred[]{:T(512)S(6)} %eq.2, ...), kind=kLoop, calls=%fused_computation.4 | loop fusion | flops 2396160 | bytes 9584641 | tf_op jit(solution)/shard_map/convert
  236.0 1.6 pad_maximum_fusion.1
  237.7 1.6 pad_maximum_fusion
  239.3 0.7 copy.25
  240.1 0.8 constant_dynamic-slice_fusion
  240.8 0.5 slice_bitcast_fusion.9
  (15 shorter events, 0.3 us)
Async XLA Ops:
  1.8 4.7 %copy-start.2 = (bf16[192,768]{1,0:T(8,128)(2,1)S(1)}, bf16[192,768]{1,0:T(8,128)(2,1)}, u32[]{:S(2)}) copy-start(bf16[192,768]{1,0:T(8,128)(2,1)} %param.15) | copy-start | bytes 884740
  5.1 5.3 %copy-start = (bf16[768,768]{1,0:T(8,128)(2,1)S(1)}, bf16[768,768]{1,0:T(8,128)(2,1)}, u32[]{:S(2)}) copy-start(bf16[768,768]{1,0:T(8,128)(2,1)} %param.17) | copy-start | bytes 3538948
  5.1 5.4 %copy-start.1 = (bf16[768,768]{1,0:T(8,128)(2,1)S(1)}, bf16[768,768]{1,0:T(8,128)(2,1)}, u32[]{:S(2)}) copy-start(bf16[768,768]{1,0:T(8,128)(2,1)} %param.16) | copy-start | bytes 3538948

commit v3 on v2

--- a/solution.py
+++ b/solution.py
@@ -51,35 +51,73 @@
 
 
 HEADS = ((0, 1, 2, False), (0, 1, 2, True), (3, 4, 3, False))
-SL = 512
+
+
+ZFIRST = (False, True, True, False, False, False, False, True, False)
+REUSE = (1, 2, 3)
+
+PLAN = {
+    ("start", 0): (("s", 0, 0, 0), ("c", 0, 0, 0)),
+    ("L", 2): (("g", 0, 0, 1), ("s", 1, 1, 0), ("s", 0, 1, 0), ("d", 0, 0, 0)),
+    ("F", 4): (("g", 0, 0, 2),),
+    ("F", 5): (("g", 0, 1, 1),),
+    ("F", 8): (("g", 0, 0, 3),),
+    ("j", 2): (("g", 0, 1, 2), ("g", 0, 1, 3), ("c", 1, 0, 0), ("g", 1, 1, 1), ("s", 2, 0, 0), ("s", 2, 1, 0),
+        ("g", 0, 0, 4), ("c", 2, 0, 0), ("g", 1, 1, 2), ("g", 0, 1, 4), ("g", 2, 1, 1), ("d", 2, 0, 0),
+        ("g", 1, 1, 3), ("w", 0, 0, 0)),
+    ("F", 12): (("g", 2, 1, 2), ("g", 2, 0, 1), ("s", 1, 0, 0)),
+    ("F", 15): (("g", 1, 1, 4),),
+    ("F", 16): (("g", 1, 0, 1),),
+    ("F", 17): (("g", 2, 1, 3),),
+    ("F", 18): (("g", 2, 0, 2), ("d", 1, 0, 0)),
+    ("fill", 1): (("g", 1, 0, 2),),
+    ("O", 0): (("g", 2, 0, 3),),
+    ("O", 1): (("g", 1, 0, 3), ("g", 2, 1, 4)),
+    ("O", 2): (("r", 0, 0, 1), ("r", 1, 0, 1)),
+    ("O", 4): (("r", 2, 0, 1), ("r", 3, 0, 1), ("g", 1, 0, 4), ("g", 2, 0, 4), ("w", 2, 0, 0)),
+    ("fill", 2): (("w", 1, 0, 0),),
+    ("P", 0): (("r", 4, 0, 1),),
+    ("P", 1): (("r", 1, 0, 2),),
+    ("P", 2): (("r", 0, 0, 2),),
+    ("P", 4): (("r", 2, 0, 2),),
+    ("P", 5): (("r", 1, 0, 3), ("r", 5, 0, 1)),
+    ("fill", 4): (("r", 3, 0, 2),),
+    ("B", 3): (("r", 1, 0, 4), ("r", 2, 0, 3), ("r", 0, 0, 3)),
+    ("B", 4): (("r", 4, 0, 2),),
+    ("B", 6): (("r", 2, 0, 4), ("r", 3, 0, 3), ("r", 0, 0, 4)),
+    ("B", 8): (("r", 5, 0, 2),),
+    ("B", 9): (("r", 3, 0, 4),),
+    ("b", 1): (("r", 6, 0, 1), ("r", 7, 0, 1), ("r", 5, 0, 3), ("r", 5, 0, 4), ("r", 8, 0, 1), ("r", 4, 0, 3)),
+    ("B", 14): (("r", 4, 0, 4), ("r", 6, 0, 2)),
+    ("B", 15): (("r", 7, 0, 2),),
+    ("B", 18): (("r", 8, 0, 2),),
+    ("fill", 6): (("r", 6, 0, 3), ("r", 8, 0, 3), ("r", 6, 0, 4), ("r", 7, 0, 3), ("r", 7, 0, 4), ("r", 8, 0, 4)),
+}
 
 
 def layer_kernel(
     split, tokens, cots, g1, s1, g2, s2, own,
-    wf, res, vecs, out, outs, gtok, gtoks,
-    tok, cotr, cotp, n1, qkv, prob, mx, mid, br, gn, n2, ust, dst, wbf, ta, tb, gp, gmix,
-    po, ps, cr, xr, zr, gv, vcr, vr,
-    isem, wsem, csend, crecv, ysend, yrecv, dsend, drecv, zsend, zrecv, xsend, xrecv,
-    rcs, rcr, rxs, rxr, rzs, rzr, osend, orecv, vsend, vrecv,
+    wf, vecs, gqkv, gout, gup, gdown, output, gtok, outs, gtoks,
+    tok, stage, cotp, n1, qkv, prob, mx, mid, br, gn, n2, ust, dst, wbf, ta, tb, gp, gmix,
+    po, ps, cr, ra, rb, rc, gv, vcr, vr,
+    isem, wsem, csend, crecv, ysend, yrecv, dsend, drecv, rcs, rcr, rsend, rrecv, osend, orecv, vsend, vrecv,
 ):
     ex, rows, width = tok.shape
     rpad = n1.shape[1]
     t = ex * rpad
     d, tt = lax.axis_index("dp"), lax.axis_index("tensor")
-    z, x = d // 2, lax.rem(d, 2)
+    zh, zl, x = d // 4, lax.rem(d // 2, 2), lax.rem(d, 2)
     y, c = tt // 2, lax.rem(tt, 2)
     sib = (d, y * 2 + 1 - c)
     ynb = (d, (1 - y) * 2 + c)
-    xnb = (z * 2 + 1 - x, tt)
+
+    def dpi(fh, fl, fx):
+        return ((1 - zh) if fh else zh) * 4 + ((1 - zl) if fl else zl) * 2 + ((1 - x) if fx else x)
+
+    znb2, znb1, xnb = (dpi(1, 0, 0), tt), (dpi(0, 1, 0), tt), (dpi(0, 0, 1), tt)
 
     def band(i):
         return pl.ds(pl.multiple_of(i * (width // 8), width // 8), width // 8)
-
-    def zof(k):
-        return lax.rem(z + k, 4)
-
-    def znb(k):
-        return (zof(k) * 2 + x, tt)
 
     peers = [sib, ynb] + [(lax.rem(d + k, 8), tt) for k in range(1, 8)]
     barrier = pltpu.get_barrier_semaphore()
@@ -87,11 +125,14 @@
         pl.semaphore_signal(barrier, 1, device_id=p, device_id_type=MESH)
     pl.semaphore_wait(barrier, len(peers))
 
-    def y_slice(p):
-        return rcopy(own.at[p, band(d), :SL], wf.at[1, p, band(d), :SL], ysend.at[p], yrecv.at[p], ynb)
+    def third(h):
+        return slice(h * CH, (h + 1) * CH)
+
+    def y_slice(p, h):
+        return rcopy(own.at[p, band(d), third(h)], wf.at[1, p, band(d), third(h)], ysend.at[p, h], yrecv.at[p, h], ynb)
 
     def y_direct(p):
-        return rcopy(own.at[p, :, SL:], wf.at[1, p, :, SL:], dsend.at[p], drecv.at[p], ynb)
+        return rcopy(own.at[p, :, third(2)], wf.at[1, p, :, third(2)], ysend.at[p, 2], yrecv.at[p, 2], ynb)
 
     def c_first(p):
         return rcopy(own.at[p], wf.at[0, p], csend.at[p], crecv.at[p], sib)
@@ -99,31 +140,37 @@
     def c_second(p):
         return rcopy(wf.at[1, p], wf.at[2, p], csend.at[3 + p], crecv.at[3 + p], sib)
 
-    def z_copy(p, k, slot, sem):
-        blk = wf.at[1, p, band(slot), :SL]
-        return rcopy(blk, blk, zsend.at[p, k - 1], zrecv.at[p, sem], znb(k))
-
-    def x_copy(p, k, slot):
-        blk = wf.at[1, p, band(slot), :SL]
-        return rcopy(blk, blk, xsend.at[p, k], xrecv.at[p, k], xnb)
-
-    def g1_step(p):
-        y_slice(p).wait_recv()
-        for k in (1, 2, 3):
-            z_copy(p, k, d, 3 - k).start()
-        x_copy(p, 0, d).start()
-
-    def g2_step(p):
-        for k in (1, 2, 3):
-            s = zof(k) * 2 + x
-            z_copy(p, k, s, k - 1).wait_recv()
-            x_copy(p, k, s).start()
-
-    def g3_step(p):
-        for k in (0, 1, 2, 3):
-            x_copy(p, k, zof(k) * 2 + 1 - x).wait_recv()
-        y_direct(p).wait_recv()
-        c_second(p).start()
+    hops = (
+        (dpi(0, 0, 0), dpi(1, 0, 0), znb2),
+        (dpi(0, 0, 0), dpi(0, 1, 0), znb1),
+        (dpi(1, 0, 0), dpi(1, 1, 0), znb1),
+        (dpi(0, 0, 0), dpi(0, 0, 1), xnb),
+        (dpi(1, 0, 0), dpi(1, 0, 1), xnb),
+        (dpi(0, 1, 0), dpi(0, 1, 1), xnb),
+        (dpi(1, 1, 0), dpi(1, 1, 1), xnb),
+    )
+
+    def hop(p, h, k, arriving=False):
+        blk = wf.at[1, p, band(hops[k][1] if arriving else hops[k][0]), third(h)]
+        return rcopy(blk, blk, dsend.at[2 * p + h, k], drecv.at[2 * p + h, k], hops[k][2])
+
+    def g_step(p, h, stage):
+        if stage == 1:
+            y_slice(p, h).wait_recv()
+            go = (0, 1, 3)
+        elif stage == 2:
+            hop(p, h, 0, True).wait_recv()
+            hop(p, h, 1, True).wait_recv()
+            go = (2, 4, 5)
+        elif stage == 3:
+            hop(p, h, 2, True).wait_recv()
+            go = (6,)
+        else:
+            for k in (3, 4, 5, 6):
+                hop(p, h, k, True).wait_recv()
+            go = ()
+        for k in go:
+            hop(p, h, k).start()
 
     def fetch(j, p, i, b):
         def src(ref):
@@ -148,98 +195,154 @@
 
     def load_attn(j):
         fetch(j, 0, 0, 0)
-        for i in range(3):
-            if i < 2:
-                fetch(j, 0, i + 1, (i + 1) % 2)
-            fetched(0, i % 2)
-            wbf[:, i * CH : (i + 1) * CH] = ust[i % 2].astype(BF16)
+        fetch(j, 0, 1, 1)
+
+    def take_attn(j):
+        fetched(0, 0)
+        wbf[j, :, :CH] = ust[0].astype(BF16)
+        fetch(j, 0, 2, 0)
+        fetched(0, 1)
+        wbf[j, :, CH : 2 * CH] = ust[1].astype(BF16)
+        fetched(0, 0)
+        wbf[j, :, 2 * CH :] = ust[0].astype(BF16)
 
     def c_grad(u, slot):
-        return rcopy(ps.at[slot], cr.at[u], rcs.at[u], rcr.at[u], sib)
-
-    def x_grad(u, pu, side):
-        return rcopy(po.at[pu, :, side], xr.at[u], rxs.at[u], rxr.at[u], xnb)
-
-    def z_grad(u, pu, k, slot):
-        return rcopy(po.at[pu, zof(k), x], zr.at[u, slot], rzs.at[u, k - 1], rzr.at[u, slot], znb(k))
-
-    def r1_step(u, pu):
-        c_grad(u, 0).wait_recv()
-        po[pu, :, 1 - x] += cr[u, :, 1 - x]
-        x_grad(u, pu, 1 - x).start()
-        po[pu, :, x] += cr[u, :, x]
-
-    def r2_step(u, pu):
-        x_grad(u, pu, x).wait_recv()
-        po[pu, :, x] += xr[u]
-        for k in (1, 2, 3):
-            z_grad(u, pu, k, 3 - k).start()
-
-    def r3_step(u, pu):
-        for k in (1, 2, 3):
-            z_grad(u, pu, k, k - 1).wait_recv()
-        res[u] = po[pu, z, x] + zr[u, 0] + zr[u, 1] + zr[u, 2]
-
-    for p in range(3):
-        y_slice(p).start()
-    c_first(0).start()
-    y_direct(0).start()
+        return rcopy(ps.at[slot], cr.at[u % 6], rcs.at[u], rcr.at[u], sib)
+
+    def views(pu, zfirst):
+        if zfirst:
+            return (
+                ((pu, slice(None), 1 - zl), (pu, slice(None), zl), znb1),
+                ((pu, 1 - zh, zl), (pu, zh, zl), znb2),
+                ((pu, zh, zl, 1 - x), (pu, zh, zl, x), xnb),
+            )
+        return (
+            ((pu, slice(None), slice(None), 1 - x), (pu, slice(None), slice(None), x), xnb),
+            ((pu, slice(None), 1 - zl, x), (pu, slice(None), zl, x), znb1),
+            ((pu, 1 - zh, zl, x), (pu, zh, zl, x), znb2),
+        )
+
+    def halving(u, pu, k, zfirst):
+        src = po.at[views(pu, zfirst)[k][0]]
+        return rcopy(src, (ra, rb, rc)[k].at[u], rsend.at[u, k], rrecv.at[u, k], views(pu, zfirst)[k][2])
+
+    def r_step(u, pu, stage, zfirst):
+        view = views(pu, zfirst)
+        if stage == 1:
+            c_grad(u, 0).wait_recv()
+            away = view[0][0][1:]
+            po[(pu,) + away] += cr[(u % 6,) + away]
+            halving(u, pu, 0, zfirst).start()
+            keep = view[0][1][1:]
+            po[(pu,) + keep] += cr[(u % 6,) + keep]
+        elif stage < 4:
+            k = stage - 2
+            halving(u, pu, k, zfirst).wait_recv()
+            po[view[k][1]] += (ra, rb)[k][u]
+            halving(u, pu, k + 1, zfirst).start()
+        else:
+            halving(u, pu, 2, zfirst).wait_recv()
+            hand_out(u, po[view[2][1]] + rc[u])
+
+    def hand_out(u, g):
+        if u < 6:
+            cols = slice(u // 2 * CH, (u // 2 + 1) * CH)
+            if u % 2:
+                gup[:, cols] = g
+            else:
+                gdown[:, cols] = g
+        elif u == 6:
+            gqkv[0, :, :128] = g[:, :128]
+            gqkv[1, :, :128] = g[:, 128:]
+        elif u == 7:
+            gqkv[2, :, :128] = g[:, :128]
+            gqkv[0, :, 128:] = g[:, 128 : 128 + HD]
+            gqkv[2, :, 128:] = g[:, 128 + HD :]
+        else:
+            gqkv[1, :, 128:] = g[:, :HD]
+            turned = g.T
+            gout[128:, :] = turned[HD:128]
+            gout[:128, :] = turned[128:]
+
+    def r_sent(u, pu, zfirst):
+        for k in range(3):
+            halving(u, pu, k, zfirst).wait_send()
+
+    def place_of(u):
+        return u if u < 6 else REUSE[u - 6]
+
+    def run(steps):
+        for what, a, b, stage in steps:
+            if what == "g":
+                g_step(a, b, stage)
+            elif what == "s":
+                y_slice(a, b).start()
+            elif what == "d":
+                y_direct(a).start()
+            elif what == "c":
+                c_first(a).start()
+            elif what == "w":
+                y_direct(a).wait_recv()
+                c_second(a).start()
+            else:
+                r_step(a, place_of(a), stage, ZFIRST[a])
+
+    def tick(at, where):
+        for (name, when), steps in PLAN.items():
+            if name == where:
+                @pl.when(at == when)
+                def _(steps=steps):
+                    run(steps)
+
+    def fill(where, at):
+        run(PLAN.get((where, at), ()))
+
+    fill("start", 0)
+    load_attn(0)
+    cin = pltpu.make_async_copy(cots.at[pl.ds(c * ex, ex)], tok, isem.at[1])
+    cin.start()
+    cotp[...] = jnp.zeros_like(cotp)
+    cin.wait()
+
+    @pl.loop(0, ex)
+    def _(e):
+        cotp[e, :rows, :] = tok[e]
+
     tin = pltpu.make_async_copy(tokens.at[pl.ds(c * ex, ex)], tok, isem.at[0])
     tin.start()
+    ta[...] = cotp[...].reshape(t, width).T
     tin.wait()
     n1[...] = jnp.zeros_like(n1)
     mid[...] = jnp.zeros_like(mid)
-    cotp[...] = jnp.zeros_like(cotp)
     gv[...] = jnp.zeros_like(gv)
 
     @pl.loop(0, ex)
     def _(e):
+        tick(e, "L")
         v = tok[e].astype(F32)
         xhat, _ = ln_stats(v)
         n1[e, :rows, :] = (xhat * g1[...][None] + s1[...][None]).astype(BF16)
         mid[e, :rows, :] = v
 
-    c_first(1).start()
-    c_first(2).start()
-
     low_half = lax.broadcasted_iota(jnp.int32, (rpad, 128), 1) < HD
     qi = lax.broadcasted_iota(jnp.int32, (rpad, rpad), 0)
     kj = lax.broadcasted_iota(jnp.int32, (rpad, rpad), 1)
 
     @pl.loop(0, 4)
     def _(j):
-        @pl.when(j == 1)
-        def _():
-            g1_step(0)
+        take_attn(j)
+
+        @pl.when(j == 0)
+        def _():
             c_first(0).wait_recv()
-
-        @pl.when(j == 2)
-        def _():
-            ccopy = pltpu.make_async_copy(cots.at[pl.ds(c * ex, ex)], cotr, isem.at[1])
-            ccopy.start()
-            ccopy.wait()
-
-            @pl.loop(0, ex)
-            def _(e):
-                cotp[e, :rows, :] = cotr[e]
-
-            ta[...] = cotp[...].reshape(t, width).T
-            g2_step(0)
-            y_direct(1).start()
-            y_direct(2).start()
-            g3_step(0)
-            g1_step(1)
-
-        @pl.when(j == 3)
-        def _():
-            g1_step(2)
-            c_second(0).wait_recv()
-
-        load_attn(j)
-        qkv[j] = mm(n1[...].reshape(t, width), wbf[:, :640]).astype(BF16).reshape(ex, rpad, 640)
+            load_attn(1)
+
+        tick(j * 5, "F")
+        qkv[j] = mm(n1[...].reshape(t, width), wbf[j, :, :640]).astype(BF16).reshape(ex, rpad, 640)
 
         @pl.loop(0, ex)
         def _(e):
+            tick(j * 5 + 1 + e, "F")
             allowed = kj <= jnp.maximum(qi, PATCHES - 1 + split[c * ex + e])
             outs_h = []
             for h, (gq, gk, gvv, high) in enumerate(HEADS):
@@ -257,9 +360,18 @@
             mx[j, e, :, :128] = jnp.where(low_half, zero, outs_h[2]).astype(BF16)
             mx[j, e, :, 128:] = jnp.where(low_half, outs_h[0], outs_h[1]).astype(BF16)
 
-        mid[...] += mm_nt(mx[j].reshape(t, 256), wbf[:, 512:]).reshape(ex, rpad, width)
-
-    g2_step(1)
+        tick(j * 5 + 4, "F")
+        mid[...] += mm_nt(mx[j].reshape(t, 256), wbf[j, :, 512:]).reshape(ex, rpad, width)
+
+        @pl.when(j == 1)
+        def _():
+            fill("j", 2)
+            load_attn(2)
+
+        @pl.when(j == 2)
+        def _():
+            c_second(0).wait_recv()
+            load_attn(3)
 
     @pl.loop(0, ex)
     def _(e):
@@ -293,6 +405,7 @@
         fetched(1, b)
         fetched(2, b)
 
+    fill("fill", 1)
     c_first(1).wait_recv()
     c_first(2).wait_recv()
     fetch2(1, 0, 0)
@@ -328,18 +441,10 @@
         def _():
             po[2 * i] = gd
             po[2 * i + 1] = gu
-            r1_step(2 * i, 2 * i)
-            r1_step(2 * i + 1, 2 * i + 1)
-
-        @pl.when(n == 1)
-        def _():
-            g2_step(2)
-
-        @pl.when(n == 3)
-        def _():
-            g3_step(1)
-
-    g3_step(2)
+
+        tick(n, "O")
+
+    fill("fill", 2)
     fetch2(2, 0, 0)
 
     @pl.loop(0, 6)
@@ -357,13 +462,11 @@
 
         fetched2(b)
         chunk(b)
+        tick(n, "P")
 
     o_copy = rcopy(br, outs, osend.at[0], orecv.at[0], sib)
     o_copy.start()
-    o_keep = pltpu.make_async_copy(br, out, isem.at[2])
-    o_keep.start()
-    r2_step(0, 0)
-    r2_step(1, 1)
+    fill("fill", 3)
 
     @pl.loop(0, ex)
     def _(e):
@@ -373,21 +476,30 @@
         gm = cotp[e].astype(F32) + back
         mid[e] = gm
         n2[e] = gm.astype(BF16)
+        stage[e] = br[e, :rows, :].astype(BF16)
         gn[e] = jnp.zeros((rpad, width), F32)
 
+    fill("fill", 4)
     gml = n2
     ta[...] = gml[...].reshape(t, width).T
     tb[...] = n1[...].reshape(t, width).T
     scale = HD ** -0.5
 
+    mine, theirs = pl.ds(c * ex, ex), pl.ds((1 - c) * ex, ex)
+    o_keep = pltpu.make_async_copy(stage, output.at[mine], isem.at[2])
+    o_keep.start()
+    o_back = pltpu.make_async_copy(outs, br, isem.at[0])
+    o_other = pltpu.make_async_copy(stage, output.at[theirs], isem.at[1])
+
     @pl.loop(0, 4)
     def _(n):
         j = jnp.where(n < 2, 1 - n, n)
-        load_attn(j)
-        gmix[...] = mm(gml[...].reshape(t, width), wbf[:, 512:]).astype(BF16).reshape(ex, rpad, 256)
+        tick(n * 5, "B")
+        gmix[...] = mm(gml[...].reshape(t, width), wbf[j, :, 512:]).astype(BF16).reshape(ex, rpad, 256)
 
         @pl.loop(0, ex)
         def _(e):
+            tick(n * 5 + 1 + e, "B")
             dq, dk, dv = [], [], []
             for h, (gq, gk, gvv, high) in enumerate(HEADS):
                 gx = gmix[e, :, :128] if h == 2 else gmix[e, :, 128:]
@@ -407,8 +519,9 @@
             gp[e, :, 384:512] = jnp.where(low_half, dq[2], dv[2]).astype(BF16)
             gp[e, :, 512:640] = jnp.where(low_half, dk[2], zero).astype(BF16)
 
+        tick(n * 5 + 4, "B")
         gpf = gp[...].reshape(t, 640)
-        gn[...] += mm_nt(gpf, wbf[:, :640]).reshape(ex, rpad, width)
+        gn[...] += mm_nt(gpf, wbf[j, :, :640]).reshape(ex, rpad, width)
 
         def grads(write):
             write(0, mm(tb[...], gpf[:, :256]).reshape(shape5))
@@ -430,48 +543,49 @@
 
         @pl.when(n == 1)
         def _():
-            r3_step(0, 0)
-            r3_step(1, 1)
-            r2_step(2, 2)
-            r2_step(3, 3)
-            for u in range(2):
-                x_grad(u, u, 1 - x).wait_send()
-                for k in (1, 2, 3):
-                    z_grad(u, u, k, 3 - k).wait_send()
+            fill("b", 0)
+            for u in REUSE:
+                r_sent(u, u, ZFIRST[u])
 
             def write(i, g):
-                pu = (0, 1, 6)[i]
-                po[pu] = g
-                r1_step(6 + i, pu)
+                po[REUSE[i]] = g
 
             grads(write)
+            fill("b", 1)
+            o_copy.wait()
+            o_back.start()
 
         @pl.when(n == 2)
         def _():
-            r3_step(2, 2)
-            r3_step(3, 3)
-            r2_step(4, 4)
-            r2_step(5, 5)
-
-    r2_step(6, 0)
-
-    o_copy.wait_send()
-    o_keep.wait()
+            o_back.wait()
+            o_keep.wait()
+
+            @pl.loop(0, ex)
+            def _(e):
+                stage[e] = br[e, :rows, :].astype(BF16)
+
+            o_other.start()
+
+    fill("fill", 5)
+
+    o_other.wait()
 
     @pl.loop(0, ex)
     def _(e):
         back, dg, ds = ln_back(tok[e].astype(F32), gn[e, :rows, :], g1[...][None])
         gv[0:1, :] += dg
         gv[1:2, :] += ds
-        br[e, :rows, :] = mid[e, :rows, :] + back
+        g = mid[e, :rows, :] + back
+        br[e, :rows, :] = g
+        tok[e] = g.astype(BF16)
 
     t_copy = rcopy(br, gtoks, osend.at[1], orecv.at[1], sib)
     t_copy.start()
-    t_keep = pltpu.make_async_copy(br, gtok, isem.at[2])
+    t_keep = pltpu.make_async_copy(tok, gtok.at[mine], isem.at[2])
     t_keep.start()
+    t_back = pltpu.make_async_copy(gtoks, gn, isem.at[0])
     v_copy = rcopy(gv, vcr, osend.at[2], orecv.at[2], sib)
     v_copy.start()
-    r2_step(7, 1)
     v_copy.wait()
     gv[...] += vcr[...]
     v_sends = []
@@ -479,9 +593,9 @@
         cp = rcopy(gv, vr.at[7 - k], vsend.at[k - 1], vrecv.at[7 - k], (lax.rem(d + k, 8), tt))
         cp.start()
         v_sends.append(cp)
-    r2_step(8, 6)
-    for u in range(4, 9):
-        r3_step(u, (0, 1, 2, 3, 4, 5, 0, 1, 6)[u])
+    t_copy.wait()
+    t_back.start()
+    fill("fill", 6)
     for k in range(1, 8):
         rcopy(gv, vr.at[k - 1], vsend.at[k - 1], vrecv.at[k - 1], sib).wait_recv()
     acc = None
@@ -491,29 +605,31 @@
         acc = term if acc is None else acc + term
     vecs[...] = acc
 
-    c_second(1).wait_send()
-    o_copy.wait_recv()
-    t_copy.wait()
+    t_back.wait()
     t_keep.wait()
+
+    @pl.loop(0, ex)
+    def _(e):
+        tok[e] = gn[e, :rows, :].astype(BF16)
+
+    t_other = pltpu.make_async_copy(tok, gtok.at[theirs], isem.at[1])
+    t_other.start()
     for cp in v_sends:
         cp.wait_send()
     for p in range(3):
-        y_slice(p).wait_send()
         y_direct(p).wait_send()
         c_first(p).wait_send()
-        for k in (1, 2, 3):
-            z_copy(p, k, d, 3 - k).wait_send()
-        for k in (0, 1, 2, 3):
-            x_copy(p, k, d).wait_send()
-    c_second(0).wait_send()
-    c_second(2).wait_send()
-    for u in range(2, 9):
-        pu = (0, 1, 2, 3, 4, 5, 0, 1, 6)[u]
-        x_grad(u, pu, 1 - x).wait_send()
-        for k in (1, 2, 3):
-            z_grad(u, pu, k, 3 - k).wait_send()
+        c_second(p).wait_send()
+        for h in range(2):
+            y_slice(p, h).wait_send()
+            for k in range(7):
+                hop(p, h, k).wait_send()
+    for u in range(9):
+        if u not in REUSE:
+            r_sent(u, place_of(u), ZFIRST[u])
     for u in range(6, 9):
         c_grad(u, u - 6).wait_send()
+    t_other.wait()
 
 
 def layer(split, tokens, cots, g1, s1, g2, s2, own):
@@ -532,24 +648,23 @@
     return pl.pallas_call(
         layer_kernel,
         out_shape=(
-            sds((3, 3, width, 768), F32), sds((9, band, CH), F32), sds((8, width), F32),
-            sds(act, F32), sds(act, F32), sds(act, F32), sds(act, F32),
+            sds((3, 3, width, 768), F32), sds((8, width), F32),
+            sds((3, band, 192), F32), sds((192, band), F32), sds((band, 768), F32), sds((band, 768), F32),
+            sds(tokens.shape, BF16), sds(tokens.shape, BF16), sds(act, F32), sds(act, F32),
         ),
         in_specs=[SM, ANY, ANY, VM, VM, VM, VM, ANY],
-        out_specs=(ANY, VM, VM, ANY, ANY, ANY, ANY),
+        out_specs=(ANY, VM, VM, VM, VM, VM, ANY, ANY, ANY, ANY),
         scratch_shapes=[
             vm((ex, rows, width), BF16), vm((ex, rows, width), BF16), vm(act, BF16), vm(act, BF16),
             vm((4, ex, rpad, 640), BF16), vm((4, ex, 3, rpad, rpad), BF16), vm((4, ex, rpad, 256), BF16),
             vm(act, F32), vm(act, F32), vm(act, F32), vm(act, BF16),
-            vm((2, width, CH), F32), vm((2, CH, width), F32), vm((width, 768), BF16),
+            vm((2, width, CH), F32), vm((2, CH, width), F32), vm((4, width, 768), BF16),
             vm((width, t), BF16), vm((width, t), BF16), vm((ex, rpad, 640), BF16), vm((ex, rpad, 256), BF16),
-            vm((7, 4, 2, band, CH), F32), vm((4, 4, 2, band, CH), F32), vm((9, 4, 2, band, CH), F32),
-            vm((9, 4, band, CH), F32), vm((9, 3, band, CH), F32),
+            vm((6, 2, 2, 2, band, CH), F32), vm((4, 2, 2, 2, band, CH), F32), vm((6, 2, 2, 2, band, CH), F32),
+            vm((9, 2, 2, band, CH), F32), vm((9, 2, band, CH), F32), vm((9, band, CH), F32),
             vm((8, width), F32), vm((8, width), F32), vm((7, 8, width), F32),
-            dma((3,)), dma((2, 2)), dma((6,)), dma((6,)), dma((3,)), dma((3,)), dma((3,)), dma((3,)),
-            dma((3, 3)), dma((3, 3)), dma((3, 4)), dma((3, 4)),
-            dma((9,)), dma((9,)), dma((9,)), dma((9,)), dma((9, 3)), dma((9, 3)), dma((3,)), dma((3,)),
-            dma((7,)), dma((7,)),
+            dma((3,)), dma((2, 2)), dma((6,)), dma((6,)), dma((3, 3)), dma((3, 3)), dma((6, 7)), dma((6, 7)),
+            dma((9,)), dma((9,)), dma((9, 3)), dma((9, 3)), dma((3,)), dma((3,)), dma((7,)), dma((7,)),
         ],
         compiler_params=pltpu.CompilerParams(collective_id=0, has_side_effects=True, vmem_limit_bytes=VLIM),
         name="layer",
@@ -559,38 +674,51 @@
 VLIM = 64 * 1024 * 1024 - 64 * 1024
 
 
+def prepare_kernel(w_qkv, w_out, w_up, w_down, own):
+    part = pl.program_id(0)
+
+    @pl.when(part == 0)
+    def _():
+        q, k, v = (w_qkv[i].astype(F32).T for i in range(3))
+        o = w_out[...].astype(F32).T
+        for i, g in enumerate((
+            q[:, :128], k[:, :128], v[:, :128], jnp.concatenate([q[:, 128:], v[:, 128:]], axis=1),
+            jnp.concatenate([k[:, 128:], o[:, 128:]], axis=1), o[:, :128],
+        )):
+            own[0, :, i * 128 : (i + 1) * 128] = g
+
+    @pl.when(part == 1)
+    def _():
+        own[0] = w_up[...].astype(F32)
+
+    @pl.when(part == 2)
+    def _():
+        own[0] = w_down[...].astype(F32)
+
+
+def prepare(w_qkv, w_out, w_up, w_down):
+    width = w_up.shape[0]
+    whole = lambda w: pl.BlockSpec(w.shape, lambda i: (0,) * w.ndim)
+    return pl.pallas_call(
+        prepare_kernel,
+        grid=(3,),
+        out_shape=jax.ShapeDtypeStruct((3, width, 768), F32),
+        in_specs=[whole(w) for w in (w_qkv, w_out, w_up, w_down)],
+        out_specs=pl.BlockSpec((1, width, 768), lambda i: (i, 0, 0)),
+        name="prepare",
+    )(w_qkv, w_out, w_up, w_down)
+
+
 def fast_device(tokens, cotangent, split_point, w_qkv, w_out, w_up, w_down, gain_one, shift_one, gain_two, shift_two):
     batch, length, width = tokens.shape
-    c = lax.rem(lax.axis_index("tensor"), 2)
     d = lax.axis_index("dp")
     band = width // 8
-    q, k, v, o = w_qkv[0], w_qkv[1], w_qkv[2], w_out.T
-    attn = jnp.concatenate(
-        [q[:, :128], k[:, :128], v[:, :128], q[:, 128:], v[:, 128:], k[:, 128:], o[:, 128:], o[:, :128]], axis=1
-    )
-    own = jnp.stack([attn, w_up, w_down]).astype(F32)
-    _, res, vecs, out, outs, gtok, gtoks = layer(
+    own = prepare(w_qkv.transpose(0, 2, 1), w_out, w_up, w_down)
+    _, vecs, gqkv, gout, gup, gdown, output, gtok, _, _ = layer(
         split_point, tokens, cotangent, gain_one, shift_one, gain_two, shift_two, own
     )
-
-    def both(mine, other):
-        mine, other = mine[:, :length], other[:, :length]
-        first = jnp.where(c == 0, mine, other)
-        second = jnp.where(c == 0, other, mine)
-        return jnp.concatenate([first, second], axis=0).astype(BF16)
-
-    ra = jnp.concatenate([res[6], res[7], res[8]], axis=1)
-    gq = jnp.concatenate([ra[:, 0:128], ra[:, 384:448]], axis=1)
-    gk = jnp.concatenate([ra[:, 128:256], ra[:, 512:576]], axis=1)
-    gv = jnp.concatenate([ra[:, 256:384], ra[:, 448:512]], axis=1)
-    go = jnp.concatenate([ra[:, 640:768], ra[:, 576:640]], axis=1).T
-    ru = jnp.concatenate([res[1], res[3], res[5]], axis=1)
-    rd = jnp.concatenate([res[0], res[2], res[4]], axis=1).T
     mine = lax.dynamic_slice_in_dim(vecs, d * band, band, 1)
-    return (
-        both(out, outs), both(gtok, gtoks), jnp.stack([gq, gk, gv]), go, ru, rd,
-        mine[0], mine[1], mine[2], mine[3],
-    )
+    return output, gtok, gqkv, gout, gup, gdown.T, mine[0], mine[1], mine[2], mine[3]
 
 
 def layer_norm(values, gain_vec, shift_vec):

time: 242 us -> 188 us (0.78)
  Pallas kernels: 215 us -> 178 us
  other arithmetic: 12.8 us -> 0 us
  local copies, waits for them, and re-layouts: 13.3 us -> 8.96 us
    pallas_call x1, Pallas kernels: 215 us -> 172 us  [layer(): pl.pallas_call(layer_kernel, out_shape=(sds((3, 3, width, 768), F32), sds...]
    slice x13 -> x0, local copies, waits for them, and re-layouts: 6.82 us -> none  [the longest x1 1.2 us: fast_device(): q, k, v, o = (w_qkv[0], w_qkv[1], w_qkv[2], w_out.T)]
    unnamed x11 -> x16, local copies, waits for them, and re-layouts: 1.43 us -> 7.65 us
    pallas_call x0 -> x1, Pallas kernels: none -> 5.65 us  [prepare(): pl.pallas_call(prepare_kernel, grid=(3,), out_shape=jax.ShapeDtypeStruct(...]
    another operation x5 -> x0, other arithmetic: 5.14 us -> none
    concatenate x3 -> x0, other arithmetic: 4.15 us -> none  [the longest x2 3.3 us: both(): return jnp.concatenate([first, second], axis=0).astype(BF16)]
    convert_element_type x1 -> x0, other arithmetic: 3.48 us -> none  [fast_device(): own = jnp.stack([attn, w_up, w_down]).astype(F32)]
where the time goes in v3:
time: 188 us; the launch traced here: 187 us
  Pallas kernels  178 us (95%)
  local copies, waits for them, and re-layouts  8.96 us (5%)
    pallas_call x1, Pallas kernels, layer(): pl.pallas_call(layer_kernel, out_shape=(sds((3, 3, width, 768), F32), sds...  172 us
    unnamed x16, local copies, waits for them, and re-layouts  7.65 us
    pallas_call x1, Pallas kernels, prepare(): pl.pallas_call(prepare_kernel, grid=(3,), out_shape=jax.ShapeDtypeStruct(...  5.65 us

profile of v3, /device:TPU:0, one launch (start us, length us, event | category | flops | bytes accessed | tf_op | source)
XLA Modules:
  0.0 187.4 jit_solution(4765489527111421145)
XLA Ops:
  0.6 5.6 %prepare.1.own = f32[3,768,768]{2,1,0:T(8,128)} custom-call(bf16[3,192,768]{2,1,0:T(8,128)(2,1)} %bitcast.10, bf16[192,768]{1,0:T(8,128)(2,1)} %w_out.1, bf16[768,768]{1,0:T(8,128)(2,1)} %w_up.1, bf16[768,768]{1,0:T(8,128)(2,1)} %w_down.1), custom_call_target="tpu_custom_call" | custom-call | tf_op jit(solution)/shard_map/prepare/pallas_call | solution.py:702
  6.3 172.1 %layer.1 = (f32[3,3,768,768]{3,2,1,0:T(8,128)}, f32[8,768]{1,0:T(8,128)}, f32[3,96,192]{2,1,0:T(8,128)}, f32[192,96]{1,0:T(8,128)}, f32[96,768]{1,0:T(8,128)}, /...) custom-call(s32[6]{0:T(128)} %split.1, ...), custom_call_target="tpu_custom_call" | custom-call | tf_op jit(solution)/shard_map/layer/pallas_call | solution.py:648
  178.4 0.8 constant_dynamic-slice_fusion
  179.2 0.5 slice_bitcast_fusion
  179.7 0.0 copy-start
  179.7 3.4 %copy.27 = bf16[6,260,768]{2,1,0:T(8,128)(2,1)} copy(bf16[6,260,768]{2,1,0:T(8,128)(2,1)} %get-tuple-element.38) | data formatting | bytes 4792320
  183.1 0.0 copy-done
  183.1 0.0 copy-start.3
  183.1 0.0 copy-start.4
  183.1 0.0 copy-start.2
  183.1 0.0 copy-start.1
  183.1 1.4 copy.28
  184.6 0.0 copy-done.3
  184.6 0.7 copy.29
  185.3 0.0 copy-done.4
  185.3 0.6 copy.30
  185.9 0.0 copy-done.2
  185.9 0.7 copy.31
  186.6 0.0 copy-done.1
  186.6 0.7 copy.32
Async XLA Ops:
  179.7 3.4 %copy-start = (bf16[6,260,768]{2,1,0:T(8,128)(2,1)S(1)}, bf16[6,260,768]{2,1,0:T(8,128)(2,1)}, u32[]{:S(2)}) copy-start(bf16[6,260,768]{2,1,0:T(8,128)(2,1)} %get-tuple-element.39) | copy-start | bytes 7188484
  183.1 1.5 copy-start.3
  183.1 2.2 %copy-start.4 = (f32[192,96]{1,0:T(8,128)S(1)}, f32[192,96]{1,0:T(8,128)}, u32[]{:S(2)}) copy-start(f32[192,96]{1,0:T(8,128)} %get-tuple-element.41) | copy-start | bytes 221188
  183.1 2.8 %copy-start.2 = (f32[96,768]{1,0:T(8,128)S(1)}, f32[96,768]{1,0:T(8,128)}, u32[]{:S(2)}) copy-start(f32[96,768]{1,0:T(8,128)} %get-tuple-element.42) | copy-start | bytes 884740
  183.1 3.5 %copy-start.1 = (f32[96,768]{1,0:T(8,128)S(1)}, f32[96,768]{1,0:T(8,128)}, u32[]{:S(2)}) copy-start(f32[96,768]{1,0:T(8,128)} %get-tuple-element.22) | copy-start | bytes 884740

commit v4 on v3

--- a/solution.py
+++ b/solution.py
@@ -50,57 +50,56 @@
     )
 
 
-HEADS = ((0, 1, 2, False), (0, 1, 2, True), (3, 4, 3, False))
-
-
-ZFIRST = (False, True, True, False, False, False, False, True, False)
-REUSE = (1, 2, 3)
+ZFIRST = (False, True, False, True, False, False, True, False, False)
 
 PLAN = {
-    ("start", 0): (("s", 0, 0, 0), ("c", 0, 0, 0)),
-    ("L", 2): (("g", 0, 0, 1), ("s", 1, 1, 0), ("s", 0, 1, 0), ("d", 0, 0, 0)),
-    ("F", 4): (("g", 0, 0, 2),),
-    ("F", 5): (("g", 0, 1, 1),),
-    ("F", 8): (("g", 0, 0, 3),),
-    ("j", 2): (("g", 0, 1, 2), ("g", 0, 1, 3), ("c", 1, 0, 0), ("g", 1, 1, 1), ("s", 2, 0, 0), ("s", 2, 1, 0),
-        ("g", 0, 0, 4), ("c", 2, 0, 0), ("g", 1, 1, 2), ("g", 0, 1, 4), ("g", 2, 1, 1), ("d", 2, 0, 0),
-        ("g", 1, 1, 3), ("w", 0, 0, 0)),
-    ("F", 12): (("g", 2, 1, 2), ("g", 2, 0, 1), ("s", 1, 0, 0)),
-    ("F", 15): (("g", 1, 1, 4),),
-    ("F", 16): (("g", 1, 0, 1),),
-    ("F", 17): (("g", 2, 1, 3),),
-    ("F", 18): (("g", 2, 0, 2), ("d", 1, 0, 0)),
+    ("start", 0): (("c", 0, 0, 0), ("s", 0, 1, 0)),
+    ("L", 0): (("s", 0, 0, 0),),
+    ("L", 2): (("g", 0, 1, 1),),
+    ("own", 0): (("c", 1, 0, 0), ("c", 2, 0, 0), ("s", 2, 0, 0)),
+    ("F", 1): (("g", 0, 0, 1),),
+    ("F", 2): (("d", 0, 0, 0),),
+    ("F", 3): (("g", 2, 0, 1),),
+    ("j", 1): (("g", 0, 1, 2),),
+    ("j", 2): (("g", 0, 0, 2), ("g", 2, 0, 2), ("g", 0, 1, 3), ("s", 1, 1, 0), ("g", 0, 0, 3), ("s", 2, 1, 0),
+        ("g", 2, 0, 3), ("s", 1, 0, 0), ("g", 1, 1, 1), ("d", 1, 0, 0), ("g", 0, 1, 4), ("g", 2, 1, 1),
+        ("g", 0, 0, 4), ("w", 0, 0, 0)),
+    ("F", 7): (("g", 1, 0, 1),),
+    ("F", 8): (("g", 2, 0, 4),),
+    ("F", 9): (("g", 1, 1, 2),),
+    ("F", 11): (("g", 2, 1, 2),),
     ("fill", 1): (("g", 1, 0, 2),),
-    ("O", 0): (("g", 2, 0, 3),),
-    ("O", 1): (("g", 1, 0, 3), ("g", 2, 1, 4)),
-    ("O", 2): (("r", 0, 0, 1), ("r", 1, 0, 1)),
-    ("O", 4): (("r", 2, 0, 1), ("r", 3, 0, 1), ("g", 1, 0, 4), ("g", 2, 0, 4), ("w", 2, 0, 0)),
-    ("fill", 2): (("w", 1, 0, 0),),
-    ("P", 0): (("r", 4, 0, 1),),
-    ("P", 1): (("r", 1, 0, 2),),
-    ("P", 2): (("r", 0, 0, 2),),
-    ("P", 4): (("r", 2, 0, 2),),
-    ("P", 5): (("r", 1, 0, 3), ("r", 5, 0, 1)),
-    ("fill", 4): (("r", 3, 0, 2),),
-    ("B", 3): (("r", 1, 0, 4), ("r", 2, 0, 3), ("r", 0, 0, 3)),
-    ("B", 4): (("r", 4, 0, 2),),
-    ("B", 6): (("r", 2, 0, 4), ("r", 3, 0, 3), ("r", 0, 0, 4)),
-    ("B", 8): (("r", 5, 0, 2),),
-    ("B", 9): (("r", 3, 0, 4),),
-    ("b", 1): (("r", 6, 0, 1), ("r", 7, 0, 1), ("r", 5, 0, 3), ("r", 5, 0, 4), ("r", 8, 0, 1), ("r", 4, 0, 3)),
-    ("B", 14): (("r", 4, 0, 4), ("r", 6, 0, 2)),
-    ("B", 15): (("r", 7, 0, 2),),
-    ("B", 18): (("r", 8, 0, 2),),
-    ("fill", 6): (("r", 6, 0, 3), ("r", 8, 0, 3), ("r", 6, 0, 4), ("r", 7, 0, 3), ("r", 7, 0, 4), ("r", 8, 0, 4)),
+    ("O", 0): (("d", 2, 0, 0),),
+    ("O", 1): (("g", 1, 1, 3),),
+    ("O", 2): (("r", 1, 0, 1), ("g", 2, 1, 3), ("g", 1, 0, 3)),
+    ("O", 3): (("g", 1, 1, 4), ("r", 0, 0, 1)),
+    ("O", 4): (("r", 3, 0, 1),),
+    ("O", 5): (("g", 2, 1, 4), ("g", 1, 0, 4), ("w", 1, 0, 0)),
+    ("fill", 2): (("r", 4, 0, 1), ("w", 2, 0, 0)),
+    ("P", 0): (("r", 1, 0, 2),),
+    ("n", 2): (("r", 0, 0, 2), ("r", 2, 0, 1)),
+    ("P", 3): (("r", 3, 0, 2),),
+    ("fill", 4): (("r", 4, 0, 2), ("r", 5, 0, 1)),
+    ("B", 2): (("r", 0, 0, 3),),
+    ("B", 3): (("r", 2, 0, 2),),
+    ("B", 4): (("r", 1, 0, 3),),
+    ("B", 5): (("r", 3, 0, 3), ("r", 0, 0, 4), ("r", 4, 0, 3)),
+    ("b", 0): (("r", 1, 0, 4), ("r", 5, 0, 2), ("r", 3, 0, 4)),
+    ("b", 1): (("r", 4, 0, 4), ("r", 8, 0, 1), ("r", 2, 0, 3), ("r", 6, 0, 1), ("r", 7, 0, 1)),
+    ("B", 8): (("r", 5, 0, 3), ("r", 2, 0, 4)),
+    ("B", 11): (("r", 8, 0, 2),),
+    ("fill", 5): (("r", 5, 0, 4),),
+    ("fill", 6): (("r", 6, 0, 2), ("r", 7, 0, 2), ("r", 8, 0, 3), ("r", 6, 0, 3), ("r", 7, 0, 3), ("r", 6, 0, 4),
+        ("r", 8, 0, 4), ("r", 7, 0, 4)),
 }
 
 
 def layer_kernel(
-    split, tokens, cots, g1, s1, g2, s2, own,
-    wf, vecs, gqkv, gout, gup, gdown, output, gtok, outs, gtoks,
-    tok, stage, cotp, n1, qkv, prob, mx, mid, br, gn, n2, ust, dst, wbf, ta, tb, gp, gmix,
+    split, tokens, cots, g1, s1, g2, s2, w_qkv, w_out, w_up, w_down,
+    own, wf, vecs, gqkv, gout, gup, gdown, output, gtok, outs, gtoks,
+    tok, stage, cotp, n1, qkv, prob, mx, mid, br, gn, n2, ust, wbf, ta, tb, gp, gmix,
     po, ps, cr, ra, rb, rc, gv, vcr, vr,
-    isem, wsem, csend, crecv, ysend, yrecv, dsend, drecv, rcs, rcr, rsend, rrecv, osend, orecv, vsend, vrecv,
+    isem, ksem, wsem, csend, crecv, ysend, yrecv, dsend, drecv, rcs, rcr, rsend, rrecv, osend, orecv, vsend, vrecv,
 ):
     ex, rows, width = tok.shape
     rpad = n1.shape[1]
@@ -114,10 +113,22 @@
     def dpi(fh, fl, fx):
         return ((1 - zh) if fh else zh) * 4 + ((1 - zl) if fl else zl) * 2 + ((1 - x) if fx else x)
 
+    def at(fh, fl, fx):
+        return ((1 - zh) if fh else zh, (1 - zl) if fl else zl, (1 - x) if fx else x)
+
     znb2, znb1, xnb = (dpi(1, 0, 0), tt), (dpi(0, 1, 0), tt), (dpi(0, 0, 1), tt)
 
-    def band(i):
-        return pl.ds(pl.multiple_of(i * (width // 8), width // 8), width // 8)
+    coming = [
+        pltpu.make_async_copy(w_qkv.at[i], wbf.at[1, pl.ds(192 * i, 192)], isem.at[i]) for i in range(3)
+    ] + [
+        pltpu.make_async_copy(w_out, wbf.at[1, pl.ds(576, 192)], isem.at[3]),
+        pltpu.make_async_copy(w_up, wbf.at[2], isem.at[4]),
+        pltpu.make_async_copy(w_down, wbf.at[3], isem.at[5]),
+        pltpu.make_async_copy(tokens.at[pl.ds(c * ex, ex)], tok, isem.at[6]),
+        pltpu.make_async_copy(cots.at[pl.ds(c * ex, ex)], stage, isem.at[7]),
+    ]
+    for cp in coming:
+        cp.start()
 
     peers = [sib, ynb] + [(lax.rem(d + k, 8), tt) for k in range(1, 8)]
     barrier = pltpu.get_barrier_semaphore()
@@ -125,14 +136,12 @@
         pl.semaphore_signal(barrier, 1, device_id=p, device_id_type=MESH)
     pl.semaphore_wait(barrier, len(peers))
 
-    def third(h):
-        return slice(h * CH, (h + 1) * CH)
-
     def y_slice(p, h):
-        return rcopy(own.at[p, band(d), third(h)], wf.at[1, p, band(d), third(h)], ysend.at[p, h], yrecv.at[p, h], ynb)
+        blk = (p, h) + at(0, 0, 0)
+        return rcopy(own.at[blk], wf.at[(1,) + blk], ysend.at[p, h], yrecv.at[p, h], ynb)
 
     def y_direct(p):
-        return rcopy(own.at[p, :, third(2)], wf.at[1, p, :, third(2)], ysend.at[p, 2], yrecv.at[p, 2], ynb)
+        return rcopy(own.at[p, 2], wf.at[1, p, 2], ysend.at[p, 2], yrecv.at[p, 2], ynb)
 
     def c_first(p):
         return rcopy(own.at[p], wf.at[0, p], csend.at[p], crecv.at[p], sib)
@@ -141,17 +150,17 @@
         return rcopy(wf.at[1, p], wf.at[2, p], csend.at[3 + p], crecv.at[3 + p], sib)
 
     hops = (
-        (dpi(0, 0, 0), dpi(1, 0, 0), znb2),
-        (dpi(0, 0, 0), dpi(0, 1, 0), znb1),
-        (dpi(1, 0, 0), dpi(1, 1, 0), znb1),
-        (dpi(0, 0, 0), dpi(0, 0, 1), xnb),
-        (dpi(1, 0, 0), dpi(1, 0, 1), xnb),
-        (dpi(0, 1, 0), dpi(0, 1, 1), xnb),
-        (dpi(1, 1, 0), dpi(1, 1, 1), xnb),
+        (at(0, 0, 0), at(1, 0, 0), znb2),
+        (at(0, 0, 0), at(0, 1, 0), znb1),
+        (at(1, 0, 0), at(1, 1, 0), znb1),
+        (at(0, 0, 0), at(0, 0, 1), xnb),
+        (at(1, 0, 0), at(1, 0, 1), xnb),
+        (at(0, 1, 0), at(0, 1, 1), xnb),
+        (at(1, 1, 0), at(1, 1, 1), xnb),
     )
 
     def hop(p, h, k, arriving=False):
-        blk = wf.at[1, p, band(hops[k][1] if arriving else hops[k][0]), third(h)]
+        blk = wf.at[(1, p, h) + (hops[k][1] if arriving else hops[k][0])]
         return rcopy(blk, blk, dsend.at[2 * p + h, k], drecv.at[2 * p + h, k], hops[k][2])
 
     def g_step(p, h, stage):
@@ -173,41 +182,31 @@
             hop(p, h, k).start()
 
     def fetch(j, p, i, b):
-        def src(ref):
-            if p == 2:
-                return ref.at[pl.ds(pl.multiple_of(i * CH, CH), CH), :]
-            return ref.at[:, pl.ds(pl.multiple_of(i * CH, CH), CH)]
-
-        dstr = (dst if p == 2 else ust).at[b]
-        sem = wsem.at[1 if p == 2 else 0, b]
-
         @pl.when(j == 0)
         def _():
-            pltpu.make_async_copy(src(own.at[p]), dstr, sem).start()
+            pltpu.make_async_copy(own.at[p, i], ust.at[b], wsem.at[b]).start()
 
         @pl.when(j > 0)
         def _():
-            pltpu.make_async_copy(src(wf.at[jnp.maximum(j - 1, 0), p]), dstr, sem).start()
-
-    def fetched(p, b):
-        dstr = (dst if p == 2 else ust).at[b]
-        pltpu.make_async_copy(dstr, dstr, wsem.at[1 if p == 2 else 0, b]).wait()
+            pltpu.make_async_copy(wf.at[jnp.maximum(j - 1, 0), p, i], ust.at[b], wsem.at[b]).start()
+
+    def fetched(b):
+        pltpu.make_async_copy(ust.at[b], ust.at[b], wsem.at[b]).wait()
+        return ust[b].reshape(width, CH).astype(BF16)
 
     def load_attn(j):
-        fetch(j, 0, 0, 0)
-        fetch(j, 0, 1, 1)
+        for i in range(3):
+            fetch(j, 0, i, i)
 
     def take_attn(j):
-        fetched(0, 0)
-        wbf[j, :, :CH] = ust[0].astype(BF16)
-        fetch(j, 0, 2, 0)
-        fetched(0, 1)
-        wbf[j, :, CH : 2 * CH] = ust[1].astype(BF16)
-        fetched(0, 0)
-        wbf[j, :, 2 * CH :] = ust[0].astype(BF16)
+        for i in range(3):
+            wbf[j, :, i * CH : (i + 1) * CH] = fetched(i)
 
     def c_grad(u, slot):
         return rcopy(ps.at[slot], cr.at[u % 6], rcs.at[u], rcr.at[u], sib)
+
+    def place_of(u):
+        return (po, u) if u < 6 else (ust, u - 6)
 
     def views(pu, zfirst):
         if zfirst:
@@ -222,27 +221,28 @@
             ((pu, 1 - zh, zl, x), (pu, zh, zl, x), znb2),
         )
 
-    def halving(u, pu, k, zfirst):
-        src = po.at[views(pu, zfirst)[k][0]]
-        return rcopy(src, (ra, rb, rc)[k].at[u], rsend.at[u, k], rrecv.at[u, k], views(pu, zfirst)[k][2])
-
-    def r_step(u, pu, stage, zfirst):
-        view = views(pu, zfirst)
+    def halving(u, k):
+        ref, pu = place_of(u)
+        away, _, to = views(pu, ZFIRST[u])[k]
+        return rcopy(ref.at[away], (ra, rb, rc)[k].at[u], rsend.at[u, k], rrecv.at[u, k], to)
+
+    def r_step(u, stage):
+        ref, pu = place_of(u)
+        view = views(pu, ZFIRST[u])
         if stage == 1:
             c_grad(u, 0).wait_recv()
-            away = view[0][0][1:]
-            po[(pu,) + away] += cr[(u % 6,) + away]
-            halving(u, pu, 0, zfirst).start()
-            keep = view[0][1][1:]
-            po[(pu,) + keep] += cr[(u % 6,) + keep]
+            away, keep = view[0][0], view[0][1]
+            ref[away] += cr[(u % 6,) + away[1:]]
+            halving(u, 0).start()
+            ref[keep] += cr[(u % 6,) + keep[1:]]
         elif stage < 4:
             k = stage - 2
-            halving(u, pu, k, zfirst).wait_recv()
-            po[view[k][1]] += (ra, rb)[k][u]
-            halving(u, pu, k + 1, zfirst).start()
+            halving(u, k).wait_recv()
+            ref[view[k][1]] += (ra, rb)[k][u]
+            halving(u, k + 1).start()
         else:
-            halving(u, pu, 2, zfirst).wait_recv()
-            hand_out(u, po[view[2][1]] + rc[u])
+            halving(u, 2).wait_recv()
+            hand_out(u, ref[view[2][1]] + rc[u])
 
     def hand_out(u, g):
         if u < 6:
@@ -264,13 +264,6 @@
             gout[128:, :] = turned[HD:128]
             gout[:128, :] = turned[128:]
 
-    def r_sent(u, pu, zfirst):
-        for k in range(3):
-            halving(u, pu, k, zfirst).wait_send()
-
-    def place_of(u):
-        return u if u < 6 else REUSE[u - 6]
-
     def run(steps):
         for what, a, b, stage in steps:
             if what == "g":
@@ -285,7 +278,7 @@
                 y_direct(a).wait_recv()
                 c_second(a).start()
             else:
-                r_step(a, place_of(a), stage, ZFIRST[a])
+                r_step(a, stage)
 
     def tick(at, where):
         for (name, when), steps in PLAN.items():
@@ -297,21 +290,32 @@
     def fill(where, at):
         run(PLAN.get((where, at), ()))
 
+    for cp in coming[:4]:
+        cp.wait()
+    q_, k_, v_, o_ = 0, 192, 384, 576
+    row = 0
+    for src, n in (
+        (q_, 128), (k_, 128), (v_, 128), (q_ + 128, HD), (v_ + 128, HD), (k_ + 128, HD), (o_ + 128, HD), (o_, 128),
+    ):
+        wbf[0, row : row + n, :] = wbf[1, src : src + n, :]
+        row += n
+    unit = ust.shape[1:]
+
+    def keep_own(p, h, v, ref, slot):
+        ref[slot] = v.astype(F32).reshape(unit)
+        cp = pltpu.make_async_copy(ref.at[slot], own.at[p, h], ksem.at[p, h])
+        cp.start()
+        return cp
+
+    kept = [keep_own(0, h, wbf[0, :, h * CH : (h + 1) * CH], ps, h) for h in range(3)]
+    for cp in kept:
+        cp.wait()
     fill("start", 0)
-    load_attn(0)
-    cin = pltpu.make_async_copy(cots.at[pl.ds(c * ex, ex)], tok, isem.at[1])
-    cin.start()
-    cotp[...] = jnp.zeros_like(cotp)
-    cin.wait()
-
-    @pl.loop(0, ex)
-    def _(e):
-        cotp[e, :rows, :] = tok[e]
-
-    tin = pltpu.make_async_copy(tokens.at[pl.ds(c * ex, ex)], tok, isem.at[0])
-    tin.start()
-    ta[...] = cotp[...].reshape(t, width).T
-    tin.wait()
+    coming[4].wait()
+    kept = [keep_own(1, h, wbf[2, :, h * CH : (h + 1) * CH], po, h) for h in range(3)]
+    coming[5].wait()
+    kept += [keep_own(2, h, wbf[3, h * CH : (h + 1) * CH, :].T, po, 3 + h) for h in range(3)]
+    coming[6].wait()
     n1[...] = jnp.zeros_like(n1)
     mid[...] = jnp.zeros_like(mid)
     gv[...] = jnp.zeros_like(gv)
@@ -324,52 +328,81 @@
         n1[e, :rows, :] = (xhat * g1[...][None] + s1[...][None]).astype(BF16)
         mid[e, :rows, :] = v
 
+    for cp in kept:
+        cp.wait()
+    fill("own", 0)
+
     low_half = lax.broadcasted_iota(jnp.int32, (rpad, 128), 1) < HD
     qi = lax.broadcasted_iota(jnp.int32, (rpad, rpad), 0)
     kj = lax.broadcasted_iota(jnp.int32, (rpad, rpad), 1)
 
+    def group(j, e, i):
+        return qkv[j, e, :, i * 128 : (i + 1) * 128]
+
+    def half(v, high):
+        return jnp.where(low_half != high, v, jnp.zeros_like(v))
+
+    def pair(v):
+        return jnp.concatenate([half(v, False), half(v, True)], axis=0)
+
     @pl.loop(0, 4)
     def _(j):
-        take_attn(j)
+        @pl.when(j > 0)
+        def _():
+            take_attn(j)
 
         @pl.when(j == 0)
         def _():
+            fill("j", 0)
             c_first(0).wait_recv()
             load_attn(1)
 
-        tick(j * 5, "F")
-        qkv[j] = mm(n1[...].reshape(t, width), wbf[j, :, :640]).astype(BF16).reshape(ex, rpad, 640)
-
-        @pl.loop(0, ex)
-        def _(e):
-            tick(j * 5 + 1 + e, "F")
+        tick(j * 3, "F")
+        qkv[j] = mm_nt(n1[...].reshape(t, width), wbf[j, :640, :]).astype(BF16).reshape(ex, rpad, 640)
+        tick(j * 3 + 1, "F")
+
+        def scores(e):
+            q01, q2 = pair(group(j, e, 0)), half(group(j, e, 3), False)
+            return mm_nt(q01, group(j, e, 1)), mm_nt(q2, group(j, e, 4))
+
+        nxt = scores(0)
+        for e in range(ex):
+            s01, s2 = nxt
+            if e + 1 < ex:
+                nxt = scores(e + 1)
             allowed = kj <= jnp.maximum(qi, PATCHES - 1 + split[c * ex + e])
-            outs_h = []
-            for h, (gq, gk, gvv, high) in enumerate(HEADS):
-                q = qkv[j, e, :, gq * 128 : gq * 128 + 128]
-                q = jnp.where(low_half != high, q, jnp.zeros_like(q))
-                k = qkv[j, e, :, gk * 128 : gk * 128 + 128]
-                s = mm_nt(q, k) * (HD ** -0.5)
-                s = jnp.where(allowed, s, -1e30)
-                top = jnp.max(s, axis=-1, keepdims=True)
-                p = jnp.exp(s - top)
+            ps_h = []
+            for h, s in enumerate((s01[:rpad], s01[rpad:], s2)):
+                s = jnp.where(allowed, s * (HD ** -0.5), -1e30)
+                p = jnp.exp(s - jnp.max(s, axis=-1, keepdims=True))
                 p = (p * (1.0 / jnp.sum(p, axis=-1, keepdims=True))).astype(BF16)
                 prob[j, e, h] = p
-                outs_h.append(mm(p, qkv[j, e, :, gvv * 128 : gvv * 128 + 128]))
-            zero = jnp.zeros((rpad, 128), F32)
-            mx[j, e, :, :128] = jnp.where(low_half, zero, outs_h[2]).astype(BF16)
-            mx[j, e, :, 128:] = jnp.where(low_half, outs_h[0], outs_h[1]).astype(BF16)
-
-        tick(j * 5 + 4, "F")
-        mid[...] += mm_nt(mx[j].reshape(t, 256), wbf[j, :, 512:]).reshape(ex, rpad, width)
+                ps_h.append(p)
+            o01 = mm(jnp.concatenate(ps_h[:2], axis=0), group(j, e, 2))
+            o2 = mm(ps_h[2], group(j, e, 3))
+            mx[j, e, :, :128] = jnp.where(low_half, 0.0, o2).astype(BF16)
+            mx[j, e, :, 128:] = jnp.where(low_half, o01[:rpad], o01[rpad:]).astype(BF16)
+
+        tick(j * 3 + 2, "F")
+        mid[...] += mm(mx[j].reshape(t, 256), wbf[j, 512:, :]).reshape(ex, rpad, width)
 
         @pl.when(j == 1)
         def _():
+            fill("j", 1)
+            coming[7].wait()
+            cotp[...] = jnp.zeros_like(cotp)
+
+            @pl.loop(0, ex)
+            def _(e):
+                cotp[e, :rows, :] = stage[e]
+
+            ta[...] = cotp[...].reshape(t, width).T
             fill("j", 2)
             load_attn(2)
 
         @pl.when(j == 2)
         def _():
+            fill("j", 3)
             c_second(0).wait_recv()
             load_attn(3)
 
@@ -386,24 +419,19 @@
     tb[...] = n2[...].reshape(t, width).T
 
     def chunk(b):
-        u = ust[b].astype(BF16)
-        dn = dst[b].astype(BF16)
+        u, dn = fetched(b), fetched(2 + b)
         pre = mm(n2[...].reshape(t, width), u)
-        ga = mm_nt(cotp[...].reshape(t, width), dn)
+        ga = mm(cotp[...].reshape(t, width), dn)
         phi = 0.5 * (1.0 + lax.erf(pre * (0.5 ** 0.5)))
         act = (pre * phi).astype(BF16)
         gpre = (ga * (phi + pre * jnp.exp(-0.5 * pre * pre) * 0.3989422804014327)).astype(BF16)
-        br[...] += mm(act, dn).reshape(ex, rpad, width)
+        br[...] += mm_nt(act, dn).reshape(ex, rpad, width)
         gn[...] += mm_nt(gpre, u).reshape(ex, rpad, width)
         return act, gpre
 
     def fetch2(j, i, b):
         fetch(j, 1, i, b)
-        fetch(j, 2, i, b)
-
-    def fetched2(b):
-        fetched(1, b)
-        fetched(2, b)
+        fetch(j, 2, i, 2 + b)
 
     fill("fill", 1)
     c_first(1).wait_recv()
@@ -419,7 +447,6 @@
         def _():
             fetch2(b, (n + 1) // 2, 1 - b)
 
-        fetched2(b)
         act, gpre = chunk(b)
         gd = mm(ta[...], act).reshape(shape5)
         gu = mm(tb[...], gpre).reshape(shape5)
@@ -453,6 +480,7 @@
 
         @pl.when(n == 2)
         def _():
+            fill("n", 2)
             c_second(1).wait_recv()
             c_second(2).wait_recv()
 
@@ -460,7 +488,6 @@
         def _():
             fetch2(2 + (n + 1) // 3, lax.rem(n + 1, 3), 1 - b)
 
-        fetched2(b)
         chunk(b)
         tick(n, "P")
 
@@ -494,34 +521,39 @@
     @pl.loop(0, 4)
     def _(n):
         j = jnp.where(n < 2, 1 - n, n)
-        tick(n * 5, "B")
-        gmix[...] = mm(gml[...].reshape(t, width), wbf[j, :, 512:]).astype(BF16).reshape(ex, rpad, 256)
-
-        @pl.loop(0, ex)
-        def _(e):
-            tick(n * 5 + 1 + e, "B")
-            dq, dk, dv = [], [], []
-            for h, (gq, gk, gvv, high) in enumerate(HEADS):
-                gx = gmix[e, :, :128] if h == 2 else gmix[e, :, 128:]
-                gx = jnp.where(low_half != (high or h == 2), gx, jnp.zeros_like(gx))
-                p = prob[j, e, h]
-                dp = mm_nt(gx, qkv[j, e, :, gvv * 128 : gvv * 128 + 128])
-                pf = p.astype(F32)
+        tick(n * 3, "B")
+        gmix[...] = mm_nt(gml[...].reshape(t, width), wbf[j, 512:, :]).astype(BF16).reshape(ex, rpad, 256)
+        tick(n * 3 + 1, "B")
+
+        def first(e):
+            g01, g2_ = pair(gmix[e, :, 128:]), half(gmix[e, :, :128], True)
+            return g01, g2_, mm_nt(g01, group(j, e, 2)), mm_nt(g2_, group(j, e, 3))
+
+        nxt = first(0)
+        for e in range(ex):
+            g01, g2_, d01, d2 = nxt
+            if e + 1 < ex:
+                nxt = first(e + 1)
+            q01 = pair(group(j, e, 0))
+            ds = []
+            for h, dp in enumerate((d01[:rpad], d01[rpad:], d2)):
+                pf = prob[j, e, h].astype(F32)
                 pd = pf * dp
-                ds = (pd - pf * jnp.sum(pd, axis=-1, keepdims=True)).astype(BF16)
-                dq.append(mm(ds, qkv[j, e, :, gk * 128 : gk * 128 + 128]) * scale)
-                dk.append(mm_tn(ds, qkv[j, e, :, gq * 128 : gq * 128 + 128]) * scale)
-                dv.append(mm_tn(p, gx))
-            zero = jnp.zeros((rpad, 128), F32)
-            gp[e, :, 0:128] = jnp.where(low_half, dq[0], dq[1]).astype(BF16)
-            gp[e, :, 128:256] = jnp.where(low_half, dk[0], dk[1]).astype(BF16)
-            gp[e, :, 256:384] = jnp.where(low_half, dv[0], dv[1]).astype(BF16)
-            gp[e, :, 384:512] = jnp.where(low_half, dq[2], dv[2]).astype(BF16)
-            gp[e, :, 512:640] = jnp.where(low_half, dk[2], zero).astype(BF16)
-
-        tick(n * 5 + 4, "B")
+                ds.append((pd - pf * jnp.sum(pd, axis=-1, keepdims=True)).astype(BF16))
+            s01 = jnp.concatenate(ds[:2], axis=0)
+            p01 = jnp.concatenate([prob[j, e, 0], prob[j, e, 1]], axis=0)
+            dv01, dv2 = mm_tn(p01, g01), mm_tn(prob[j, e, 2], g2_)
+            dq01, dq2 = mm(s01, group(j, e, 1)) * scale, mm(ds[2], group(j, e, 4)) * scale
+            dk01, dk2 = mm_tn(s01, q01) * scale, mm_tn(ds[2], group(j, e, 3)) * scale
+            gp[e, :, 0:128] = jnp.where(low_half, dq01[:rpad], dq01[rpad:]).astype(BF16)
+            gp[e, :, 128:256] = dk01.astype(BF16)
+            gp[e, :, 256:384] = dv01.astype(BF16)
+            gp[e, :, 384:512] = jnp.where(low_half, dq2, dv2).astype(BF16)
+            gp[e, :, 512:640] = jnp.where(low_half, dk2, 0.0).astype(BF16)
+
+        tick(n * 3 + 2, "B")
         gpf = gp[...].reshape(t, 640)
-        gn[...] += mm_nt(gpf, wbf[j, :, :640]).reshape(ex, rpad, width)
+        gn[...] += mm(gpf, wbf[j, :640, :]).reshape(ex, rpad, width)
 
         def grads(write):
             write(0, mm(tb[...], gpf[:, :256]).reshape(shape5))
@@ -535,6 +567,8 @@
             for u in range(2, 6):
                 c_grad(u, (0, 1, 2, 3, 0, 1)[u]).wait_send()
 
+            o_copy.wait_recv()
+
             def write(i, g):
                 ps[i] = g
                 c_grad(6 + i, i).start()
@@ -544,15 +578,13 @@
         @pl.when(n == 1)
         def _():
             fill("b", 0)
-            for u in REUSE:
-                r_sent(u, u, ZFIRST[u])
 
             def write(i, g):
-                po[REUSE[i]] = g
+                ust[i] = g
 
             grads(write)
             fill("b", 1)
-            o_copy.wait()
+            o_copy.wait_send()
             o_back.start()
 
         @pl.when(n == 2)
@@ -603,7 +635,10 @@
         k = lax.rem(i - d + 8, 8)
         term = jnp.where(k == 0, gv[...], vr[jnp.maximum(k - 1, 0)])
         acc = term if acc is None else acc + term
-    vecs[...] = acc
+    mine_v = jnp.zeros(vecs.shape, F32)
+    for i in range(8):
+        mine_v = jnp.where(d == i, acc[:, i * (width // 8) : (i + 1) * (width // 8)], mine_v)
+    vecs[...] = mine_v
 
     t_back.wait()
     t_keep.wait()
@@ -625,14 +660,14 @@
             for k in range(7):
                 hop(p, h, k).wait_send()
     for u in range(9):
-        if u not in REUSE:
-            r_sent(u, place_of(u), ZFIRST[u])
+        for k in range(3):
+            halving(u, k).wait_send()
     for u in range(6, 9):
         c_grad(u, u - 6).wait_send()
     t_other.wait()
 
 
-def layer(split, tokens, cots, g1, s1, g2, s2, own):
+def layer(split, tokens, cots, g1, s1, g2, s2, w_qkv, w_out, w_up, w_down):
     batch, rows, width = tokens.shape
     ex = batch // 2
     rpad = -(-rows // 16) * 16
@@ -645,80 +680,43 @@
     VM = pl.BlockSpec(memory_space=pltpu.VMEM)
     SM = pl.BlockSpec(memory_space=pltpu.SMEM)
     act = (ex, rpad, width)
+    unit = (2, 2, 2, band, CH)
     return pl.pallas_call(
         layer_kernel,
         out_shape=(
-            sds((3, 3, width, 768), F32), sds((8, width), F32),
+            sds((3, 3) + unit, F32), sds((3, 3, 3) + unit, F32), sds((8, band), F32),
             sds((3, band, 192), F32), sds((192, band), F32), sds((band, 768), F32), sds((band, 768), F32),
             sds(tokens.shape, BF16), sds(tokens.shape, BF16), sds(act, F32), sds(act, F32),
         ),
-        in_specs=[SM, ANY, ANY, VM, VM, VM, VM, ANY],
-        out_specs=(ANY, VM, VM, VM, VM, VM, ANY, ANY, ANY, ANY),
+        in_specs=[SM, ANY, ANY, VM, VM, VM, VM, ANY, ANY, ANY, ANY],
+        out_specs=(ANY, ANY, VM, VM, VM, VM, VM, ANY, ANY, ANY, ANY),
         scratch_shapes=[
             vm((ex, rows, width), BF16), vm((ex, rows, width), BF16), vm(act, BF16), vm(act, BF16),
             vm((4, ex, rpad, 640), BF16), vm((4, ex, 3, rpad, rpad), BF16), vm((4, ex, rpad, 256), BF16),
             vm(act, F32), vm(act, F32), vm(act, F32), vm(act, BF16),
-            vm((2, width, CH), F32), vm((2, CH, width), F32), vm((4, width, 768), BF16),
+            vm((4,) + unit, F32), vm((4, width, 768), BF16),
             vm((width, t), BF16), vm((width, t), BF16), vm((ex, rpad, 640), BF16), vm((ex, rpad, 256), BF16),
-            vm((6, 2, 2, 2, band, CH), F32), vm((4, 2, 2, 2, band, CH), F32), vm((6, 2, 2, 2, band, CH), F32),
+            vm((6,) + unit, F32), vm((4,) + unit, F32), vm((6,) + unit, F32),
             vm((9, 2, 2, band, CH), F32), vm((9, 2, band, CH), F32), vm((9, band, CH), F32),
             vm((8, width), F32), vm((8, width), F32), vm((7, 8, width), F32),
-            dma((3,)), dma((2, 2)), dma((6,)), dma((6,)), dma((3, 3)), dma((3, 3)), dma((6, 7)), dma((6, 7)),
+            dma((8,)), dma((3, 3)), dma((4,)), dma((6,)), dma((6,)), dma((3, 3)), dma((3, 3)), dma((6, 7)), dma((6, 7)),
             dma((9,)), dma((9,)), dma((9, 3)), dma((9, 3)), dma((3,)), dma((3,)), dma((7,)), dma((7,)),
         ],
         compiler_params=pltpu.CompilerParams(collective_id=0, has_side_effects=True, vmem_limit_bytes=VLIM),
         name="layer",
-    )(split, tokens, cots, g1, s1, g2, s2, own)
+    )(split, tokens, cots, g1, s1, g2, s2, w_qkv, w_out, w_up, w_down)
 
 
 VLIM = 64 * 1024 * 1024 - 64 * 1024
-
-
-def prepare_kernel(w_qkv, w_out, w_up, w_down, own):
-    part = pl.program_id(0)
-
-    @pl.when(part == 0)
-    def _():
-        q, k, v = (w_qkv[i].astype(F32).T for i in range(3))
-        o = w_out[...].astype(F32).T
-        for i, g in enumerate((
-            q[:, :128], k[:, :128], v[:, :128], jnp.concatenate([q[:, 128:], v[:, 128:]], axis=1),
-            jnp.concatenate([k[:, 128:], o[:, 128:]], axis=1), o[:, :128],
-        )):
-            own[0, :, i * 128 : (i + 1) * 128] = g
-
-    @pl.when(part == 1)
-    def _():
-        own[0] = w_up[...].astype(F32)
-
-    @pl.when(part == 2)
-    def _():
-        own[0] = w_down[...].astype(F32)
-
-
-def prepare(w_qkv, w_out, w_up, w_down):
-    width = w_up.shape[0]
-    whole = lambda w: pl.BlockSpec(w.shape, lambda i: (0,) * w.ndim)
-    return pl.pallas_call(
-        prepare_kernel,
-        grid=(3,),
-        out_shape=jax.ShapeDtypeStruct((3, width, 768), F32),
-        in_specs=[whole(w) for w in (w_qkv, w_out, w_up, w_down)],
-        out_specs=pl.BlockSpec((1, width, 768), lambda i: (i, 0, 0)),
-        name="prepare",
-    )(w_qkv, w_out, w_up, w_down)
 
 
 def fast_device(tokens, cotangent, split_point, w_qkv, w_out, w_up, w_down, gain_one, shift_one, gain_two, shift_two):
     batch, length, width = tokens.shape
-    d = lax.axis_index("dp")
-    band = width // 8
-    own = prepare(w_qkv.transpose(0, 2, 1), w_out, w_up, w_down)
-    _, vecs, gqkv, gout, gup, gdown, output, gtok, _, _ = layer(
-        split_point, tokens, cotangent, gain_one, shift_one, gain_two, shift_two, own
-    )
-    mine = lax.dynamic_slice_in_dim(vecs, d * band, band, 1)
-    return output, gtok, gqkv, gout, gup, gdown.T, mine[0], mine[1], mine[2], mine[3]
+    _, _, vecs, gqkv, gout, gup, gdown, output, gtok, _, _ = layer(
+        split_point, tokens, cotangent, gain_one, shift_one, gain_two, shift_two,
+        w_qkv.transpose(0, 2, 1), w_out, w_up, w_down,
+    )
+    return output, gtok, gqkv, gout, gup, gdown.T, vecs[0], vecs[1], vecs[2], vecs[3]
 
 
 def layer_norm(values, gain_vec, shift_vec):

time: 188 us -> 169 us (0.90)
  Pallas kernels: 178 us -> 158 us
    pallas_call x2 -> x1, Pallas kernels: 178 us -> 158 us  [layer(): pl.pallas_call(layer_kernel, out_shape=(sds((3, 3) + unit, F32), sds((3,...]
where the time goes in v4:
time: 169 us; the launch traced here: 168 us
  Pallas kernels  158 us (93%)
  local copies, waits for them, and re-layouts  9 us (5%)
    pallas_call x1, Pallas kernels, layer(): pl.pallas_call(layer_kernel, out_shape=(sds((3, 3) + unit, F32), sds((3,...  158 us
    unnamed x16, local copies, waits for them, and re-layouts  7.65 us

profile of v4, /device:TPU:0, one launch (start us, length us, event | category | flops | bytes accessed | tf_op | source)
XLA Modules:
  0.0 167.9 jit_solution(320707910878608283)
XLA Ops:
  0.6 158.2 %layer.1 = (f32[3,3,2,2,2,96,256]{6,5,4,3,2,1,0:T(8,128)}, f32[3,3,3,2,2,2,96,256]{7,6,5,4,3,2,1,0:T(8,128)}, f32[8,96]{1,0:T(8,128)}, f32[3,96,192]{2,1,0:T(8,1...) custom-call(s32[6]{0:T(128)} %split.1, ...), custom_call_target="tpu_custom_call" | custom-call | tf_op jit(solution)/shard_map/layer/pallas_call | solution.py:684
  158.8 1.4 slice_bitcast_fusion
  160.2 0.0 copy-start
  160.2 3.4 %copy.27 = bf16[6,260,768]{2,1,0:T(8,128)(2,1)} copy(bf16[6,260,768]{2,1,0:T(8,128)(2,1)} %get-tuple-element.38) | data formatting | bytes 4792320
  163.6 0.0 copy-done
  163.6 0.0 copy-start.3
  163.6 0.0 copy-start.4
  163.6 0.0 copy-start.2
  163.6 0.0 copy-start.1
  163.6 1.4 copy.28
  165.1 0.0 copy-done.3
  165.1 0.7 copy.29
  165.8 0.0 copy-done.4
  165.8 0.6 copy.30
  166.4 0.0 copy-done.2
  166.4 0.7 copy.31
  167.2 0.0 copy-done.1
  167.2 0.7 copy.32
Async XLA Ops:
  160.2 3.4 %copy-start = (bf16[6,260,768]{2,1,0:T(8,128)(2,1)S(1)}, bf16[6,260,768]{2,1,0:T(8,128)(2,1)}, u32[]{:S(2)}) copy-start(bf16[6,260,768]{2,1,0:T(8,128)(2,1)} %get-tuple-element.39) | copy-start | bytes 7188484
  163.6 1.5 copy-start.3
  163.6 2.2 %copy-start.4 = (f32[192,96]{1,0:T(8,128)S(1)}, f32[192,96]{1,0:T(8,128)}, u32[]{:S(2)}) copy-start(f32[192,96]{1,0:T(8,128)} %get-tuple-element.41) | copy-start | bytes 221188
  163.6 2.8 %copy-start.2 = (f32[96,768]{1,0:T(8,128)S(1)}, f32[96,768]{1,0:T(8,128)}, u32[]{:S(2)}) copy-start(f32[96,768]{1,0:T(8,128)} %get-tuple-element.42) | copy-start | bytes 884740
  163.6 3.5 %copy-start.1 = (f32[96,768]{1,0:T(8,128)S(1)}, f32[96,768]{1,0:T(8,128)}, u32[]{:S(2)}) copy-start(f32[96,768]{1,0:T(8,128)} %get-tuple-element.22) | copy-start | bytes 884740

commit v5 on v4

--- a/solution.py
+++ b/solution.py
@@ -50,47 +50,45 @@
     )
 
 
-ZFIRST = (False, True, False, True, False, False, True, False, False)
+ZFIRST = (True, True, False, True, False, False, False, False, False)
 
 PLAN = {
-    ("start", 0): (("c", 0, 0, 0), ("s", 0, 1, 0)),
-    ("L", 0): (("s", 0, 0, 0),),
-    ("L", 2): (("g", 0, 1, 1),),
-    ("own", 0): (("c", 1, 0, 0), ("c", 2, 0, 0), ("s", 2, 0, 0)),
-    ("F", 1): (("g", 0, 0, 1),),
-    ("F", 2): (("d", 0, 0, 0),),
-    ("F", 3): (("g", 2, 0, 1),),
-    ("j", 1): (("g", 0, 1, 2),),
-    ("j", 2): (("g", 0, 0, 2), ("g", 2, 0, 2), ("g", 0, 1, 3), ("s", 1, 1, 0), ("g", 0, 0, 3), ("s", 2, 1, 0),
-        ("g", 2, 0, 3), ("s", 1, 0, 0), ("g", 1, 1, 1), ("d", 1, 0, 0), ("g", 0, 1, 4), ("g", 2, 1, 1),
-        ("g", 0, 0, 4), ("w", 0, 0, 0)),
-    ("F", 7): (("g", 1, 0, 1),),
-    ("F", 8): (("g", 2, 0, 4),),
-    ("F", 9): (("g", 1, 1, 2),),
-    ("F", 11): (("g", 2, 1, 2),),
-    ("fill", 1): (("g", 1, 0, 2),),
-    ("O", 0): (("d", 2, 0, 0),),
-    ("O", 1): (("g", 1, 1, 3),),
-    ("O", 2): (("r", 1, 0, 1), ("g", 2, 1, 3), ("g", 1, 0, 3)),
-    ("O", 3): (("g", 1, 1, 4), ("r", 0, 0, 1)),
-    ("O", 4): (("r", 3, 0, 1),),
-    ("O", 5): (("g", 2, 1, 4), ("g", 1, 0, 4), ("w", 1, 0, 0)),
-    ("fill", 2): (("r", 4, 0, 1), ("w", 2, 0, 0)),
-    ("P", 0): (("r", 1, 0, 2),),
-    ("n", 2): (("r", 0, 0, 2), ("r", 2, 0, 1)),
-    ("P", 3): (("r", 3, 0, 2),),
-    ("fill", 4): (("r", 4, 0, 2), ("r", 5, 0, 1)),
-    ("B", 2): (("r", 0, 0, 3),),
-    ("B", 3): (("r", 2, 0, 2),),
-    ("B", 4): (("r", 1, 0, 3),),
-    ("B", 5): (("r", 3, 0, 3), ("r", 0, 0, 4), ("r", 4, 0, 3)),
-    ("b", 0): (("r", 1, 0, 4), ("r", 5, 0, 2), ("r", 3, 0, 4)),
-    ("b", 1): (("r", 4, 0, 4), ("r", 8, 0, 1), ("r", 2, 0, 3), ("r", 6, 0, 1), ("r", 7, 0, 1)),
-    ("B", 8): (("r", 5, 0, 3), ("r", 2, 0, 4)),
-    ("B", 11): (("r", 8, 0, 2),),
-    ("fill", 5): (("r", 5, 0, 4),),
-    ("fill", 6): (("r", 6, 0, 2), ("r", 7, 0, 2), ("r", 8, 0, 3), ("r", 6, 0, 3), ("r", 7, 0, 3), ("r", 6, 0, 4),
-        ("r", 8, 0, 4), ("r", 7, 0, 4)),
+    ("start", 0): (("c", 0, 0, 0), ("s", 0, 0, 0), ("s", 0, 1, 0)),
+    ("L", 0): (("d", 0, 0, 0),),
+    ("own", 0): (("c", 1, 0, 0), ("c", 2, 0, 0)),
+    ("j", 0): (("g", 0, 0, 1),),
+    ("F", 3): (("g", 0, 1, 1),),
+    ("F", 4): (("g", 0, 0, 2),),
+    ("j", 2): (("s", 1, 0, 0), ("g", 0, 1, 2), ("g", 0, 0, 3), ("s", 1, 1, 0), ("g", 0, 1, 3), ("s", 2, 1, 0),
+        ("g", 1, 0, 1), ("s", 2, 0, 0), ("g", 0, 0, 4), ("g", 1, 1, 1), ("d", 1, 0, 0), ("g", 0, 1, 4),
+        ("w", 0, 0, 0)),
+    ("F", 6): (("g", 1, 0, 2),),
+    ("F", 7): (("g", 2, 1, 1), ("g", 2, 0, 1)),
+    ("F", 10): (("g", 1, 1, 2),),
+    ("O", 1): (("g", 1, 0, 3),),
+    ("O", 2): (("d", 2, 0, 0), ("g", 2, 1, 2), ("g", 2, 0, 2)),
+    ("O", 3): (("g", 1, 1, 3),),
+    ("O", 4): (("r", 0, 0, 1),),
+    ("O", 6): (("g", 1, 0, 4),),
+    ("O", 7): (("g", 2, 1, 3), ("g", 2, 0, 3)),
+    ("O", 9): (("r", 1, 0, 1),),
+    ("O", 11): (("r", 2, 0, 1),),
+    ("fill", 2): (("g", 1, 1, 4), ("w", 1, 0, 0), ("r", 0, 0, 2), ("g", 2, 1, 4), ("g", 2, 0, 4), ("w", 2, 0, 0)),
+    ("P", 1): (("r", 5, 0, 1), ("r", 3, 0, 1)),
+    ("P", 3): (("r", 0, 0, 3), ("r", 2, 0, 2)),
+    ("P", 4): (("r", 1, 0, 2),),
+    ("P", 5): (("r", 4, 0, 1),),
+    ("N", 2): (("r", 0, 0, 4),),
+    ("B", 3): (("r", 5, 0, 2), ("r", 2, 0, 3)),
+    ("B", 5): (("r", 4, 0, 2), ("r", 1, 0, 3)),
+    ("b", 1): (("r", 7, 0, 1), ("r", 3, 0, 2)),
+    ("B", 7): (("r", 1, 0, 4),),
+    ("B", 8): (("r", 2, 0, 4),),
+    ("B", 9): (("r", 8, 0, 1),),
+    ("B", 11): (("r", 5, 0, 3),),
+    ("fill", 6): (("r", 4, 0, 3), ("r", 7, 0, 2), ("r", 6, 0, 1), ("r", 3, 0, 3), ("r", 5, 0, 4), ("r", 4, 0, 4),
+        ("r", 7, 0, 3), ("r", 3, 0, 4), ("r", 8, 0, 2), ("r", 7, 0, 4), ("r", 6, 0, 2), ("r", 8, 0, 3),
+        ("r", 8, 0, 4), ("r", 6, 0, 3), ("r", 6, 0, 4)),
 }
 
 
@@ -127,24 +125,24 @@
         pltpu.make_async_copy(tokens.at[pl.ds(c * ex, ex)], tok, isem.at[6]),
         pltpu.make_async_copy(cots.at[pl.ds(c * ex, ex)], stage, isem.at[7]),
     ]
-    for cp in coming:
+    for cp in coming[:4]:
         cp.start()
 
     peers = [sib, ynb] + [(lax.rem(d + k, 8), tt) for k in range(1, 8)]
     barrier = pltpu.get_barrier_semaphore()
     for p in peers:
         pl.semaphore_signal(barrier, 1, device_id=p, device_id_type=MESH)
-    pl.semaphore_wait(barrier, len(peers))
 
     def y_slice(p, h):
         blk = (p, h) + at(0, 0, 0)
-        return rcopy(own.at[blk], wf.at[(1,) + blk], ysend.at[p, h], yrecv.at[p, h], ynb)
+        src = own.at[blk] if p else ps.at[(h,) + at(0, 0, 0)]
+        return rcopy(src, wf.at[(1,) + blk], ysend.at[p, h], yrecv.at[p, h], ynb)
 
     def y_direct(p):
-        return rcopy(own.at[p, 2], wf.at[1, p, 2], ysend.at[p, 2], yrecv.at[p, 2], ynb)
+        return rcopy(own.at[p, 2] if p else ps.at[2], wf.at[1, p, 2], ysend.at[p, 2], yrecv.at[p, 2], ynb)
 
     def c_first(p):
-        return rcopy(own.at[p], wf.at[0, p], csend.at[p], crecv.at[p], sib)
+        return rcopy(own.at[p] if p else ps.at[pl.ds(0, 3)], wf.at[0, p], csend.at[p], crecv.at[p], sib)
 
     def c_second(p):
         return rcopy(wf.at[1, p], wf.at[2, p], csend.at[3 + p], crecv.at[3 + p], sib)
@@ -307,10 +305,12 @@
         cp.start()
         return cp
 
-    kept = [keep_own(0, h, wbf[0, :, h * CH : (h + 1) * CH], ps, h) for h in range(3)]
-    for cp in kept:
-        cp.wait()
+    for h in range(3):
+        ps[h] = wbf[0, :, h * CH : (h + 1) * CH].astype(F32).reshape(unit)
+    pl.semaphore_wait(barrier, len(peers))
     fill("start", 0)
+    for cp in coming[4:]:
+        cp.start()
     coming[4].wait()
     kept = [keep_own(1, h, wbf[2, :, h * CH : (h + 1) * CH], po, h) for h in range(3)]
     coming[5].wait()
@@ -408,6 +408,7 @@
 
     @pl.loop(0, ex)
     def _(e):
+        tick(e, "M")
         keep = lax.broadcasted_iota(jnp.int32, (rpad, 1), 0) < rows
         v = jnp.where(keep, mid[e], 0.0)
         mid[e] = v
@@ -418,13 +419,15 @@
 
     tb[...] = n2[...].reshape(t, width).T
 
-    def chunk(b):
+    def chunk(b, between=None):
         u, dn = fetched(b), fetched(2 + b)
         pre = mm(n2[...].reshape(t, width), u)
         ga = mm(cotp[...].reshape(t, width), dn)
         phi = 0.5 * (1.0 + lax.erf(pre * (0.5 ** 0.5)))
         act = (pre * phi).astype(BF16)
         gpre = (ga * (phi + pre * jnp.exp(-0.5 * pre * pre) * 0.3989422804014327)).astype(BF16)
+        if between is not None:
+            between()
         br[...] += mm_nt(act, dn).reshape(ex, rpad, width)
         gn[...] += mm_nt(gpre, u).reshape(ex, rpad, width)
         return act, gpre
@@ -447,13 +450,20 @@
         def _():
             fetch2(b, (n + 1) // 2, 1 - b)
 
-        act, gpre = chunk(b)
+        act, gpre = chunk(b, lambda: tick(2 * n, "O"))
         gd = mm(ta[...], act).reshape(shape5)
         gu = mm(tb[...], gpre).reshape(shape5)
         slot = 2 * lax.rem(i, 2)
 
         @pl.when(b == 0)
         def _():
+            @pl.when(i == 0)
+            def _():
+                y_slice(0, 0).wait_send()
+                y_slice(0, 1).wait_send()
+                y_direct(0).wait_send()
+                c_first(0).wait_send()
+
             @pl.when(i == 2)
             def _():
                 c_grad(0, 0).wait_send()
@@ -469,7 +479,7 @@
             po[2 * i] = gd
             po[2 * i + 1] = gu
 
-        tick(n, "O")
+        tick(2 * n + 1, "O")
 
     fill("fill", 2)
     fetch2(2, 0, 0)
@@ -497,6 +507,7 @@
 
     @pl.loop(0, ex)
     def _(e):
+        tick(e, "N")
         back, dg, ds = ln_back(mid[e], gn[e], g2[...][None])
         gv[2:3, :] += dg
         gv[3:4, :] += ds
@@ -553,7 +564,6 @@
 
         tick(n * 3 + 2, "B")
         gpf = gp[...].reshape(t, 640)
-        gn[...] += mm(gpf, wbf[j, :640, :]).reshape(ex, rpad, width)
 
         def grads(write):
             write(0, mm(tb[...], gpf[:, :256]).reshape(shape5))
@@ -586,6 +596,8 @@
             fill("b", 1)
             o_copy.wait_send()
             o_back.start()
+
+        gn[...] += mm(gpf, wbf[j, :640, :]).reshape(ex, rpad, width)
 
         @pl.when(n == 2)
         def _():
@@ -618,6 +630,8 @@
     t_back = pltpu.make_async_copy(gtoks, gn, isem.at[0])
     v_copy = rcopy(gv, vcr, osend.at[2], orecv.at[2], sib)
     v_copy.start()
+    last = PLAN[("fill", 6)]
+    run(last[: len(last) // 2])
     v_copy.wait()
     gv[...] += vcr[...]
     v_sends = []
@@ -627,7 +641,7 @@
         v_sends.append(cp)
     t_copy.wait()
     t_back.start()
-    fill("fill", 6)
+    run(last[len(last) // 2 : -1])
     for k in range(1, 8):
         rcopy(gv, vr.at[k - 1], vsend.at[k - 1], vrecv.at[k - 1], sib).wait_recv()
     acc = None
@@ -639,7 +653,6 @@
     for i in range(8):
         mine_v = jnp.where(d == i, acc[:, i * (width // 8) : (i + 1) * (width // 8)], mine_v)
     vecs[...] = mine_v
-
     t_back.wait()
     t_keep.wait()
 
@@ -649,14 +662,18 @@
 
     t_other = pltpu.make_async_copy(tok, gtok.at[theirs], isem.at[1])
     t_other.start()
+    run(last[-1:])
+
     for cp in v_sends:
         cp.wait_send()
     for p in range(3):
-        y_direct(p).wait_send()
-        c_first(p).wait_send()
         c_second(p).wait_send()
+        if p:
+            y_direct(p).wait_send()
+            c_first(p).wait_send()
         for h in range(2):
-            y_slice(p, h).wait_send()
+            if p:
+                y_slice(p, h).wait_send()
             for k in range(7):
                 hop(p, h, k).wait_send()
     for u in range(9):

time: 169 us -> 166 us (0.982)
  Pallas kernels: 158 us -> 156 us
    pallas_call x1, Pallas kernels: 158 us -> 156 us  [layer(): pl.pallas_call(layer_kernel, out_shape=(sds((3, 3) + unit, F32), sds((3,...]
where the time goes in v5:
time: 166 us; the launch traced here: 165 us
  Pallas kernels  156 us (94%)
  local copies, waits for them, and re-layouts  9 us (5%)
    pallas_call x1, Pallas kernels, layer(): pl.pallas_call(layer_kernel, out_shape=(sds((3, 3) + unit, F32), sds((3,...  156 us
    unnamed x16, local copies, waits for them, and re-layouts  7.65 us

profile of v5, /device:TPU:0, one launch (start us, length us, event | category | flops | bytes accessed | tf_op | source)
XLA Modules:
  0.0 165.4 jit_solution(15675110708738371100)
XLA Ops:
  0.6 155.7 %layer.1 = (f32[3,3,2,2,2,96,256]{6,5,4,3,2,1,0:T(8,128)}, f32[3,3,3,2,2,2,96,256]{7,6,5,4,3,2,1,0:T(8,128)}, f32[8,96]{1,0:T(8,128)}, f32[3,96,192]{2,1,0:T(8,1...) custom-call(s32[6]{0:T(128)} %split.1, ...), custom_call_target="tpu_custom_call" | custom-call | tf_op jit(solution)/shard_map/layer/pallas_call | solution.py:701
  156.4 1.4 slice_bitcast_fusion
  157.7 0.0 copy-start
  157.7 3.4 %copy.27 = bf16[6,260,768]{2,1,0:T(8,128)(2,1)} copy(bf16[6,260,768]{2,1,0:T(8,128)(2,1)} %get-tuple-element.38) | data formatting | bytes 4792320
  161.1 0.0 copy-done
  161.1 0.0 copy-start.3
  161.1 0.0 copy-start.4
  161.1 0.0 copy-start.2
  161.1 0.0 copy-start.1
  161.2 1.4 copy.28
  162.6 0.0 copy-done.3
  162.6 0.7 copy.29
  163.3 0.0 copy-done.4
  163.3 0.6 copy.30
  163.9 0.0 copy-done.2
  164.0 0.7 copy.31
  164.7 0.0 copy-done.1
  164.7 0.7 copy.32
Async XLA Ops:
  157.7 3.4 %copy-start = (bf16[6,260,768]{2,1,0:T(8,128)(2,1)S(1)}, bf16[6,260,768]{2,1,0:T(8,128)(2,1)}, u32[]{:S(2)}) copy-start(bf16[6,260,768]{2,1,0:T(8,128)(2,1)} %get-tuple-element.39) | copy-start | bytes 7188484
  161.1 1.5 copy-start.3
  161.1 2.2 %copy-start.4 = (f32[192,96]{1,0:T(8,128)S(1)}, f32[192,96]{1,0:T(8,128)}, u32[]{:S(2)}) copy-start(f32[192,96]{1,0:T(8,128)} %get-tuple-element.41) | copy-start | bytes 221188
  161.1 2.8 %copy-start.2 = (f32[96,768]{1,0:T(8,128)S(1)}, f32[96,768]{1,0:T(8,128)}, u32[]{:S(2)}) copy-start(f32[96,768]{1,0:T(8,128)} %get-tuple-element.42) | copy-start | bytes 884740
  161.1 3.5 %copy-start.1 = (f32[96,768]{1,0:T(8,128)S(1)}, f32[96,768]{1,0:T(8,128)}, u32[]{:S(2)}) copy-start(f32[96,768]{1,0:T(8,128)} %get-tuple-element.22) | copy-start | bytes 884740

commit v6 on v5

--- a/solution.py
+++ b/solution.py
@@ -94,12 +94,14 @@
 
 def layer_kernel(
     split, tokens, cots, g1, s1, g2, s2, w_qkv, w_out, w_up, w_down,
-    own, wf, vecs, gqkv, gout, gup, gdown, output, gtok, outs, gtoks,
+    own, wf, vecs, gqkv, gout, gffn, results, outs, gtoks,
     tok, stage, cotp, n1, qkv, prob, mx, mid, br, gn, n2, ust, wbf, ta, tb, gp, gmix,
     po, ps, cr, ra, rb, rc, gv, vcr, vr,
     isem, ksem, wsem, csend, crecv, ysend, yrecv, dsend, drecv, rcs, rcr, rsend, rrecv, osend, orecv, vsend, vrecv,
 ):
     ex, rows, width = tok.shape
+    output, gtok = results.at[0], results.at[1]
+    gup, gdown = gffn.at[0], gffn.at[1]
     rpad = n1.shape[1]
     t = ex * rpad
     d, tt = lax.axis_index("dp"), lax.axis_index("tensor")
@@ -702,11 +704,11 @@
         layer_kernel,
         out_shape=(
             sds((3, 3) + unit, F32), sds((3, 3, 3) + unit, F32), sds((8, band), F32),
-            sds((3, band, 192), F32), sds((192, band), F32), sds((band, 768), F32), sds((band, 768), F32),
-            sds(tokens.shape, BF16), sds(tokens.shape, BF16), sds(act, F32), sds(act, F32),
+            sds((3, band, 192), F32), sds((192, band), F32), sds((2, band, 768), F32),
+            sds((2,) + tokens.shape, BF16), sds(act, F32), sds(act, F32),
         ),
         in_specs=[SM, ANY, ANY, VM, VM, VM, VM, ANY, ANY, ANY, ANY],
-        out_specs=(ANY, ANY, VM, VM, VM, VM, VM, ANY, ANY, ANY, ANY),
+        out_specs=(ANY, ANY, VM, VM, VM, VM, ANY, ANY, ANY),
         scratch_shapes=[
             vm((ex, rows, width), BF16), vm((ex, rows, width), BF16), vm(act, BF16), vm(act, BF16),
             vm((4, ex, rpad, 640), BF16), vm((4, ex, 3, rpad, rpad), BF16), vm((4, ex, rpad, 256), BF16),
@@ -729,11 +731,11 @@
 
 def fast_device(tokens, cotangent, split_point, w_qkv, w_out, w_up, w_down, gain_one, shift_one, gain_two, shift_two):
     batch, length, width = tokens.shape
-    _, _, vecs, gqkv, gout, gup, gdown, output, gtok, _, _ = layer(
+    _, _, vecs, gqkv, gout, gffn, results, _, _ = layer(
         split_point, tokens, cotangent, gain_one, shift_one, gain_two, shift_two,
         w_qkv.transpose(0, 2, 1), w_out, w_up, w_down,
     )
-    return output, gtok, gqkv, gout, gup, gdown.T, vecs[0], vecs[1], vecs[2], vecs[3]
+    return results[0], results[1], gqkv, gout, gffn[0], gffn[1].T, vecs[0], vecs[1], vecs[2], vecs[3]
 
 
 def layer_norm(values, gain_vec, shift_vec):

time: 166 us -> 164 us (0.988)
    unnamed x16 -> x10, local copies, waits for them, and re-layouts: 7.65 us -> 1.37 us
    squeeze x0 -> x1, local copies, waits for them, and re-layouts: none -> 5.04 us  [fast_device(): results[1]]
where the time goes in v6:
time: 164 us
  Pallas kernels  156 us (95%)
  local copies, waits for them, and re-layouts  7.79 us (5%)
    pallas_call x1, Pallas kernels, layer(): pl.pallas_call(layer_kernel, out_shape=(sds((3, 3) + unit, F32), sds((3,...  156 us
    squeeze x1, local copies, waits for them, and re-layouts, fast_device(): results[1]  5.04 us

profile of v6, /device:TPU:0, one launch (start us, length us, event | category | flops | bytes accessed | tf_op | source)
XLA Modules:
  0.0 164.2 jit_solution(17595981977863798508)
XLA Ops:
  0.6 155.7 %layer.1 = (f32[3,3,2,2,2,96,256]{6,5,4,3,2,1,0:T(8,128)}, f32[3,3,3,2,2,2,96,256]{7,6,5,4,3,2,1,0:T(8,128)}, f32[8,96]{1,0:T(8,128)}, f32[3,96,192]{2,1,0:T(8,1...) custom-call(s32[6]{0:T(128)} %split.1, ...), custom_call_target="tpu_custom_call" | custom-call | tf_op jit(solution)/shard_map/layer/pallas_call | solution.py:703
  156.4 0.0 copy-start.3
  156.4 0.0 copy-start
  156.4 0.0 copy-start.1
  156.4 0.0 copy-start.2
  156.4 5.0 %slice_bitcast_fusion = (bf16[6,260,768]{2,1,0:T(8,128)(2,1)}, bf16[6,260,768]{2,1,0:T(8,128)(2,1)}) fusion(bf16[2,6,260,768]{3,2,1,0:T(8,128)(2,1)} %get-tuple-element.15), kind=kLoop, calls=%fused_computation | loop fusion | bytes 9584640 | tf_op jit(solution)/shard_map/squeeze | solution.py:738
  161.4 0.0 copy-done.3
  161.5 0.5 slice_bitcast_fusion.4
  162.0 0.0 copy-done
  162.0 0.8 slice_bitcast_fusion.2
  162.8 0.0 copy-done.1
  162.8 0.7 copy.23
  163.5 0.0 copy-done.2
  163.5 0.6 copy.24
Async XLA Ops:
  156.4 5.1 %copy-start.3 = (f32[8,96]{1,0:T(8,128)S(1)}, f32[8,96]{1,0:T(8,128)}, u32[]{:S(2)}) copy-start(f32[8,96]{1,0:T(8,128)} %get-tuple-element.19) | copy-start | bytes 9220
  156.4 5.6 %copy-start = (f32[2,96,768]{2,1,0:T(8,128)S(1)}, f32[2,96,768]{2,1,0:T(8,128)}, u32[]{:S(2)}) copy-start(f32[2,96,768]{2,1,0:T(8,128)} %get-tuple-element.18) | copy-start | bytes 1769476
  156.4 6.4 %copy-start.1 = (f32[3,96,192]{2,1,0:T(8,128)S(1)}, f32[3,96,192]{2,1,0:T(8,128)}, u32[]{:S(2)}) copy-start(f32[3,96,192]{2,1,0:T(8,128)} %get-tuple-element.40) | copy-start | bytes 663556
  156.4 7.2 %copy-start.2 = (f32[192,96]{1,0:T(8,128)S(1)}, f32[192,96]{1,0:T(8,128)}, u32[]{:S(2)}) copy-start(f32[192,96]{1,0:T(8,128)} %get-tuple-element.41) | copy-start | bytes 221188

commit v7 on v6

--- a/solution.py
+++ b/solution.py
@@ -50,45 +50,47 @@
     )
 
 
-ZFIRST = (True, True, False, True, False, False, False, False, False)
+ZFIRST = (True, False, False, True, False, False, True, False, False)
 
 PLAN = {
-    ("start", 0): (("c", 0, 0, 0), ("s", 0, 0, 0), ("s", 0, 1, 0)),
-    ("L", 0): (("d", 0, 0, 0),),
+    ("start", 0): (("c", 0, 0, 0), ("s", 0, 1, 0), ("s", 0, 0, 0)),
+    ("L", 2): (("d", 0, 0, 0),),
     ("own", 0): (("c", 1, 0, 0), ("c", 2, 0, 0)),
-    ("j", 0): (("g", 0, 0, 1),),
-    ("F", 3): (("g", 0, 1, 1),),
-    ("F", 4): (("g", 0, 0, 2),),
-    ("j", 2): (("s", 1, 0, 0), ("g", 0, 1, 2), ("g", 0, 0, 3), ("s", 1, 1, 0), ("g", 0, 1, 3), ("s", 2, 1, 0),
-        ("g", 1, 0, 1), ("s", 2, 0, 0), ("g", 0, 0, 4), ("g", 1, 1, 1), ("d", 1, 0, 0), ("g", 0, 1, 4),
-        ("w", 0, 0, 0)),
-    ("F", 6): (("g", 1, 0, 2),),
-    ("F", 7): (("g", 2, 1, 1), ("g", 2, 0, 1)),
-    ("F", 10): (("g", 1, 1, 2),),
-    ("O", 1): (("g", 1, 0, 3),),
-    ("O", 2): (("d", 2, 0, 0), ("g", 2, 1, 2), ("g", 2, 0, 2)),
-    ("O", 3): (("g", 1, 1, 3),),
-    ("O", 4): (("r", 0, 0, 1),),
-    ("O", 6): (("g", 1, 0, 4),),
-    ("O", 7): (("g", 2, 1, 3), ("g", 2, 0, 3)),
-    ("O", 9): (("r", 1, 0, 1),),
-    ("O", 11): (("r", 2, 0, 1),),
-    ("fill", 2): (("g", 1, 1, 4), ("w", 1, 0, 0), ("r", 0, 0, 2), ("g", 2, 1, 4), ("g", 2, 0, 4), ("w", 2, 0, 0)),
-    ("P", 1): (("r", 5, 0, 1), ("r", 3, 0, 1)),
-    ("P", 3): (("r", 0, 0, 3), ("r", 2, 0, 2)),
-    ("P", 4): (("r", 1, 0, 2),),
-    ("P", 5): (("r", 4, 0, 1),),
-    ("N", 2): (("r", 0, 0, 4),),
-    ("B", 3): (("r", 5, 0, 2), ("r", 2, 0, 3)),
-    ("B", 5): (("r", 4, 0, 2), ("r", 1, 0, 3)),
-    ("b", 1): (("r", 7, 0, 1), ("r", 3, 0, 2)),
-    ("B", 7): (("r", 1, 0, 4),),
-    ("B", 8): (("r", 2, 0, 4),),
-    ("B", 9): (("r", 8, 0, 1),),
-    ("B", 11): (("r", 5, 0, 3),),
-    ("fill", 6): (("r", 4, 0, 3), ("r", 7, 0, 2), ("r", 6, 0, 1), ("r", 3, 0, 3), ("r", 5, 0, 4), ("r", 4, 0, 4),
-        ("r", 7, 0, 3), ("r", 3, 0, 4), ("r", 8, 0, 2), ("r", 7, 0, 4), ("r", 6, 0, 2), ("r", 8, 0, 3),
-        ("r", 8, 0, 4), ("r", 6, 0, 3), ("r", 6, 0, 4)),
+    ("j", 0): (("g", 0, 1, 1), ("g", 0, 0, 1)),
+    ("F", 3): (("s", 1, 1, 0),),
+    ("F", 5): (("s", 1, 0, 0),),
+    ("j", 2): (("g", 0, 1, 2), ("s", 2, 0, 0), ("s", 2, 1, 0), ("g", 0, 0, 2), ("g", 0, 1, 3), ("g", 0, 0, 3),
+        ("g", 1, 1, 1), ("g", 1, 0, 1), ("d", 1, 0, 0), ("g", 2, 0, 1), ("g", 0, 1, 4), ("g", 1, 1, 2),
+        ("g", 0, 0, 4), ("w", 0, 0, 0)),
+    ("j", 3): (("g", 2, 1, 1),),
+    ("F", 10): (("g", 1, 0, 2),),
+    ("M", 1): (("g", 2, 0, 2),),
+    ("M", 2): (("g", 1, 1, 3),),
+    ("O", 0): (("d", 2, 0, 0),),
+    ("O", 2): (("g", 2, 1, 2),),
+    ("O", 3): (("g", 1, 0, 3), ("g", 2, 0, 3)),
+    ("O", 5): (("r", 0, 0, 1), ("g", 2, 1, 3)),
+    ("O", 7): (("g", 1, 1, 4),),
+    ("O", 11): (("r", 2, 0, 1), ("r", 3, 0, 1)),
+    ("fill", 2): (("g", 1, 0, 4), ("g", 2, 0, 4), ("w", 1, 0, 0), ("g", 2, 1, 4), ("w", 2, 0, 0)),
+    ("P", 1): (("r", 0, 0, 2),),
+    ("n", 2): (("r", 1, 0, 1), ("r", 2, 0, 2)),
+    ("P", 3): (("r", 3, 0, 2),),
+    ("P", 4): (("r", 4, 0, 1),),
+    ("N", 2): (("r", 1, 0, 2),),
+    ("B", 2): (("r", 2, 0, 3), ("r", 0, 0, 3)),
+    ("B", 3): (("r", 3, 0, 3),),
+    ("B", 4): (("r", 4, 0, 2),),
+    ("B", 5): (("r", 2, 0, 4), ("r", 1, 0, 3), ("r", 0, 0, 4), ("r", 5, 0, 1)),
+    ("b", 1): (("r", 3, 0, 4),),
+    ("B", 6): (("r", 6, 0, 1),),
+    ("B", 8): (("r", 1, 0, 4),),
+    ("B", 10): (("r", 8, 0, 1),),
+    ("B", 11): (("r", 4, 0, 3),),
+    ("fill", 5): (("r", 5, 0, 2),),
+    ("fill", 6): (("r", 6, 0, 2), ("r", 7, 0, 1), ("r", 4, 0, 4), ("r", 8, 0, 2), ("r", 5, 0, 3), ("r", 6, 0, 3),
+        ("r", 7, 0, 2), ("r", 6, 0, 4), ("r", 5, 0, 4), ("r", 8, 0, 3), ("r", 7, 0, 3), ("r", 8, 0, 4),
+        ("r", 7, 0, 4)),
 }
 
 

time: 164 us -> 163 us (level)
  Pallas kernels: 156 us -> 154 us
    pallas_call x1, Pallas kernels: 156 us -> 154 us  [layer(): pl.pallas_call(layer_kernel, out_shape=(sds((3, 3) + unit, F32), sds((3,...]
where the time goes in v7:
time: 163 us; the launch traced here: 162 us
  Pallas kernels  154 us (94%)
  local copies, waits for them, and re-layouts  7.79 us (5%)
    pallas_call x1, Pallas kernels, layer(): pl.pallas_call(layer_kernel, out_shape=(sds((3, 3) + unit, F32), sds((3,...  154 us
    squeeze x1, local copies, waits for them, and re-layouts, fast_device(): results[1]  5.04 us

profile of v7, /device:TPU:0, one launch (start us, length us, event | category | flops | bytes accessed | tf_op | source)
XLA Modules:
  0.0 162.3 jit_solution(15451765796967383708)
XLA Ops:
  0.6 153.8 %layer.1 = (f32[3,3,2,2,2,96,256]{6,5,4,3,2,1,0:T(8,128)}, f32[3,3,3,2,2,2,96,256]{7,6,5,4,3,2,1,0:T(8,128)}, f32[8,96]{1,0:T(8,128)}, f32[3,96,192]{2,1,0:T(8,1...) custom-call(s32[6]{0:T(128)} %split.1, ...), custom_call_target="tpu_custom_call" | custom-call | tf_op jit(solution)/shard_map/layer/pallas_call | solution.py:705
  154.5 0.0 copy-start.3
  154.5 0.0 copy-start
  154.5 0.0 copy-start.1
  154.5 0.0 copy-start.2
  154.5 5.0 %slice_bitcast_fusion = (bf16[6,260,768]{2,1,0:T(8,128)(2,1)}, bf16[6,260,768]{2,1,0:T(8,128)(2,1)}) fusion(bf16[2,6,260,768]{3,2,1,0:T(8,128)(2,1)} %get-tuple-element.15), kind=kLoop, calls=%fused_computation | loop fusion | bytes 9584640 | tf_op jit(solution)/shard_map/squeeze | solution.py:740
  159.6 0.0 copy-done.3
  159.6 0.5 slice_bitcast_fusion.4
  160.1 0.0 copy-done
  160.1 0.8 slice_bitcast_fusion.2
  160.9 0.0 copy-done.1
  160.9 0.7 copy.23
  161.7 0.0 copy-done.2
  161.7 0.6 copy.24
Async XLA Ops:
  154.5 5.1 %copy-start.3 = (f32[8,96]{1,0:T(8,128)S(1)}, f32[8,96]{1,0:T(8,128)}, u32[]{:S(2)}) copy-start(f32[8,96]{1,0:T(8,128)} %get-tuple-element.19) | copy-start | bytes 9220
  154.5 5.6 %copy-start = (f32[2,96,768]{2,1,0:T(8,128)S(1)}, f32[2,96,768]{2,1,0:T(8,128)}, u32[]{:S(2)}) copy-start(f32[2,96,768]{2,1,0:T(8,128)} %get-tuple-element.18) | copy-start | bytes 1769476
  154.5 6.4 %copy-start.1 = (f32[3,96,192]{2,1,0:T(8,128)S(1)}, f32[3,96,192]{2,1,0:T(8,128)}, u32[]{:S(2)}) copy-start(f32[3,96,192]{2,1,0:T(8,128)} %get-tuple-element.40) | copy-start | bytes 663556
  154.5 7.2 %copy-start.2 = (f32[192,96]{1,0:T(8,128)S(1)}, f32[192,96]{1,0:T(8,128)}, u32[]{:S(2)}) copy-start(f32[192,96]{1,0:T(8,128)} %get-tuple-element.41) | copy-start | bytes 221188
